TPU v7x, 32 devices: a whole 2x2x4 slice. The times are simulated.
32 devices in a mesh: sub: 8 (over y, x, core), grp: 4 (over z).
Axes of the slice: x: 2, y: 2, z: 4, core: 2. Of those that a mesh axis runs over, the one named last changes fastest.
Arguments:
- res_inner: bfloat16 [2048, 16, 144], P(('sub', 'grp')), may hold values from -6 to 6
- res_face: bfloat16 [1024, 16, 144], P(('sub', 'grp')), may hold values from -6 to 6
- inner_inv: bfloat16 [2048, 144, 144], P(('sub', 'grp')), may hold values from -0.5 to 0.5
- face_coupling: bfloat16 [1024, 144, 144], P(('sub', 'grp')), may hold values from -0.5 to 0.5
- face_elem: int32 [32, 32], P(('sub', 'grp')), may hold values from 0 to 63
- face_inv: bfloat16 [1024, 144, 144], P(('sub', 'grp')), may hold values from -0.5 to 0.5
- coarse_basis: bfloat16 [1024, 64, 144], P(('sub', 'grp')), may hold values from -0.0625 to 0.0625
- coarse_map: int32 [32, 64], P(('sub', 'grp')), may hold values from 0 to 511
- coarse_inv: float32 [512, 512], P('grp'), as said below
- recv_index: int32 [32, 32], P(('sub', 'grp')), may hold values from 0 to 8, as said below
- sharers: int32 [32, 32], P(('sub', 'grp')), may hold values from 0 to 32, as said below
Outputs:
- inner_out: bfloat16 [2048, 16, 144], P(('sub', 'grp'))
- face_out: bfloat16 [1024, 16, 144], P(('sub', 'grp'))
Inputs may be any that keep to these rules, and one draw needn't show every extreme that they name: `recv_index`: row o gives, for each subdomain s at position s, the index among the 8 blocks owned by subdomain o that slot o of subdomain s refers to, or 8 where that slot is unused. `sharers`: for a used slot, the number of used slots of all subdomains that refer to the same owned block, up to all 32 of them, which some block reaches; 0 exactly for unused slots. coarse_inv is symmetric.
All inputs are finite; a program needn't handle non-finite values.
Results may differ from a plain program's by a relative error of at most 0.006.
Values may be sent and summed in bfloat16 or wider, within the bound.
No kernel may reach another device: no remote copies, remote signals or barrier semaphores. Data moves between devices by JAX's collectives and lax.ppermute only.
A program may use at most 128 MiB of HBM per device.

v0:
```python
import jax
import jax.numpy as jnp
from jax import lax
from jax.sharding import PartitionSpec as P


def send_out(partials):
    return lax.all_to_all(partials, ("sub", "grp"), split_axis=0, concat_axis=0, tiled=True)


def send_back(spread):
    return lax.all_to_all(spread, ("sub", "grp"), split_axis=0, concat_axis=0, tiled=True)


def body(
    res_inner,
    res_face,
    inner_inv,
    face_coupling,
    face_elem,
    face_inv,
    coarse_basis,
    coarse_map,
    coarse_inv,
    recv_index,
    sharers,
):
    num_faces = res_face.shape[0]
    num_owned = num_faces // 4
    elements = res_inner.shape[0]
    num_coarse = coarse_inv.shape[1]
    counts = sharers[0]
    weights = jnp.where(counts > 0, 1.0 / jnp.maximum(counts, 1).astype(jnp.float32), 0.0)
    owner_onehot = (
        recv_index[0][None, :] == jnp.arange(num_owned, dtype=jnp.int32)[:, None]
    ).astype(jnp.bfloat16)

    def assemble(partials):
        received = send_out(partials)
        flattened = received.reshape(num_faces, -1)
        owner_sum = jnp.dot(owner_onehot, flattened, preferred_element_type=jnp.float32).astype(
            jnp.bfloat16
        )
        spread = jnp.einsum(
            "of,ok->fk", owner_onehot, owner_sum, preferred_element_type=jnp.float32
        ).astype(jnp.bfloat16)
        return send_back(spread.reshape(partials.shape))

    inner_w = jnp.einsum(
        "erb,ecb->erc", res_inner, inner_inv, preferred_element_type=jnp.float32
    ).astype(jnp.bfloat16)
    nearby = inner_w[face_elem[0]]
    condensed = res_face.astype(jnp.float32) - jnp.einsum(
        "lrb,lcb->lrc", nearby, face_coupling, preferred_element_type=jnp.float32
    )
    sent = (weights[:, None, None] * condensed).astype(jnp.bfloat16)
    gathered = assemble(sent)
    restricted = (weights[:, None, None] * gathered.astype(jnp.float32)).astype(jnp.bfloat16)
    local_coarse = jnp.einsum(
        "ljb,lrb->jr", coarse_basis, restricted, preferred_element_type=jnp.float32
    )
    coarse_onehot = (
        coarse_map[0][None, :] == jnp.arange(num_coarse, dtype=jnp.int32)[:, None]
    ).astype(jnp.float32)
    partial_rhs = jnp.dot(coarse_onehot, local_coarse, precision=lax.Precision.HIGHEST)
    coarse_rhs = lax.psum(partial_rhs, ("sub", "grp"))
    row_part = jnp.dot(coarse_inv, coarse_rhs, precision=lax.Precision.HIGHEST)
    coarse_sol = lax.all_gather(row_part, "grp", axis=0, tiled=True)
    picked = jnp.einsum(
        "kj,kr->jr", coarse_onehot, coarse_sol, precision=lax.Precision.HIGHEST
    ).astype(jnp.bfloat16)
    coarse_part = jnp.einsum(
        "ljb,jr->lrb", coarse_basis, picked, preferred_element_type=jnp.float32
    )
    local_part = jnp.einsum(
        "lrb,lcb->lrc", restricted, face_inv, preferred_element_type=jnp.float32
    )
    weighted = (weights[:, None, None] * (coarse_part + local_part)).astype(jnp.bfloat16)
    face_out = assemble(weighted)
    contrib = jnp.einsum(
        "lrc,lcb->lrb", face_out, face_coupling, preferred_element_type=jnp.float32
    )
    elem_onehot = (face_elem[0][None, :] == jnp.arange(elements, dtype=jnp.int32)[:, None]).astype(
        jnp.float32
    )
    scattered = jnp.dot(
        elem_onehot, contrib.reshape(num_faces, -1), precision=lax.Precision.HIGHEST
    ).reshape(res_inner.shape)
    inner_rhs = (res_inner.astype(jnp.float32) - scattered).astype(jnp.bfloat16)
    inner_out = jnp.einsum(
        "erb,ecb->erc", inner_rhs, inner_inv, preferred_element_type=jnp.float32
    ).astype(jnp.bfloat16)
    return (inner_out, face_out)


def solution(mesh):
    return jax.shard_map(
        body,
        mesh=mesh,
        in_specs=(
            P(("sub", "grp"), None, None),
            P(("sub", "grp"), None, None),
            P(("sub", "grp"), None, None),
            P(("sub", "grp"), None, None),
            P(("sub", "grp"), None),
            P(("sub", "grp"), None, None),
            P(("sub", "grp"), None, None),
            P(("sub", "grp"), None),
            P("grp", None),
            P(("sub", "grp"), None),
            P(("sub", "grp"), None),
        ),
        out_specs=(P(("sub", "grp"), None, None), P(("sub", "grp"), None, None)),
        check_vma=False,
    )
```

profile of v0, /device:TPU:0, one launch (start us, length us, event | category | flops | bytes accessed | tf_op | source)
XLA Modules:
  0.0 140.8 jit_solution(13594599169915256372)
XLA Ops:
  0.6 0.8 fusion.20
  1.5 0.7 fusion.19
  2.1 3.8 %convolution_convert_fusion.5 = bf16[64,16,144]{2,1,0:T(8,128)(2,1)S(1)} fusion(bf16[64,16,144]{2,1,0:T(8,128)(2,1)} %param.11, bf16[64,144,144]{2,1,0:T(8,128)(2,1)} %param.13), kind=kOutput, calls=%fused_computation.6 | convolution fusion | flops 42614784 | bytes 3244032 | tf_op jit(solution)/shard_map/erb,ecb->erc/dot_general | solution.py:49
  6.0 1.3 gather_fusion
  7.3 1.8 %fusion.2 = bf16[32,16,144]{2,1,0:T(8,128)(2,1)S(1)} fusion(bf16[32,16,144]{2,1,0:T(8,128)(2,1)} %gather_fusion, bf16[32,144,144]{2,1,0:T(8,128)(2,1)S(1)} %copy-done, bf16[32,16,144]{2,1,0:T(8,128)(2,1)} %param.12, f32[32]{0:T(128)S(1)} %fusion.20), kind=kOutput, calls=%fused_computation.12 | convolution fusion | flops 21528576 | bytes 1769600 | tf_op jit(solution)/shard_map/lrb,lcb->lrc/dot_general | solution.py:53
  9.1 17.5 %all_to_all.20 = bf16[32,16,144]{2,1,0:T(8,128)(2,1)} all-to-all(bf16[32,16,144]{2,1,0:T(8,128)(2,1)S(1)} %fusion.2), channel_id=1, replica_groups=mesh['sub'=8,'grp'=4] {'sub','grp'}, dimensions={0} | all-to-all | bytes 294912 | tf_op jit(solution)/shard_map/all_to_all | solution.py:8
  26.6 1.3 reshape.70
  27.9 1.7 %convolution_convert_fusion.1 = bf16[32,2304]{1,0:T(8,128)(2,1)} fusion(bf16[32,2304]{1,0:T(8,128)(2,1)S(1)} %reshape.70, s32[32]{0:T(128)} %bitcast.41), kind=kOutput, calls=%fused_computation.2 | convolution fusion | flops 2451968 | bytes 295040 | tf_op jit(solution)/shard_map/of,ok->fk/dot_general | solution.py:44
  29.5 2.0 %reshape.71 = bf16[32,16,144]{2,1,0:T(8,128)(2,1)} reshape(bf16[32,2304]{1,0:T(8,128)(2,1)} %convolution_convert_fusion.1) | data formatting | bytes 294912 | tf_op jit(solution)/shard_map/reshape | solution.py:47
  31.6 12.9 %all_to_all.21 = bf16[32,16,144]{2,1,0:T(8,128)(2,1)S(1)} all-to-all(bf16[32,16,144]{2,1,0:T(8,128)(2,1)} %reshape.71), channel_id=1, replica_groups=mesh['sub'=8,'grp'=4] {'sub','grp'}, dimensions={0} | all-to-all | bytes 294912 | tf_op jit(solution)/shard_map/all_to_all | solution.py:12
  44.5 0.7 copy-done.2
  45.2 1.1 convolution_bitcast_fusion.1
  46.3 1.6 %fusion.9 = f32[512,16]{1,0:T(8,128)} fusion(f32[16,64]{1,0:T(8,128)S(1)} %convolution_bitcast_fusion.1, s32[64]{0:T(128)} %bitcast.43), kind=kOutput, calls=%fused_computation.24 | convolution fusion | flops 6324224 | bytes 37120 | tf_op jit(solution)/shard_map/dot_general | solution.py:65
  47.9 41.1 %psum.7 = f32[512,16]{1,0:T(8,128)} all-reduce(f32[512,16]{1,0:T(8,128)} %fusion.9), channel_id=1, replica_groups=mesh['sub'=8,'grp'=4] {'sub','grp'}, use_global_device_ids=true, to_apply=%region_0.1 | all-reduce | flops 8192 | bytes 65536 | tf_op jit(solution)/shard_map/psum | solution.py:66
  89.0 1.6 %convolution_bitcast_fusion.2 = f32[128,16]{0,1:T(8,128)S(1)} fusion(f32[512,16]{1,0:T(8,128)} %psum.7, f32[128,512]{1,0:T(8,128)} %param.19), kind=kOutput, calls=%fused_computation.15 | convolution fusion | flops 12582912 | bytes 303104 | tf_op jit(solution)/shard_map/dot_general | solution.py:67
  90.7 13.1 %all_gather.3 = f32[512,16]{0,1:T(8,128)S(1)} all-gather(f32[128,16]{0,1:T(8,128)S(1)} %convolution_bitcast_fusion.2), channel_id=1, replica_groups=mesh['sub'=8,'grp'=4] {'grp'}, dimensions={0}, use_global_device_ids=true | all-gather | bytes 40960 | tf_op jit(solution)/shard_map/all_gather | solution.py:68
  104.3 2.4 %fusion.3 = bf16[32,16,144]{2,1,0:T(8,128)(2,1)S(1)} fusion(f32[32,16,144]{2,1,0:T(8,128)S(1)} %convolution_bitcast_fusion, bf16[32,144,144]{2,1,0:T(8,128)(2,1)} %param.16, f32[32]{0:T(128)S(1)} %copy-done.6, bf16[32,16,144]{2,1,0:T(8,128)(2,1)S(1)} %copy-done.3), kind=kOutput, calls=%fused_computation.13 | convolution fusion | flops 21676032 | bytes 1917056 | tf_op jit(solution)/shard_map/lrb,lcb->lrc/dot_general | solution.py:75
  106.7 13.0 %all_to_all.22 = bf16[32,16,144]{2,1,0:T(8,128)(2,1)S(1)} all-to-all(bf16[32,16,144]{2,1,0:T(8,128)(2,1)S(1)} %fusion.3), channel_id=1, replica_groups=mesh['sub'=8,'grp'=4] {'sub','grp'}, dimensions={0} | all-to-all | bytes 294912 | tf_op jit(solution)/shard_map/all_to_all | solution.py:8
  120.3 0.4 reshape.73
  120.7 12.7 %all_to_all.23 = bf16[32,16,144]{2,1,0:T(8,128)(2,1)S(1)} all-to-all(bf16[32,16,144]{2,1,0:T(8,128)(2,1)S(1)} %reshape.73), channel_id=1, replica_groups=mesh['sub'=8,'grp'=4] {'sub','grp'}, dimensions={0} | all-to-all | bytes 294912 | tf_op jit(solution)/shard_map/all_to_all | solution.py:12
  133.4 0.4 fusion.21
  134.5 0.9 fusion.7
  135.4 4.7 %convolution_convert_fusion.4 = bf16[64,16,144]{2,1,0:T(8,128)(2,1)} fusion(bf16[64,144,144]{2,1,0:T(8,128)(2,1)} %param.13, f32[64,16,144]{2,0,1:T(8,128)S(1)} %fusion.7, bf16[64,16,144]{2,1,0:T(8,128)(2,1)} %param.11), kind=kOutput, calls=%fused_computation.5 | convolution fusion | flops 43057152 | bytes 3833856 | tf_op jit(solution)/shard_map/erb,ecb->erc/dot_general | solution.py:90
  140.1 0.7 copy.22
  (24 shorter events, 1.7 us)
Async XLA Ops:
  0.6 6.6 %copy-start = (bf16[32,144,144]{2,1,0:T(8,128)(2,1)S(1)}, bf16[32,144,144]{2,1,0:T(8,128)(2,1)}, u32[]{:S(2)}) copy-start(bf16[32,144,144]{2,1,0:T(8,128)(2,1)} %param.14) | copy-start | bytes 3981316
  1.5 5.8 %copy-start.5 = (f32[32]{0:T(128)}, f32[32]{0:T(128)S(1)}, u32[]{:S(2)}) copy-start(f32[32]{0:T(128)S(1)} %fusion.20) | copy-start | bytes 388
  7.3 38.0 %copy-start.1 = (bf16[32,64,144]{2,1,0:T(8,128)(2,1)S(1)}, bf16[32,64,144]{2,1,0:T(8,128)(2,1)}, u32[]{:S(2)}) copy-start(bf16[32,64,144]{2,1,0:T(8,128)(2,1)} %param.17) | copy-start | bytes 1769476
  29.5 74.3 %copy-start.7 = (s32[1,64]{1,0:T(1,128)S(1)}, s32[1,64]{1,0:T(1,128)}, u32[]{:S(2)}) copy-start(s32[1,64]{1,0:T(1,128)} %param.18) | copy-start | bytes 772
  31.6 72.7 %copy-start.6 = (f32[32]{0:T(128)S(1)}, f32[32]{0:T(128)}, u32[]{:S(2)}) copy-start(f32[32]{0:T(128)} %copy-done.5) | copy-start | bytes 388
  44.5 0.7 copy-start.2
  89.0 15.2 %copy-start.3 = (bf16[32,16,144]{2,1,0:T(8,128)(2,1)S(1)}, bf16[32,16,144]{2,1,0:T(8,128)(2,1)}, u32[]{:S(2)}) copy-start(bf16[32,16,144]{2,1,0:T(8,128)(2,1)} %copy-done.2) | copy-start | bytes 442372
  104.3 15.7 %copy-start.4 = (s32[1,32]{1,0:T(1,128)S(1)}, s32[1,32]{1,0:T(1,128)}, u32[]{:S(2)}) copy-start(s32[1,32]{1,0:T(1,128)} %param.20) | copy-start | bytes 388
  133.4 1.1 copy-start.8
where the time goes:
time: 141 us
  blocking collectives  110 us (78%)
  matrix products  20.8 us (15%)
  local copies, waits for them, and re-layouts  7.45 us (5%)
  other arithmetic  1.48 us (1%)
    psum x1, blocking collectives, body(): coarse_rhs = lax.psum(partial_rhs, ('sub', 'grp'))  41.1 us
    all_to_all x2, blocking collectives, send_out(): lax.all_to_all(partials, ('sub', 'grp'), split_axis=0, concat_axis=0, til...  30.4 us
    all_to_all x2, blocking collectives, send_back(): lax.all_to_all(spread, ('sub', 'grp'), split_axis=0, concat_axis=0, tiled...  25.6 us
    all_gather x1, blocking collectives, body(): coarse_sol = lax.all_gather(row_part, 'grp', axis=0, tiled=True)  13.1 us
    dot_general x1, matrix products, body(): jnp.einsum('erb,ecb->erc', inner_rhs, inner_inv, preferred_element_type=j...  4.68 us
    dot_general x1, matrix products, body(): jnp.einsum('erb,ecb->erc', res_inner, inner_inv, preferred_element_type=j...  3.82 us

commit v1 on v0

v1 whole, which is shorter than its diff:
```python
import jax
import jax.numpy as jnp
from jax import lax
from jax.sharding import PartitionSpec as P

AXES = ("sub", "grp")
DIGIT = 128


def exchange(blocks, axes=AXES):
    return lax.all_to_all(blocks, axes, split_axis=0, concat_axis=0, tiled=True)


def body(
    res_inner,
    res_face,
    inner_inv,
    face_coupling,
    face_elem,
    face_inv,
    coarse_basis,
    coarse_map,
    coarse_inv,
    recv_index,
    sharers,
):
    num_faces, rhs, width = res_face.shape
    num_owned = num_faces // 4
    elements = res_inner.shape[0]
    row_count, num_coarse = coarse_inv.shape
    groups = num_coarse // row_count
    local = coarse_map.shape[1]
    counts = sharers[0]
    weights = jnp.where(counts > 0, 1.0 / jnp.maximum(counts, 1).astype(jnp.float32), 0.0)
    owner_onehot = (
        recv_index[0][None, :] == jnp.arange(num_owned, dtype=jnp.int32)[:, None]
    ).astype(jnp.bfloat16)

    def owner_assemble(received):
        flattened = received.reshape(num_faces, -1)
        owner_sum = jnp.dot(owner_onehot, flattened, preferred_element_type=jnp.float32).astype(
            jnp.bfloat16
        )
        return jnp.einsum(
            "of,ok->fk", owner_onehot, owner_sum, preferred_element_type=jnp.float32
        ).astype(jnp.bfloat16).reshape(num_faces, rhs, width)

    inner_w = jnp.einsum(
        "erb,ecb->erc", res_inner, inner_inv, preferred_element_type=jnp.float32
    ).astype(jnp.bfloat16)
    nearby = inner_w[face_elem[0]]
    condensed = res_face.astype(jnp.float32) - jnp.einsum(
        "lrb,lcb->lrc", nearby, face_coupling, preferred_element_type=jnp.float32
    )
    sent = (weights[:, None, None] * condensed).astype(jnp.bfloat16)
    digits = jnp.stack([coarse_map[0] // DIGIT, coarse_map[0] % DIGIT]).astype(jnp.bfloat16)
    digits = jnp.pad(digits, ((0, rhs - 2), (0, 0)))
    digits = jnp.broadcast_to(digits[None], (num_faces,) + digits.shape)
    first = exchange(jnp.concatenate([sent, digits], -1))
    maps = first[:, :2, width:].astype(jnp.int32)
    maps = (maps[:, 0] * DIGIT + maps[:, 1]).reshape(-1)
    gathered = exchange(owner_assemble(first[:, :, :width]))
    restricted = (weights[:, None, None] * gathered.astype(jnp.float32)).astype(jnp.bfloat16)
    local_coarse = jnp.einsum(
        "ljb,lrb->jr", coarse_basis, restricted, preferred_element_type=jnp.float32
    )
    packed = local_coarse.reshape(-1, 128)
    all_coarse = exchange(jnp.broadcast_to(packed[None], (num_faces,) + packed.shape))
    all_coarse = all_coarse.reshape(num_faces * local, rhs)
    every = (maps[None, :] == jnp.arange(num_coarse, dtype=jnp.int32)[:, None]).astype(jnp.float32)
    coarse_rhs = jnp.dot(every, all_coarse, precision=lax.Precision.HIGHEST)
    row_part = jnp.dot(coarse_inv, coarse_rhs, precision=lax.Precision.HIGHEST)
    packed = row_part.reshape(-1, 128)
    coarse_sol = exchange(jnp.broadcast_to(packed[None], (groups,) + packed.shape), "grp")
    coarse_sol = coarse_sol.reshape(num_coarse, rhs)
    coarse_onehot = (
        coarse_map[0][None, :] == jnp.arange(num_coarse, dtype=jnp.int32)[:, None]
    ).astype(jnp.float32)
    picked = jnp.einsum(
        "kj,kr->jr", coarse_onehot, coarse_sol, precision=lax.Precision.HIGHEST
    ).astype(jnp.bfloat16)
    coarse_part = jnp.einsum(
        "ljb,jr->lrb", coarse_basis, picked, preferred_element_type=jnp.float32
    )
    local_part = jnp.einsum(
        "lrb,lcb->lrc", restricted, face_inv, preferred_element_type=jnp.float32
    )
    weighted = (weights[:, None, None] * (coarse_part + local_part)).astype(jnp.bfloat16)
    face_out = exchange(owner_assemble(exchange(weighted)))
    contrib = jnp.einsum(
        "lrc,lcb->lrb", face_out, face_coupling, preferred_element_type=jnp.float32
    )
    elem_onehot = (face_elem[0][None, :] == jnp.arange(elements, dtype=jnp.int32)[:, None]).astype(
        jnp.float32
    )
    scattered = jnp.dot(
        elem_onehot, contrib.reshape(num_faces, -1), precision=lax.Precision.HIGHEST
    ).reshape(res_inner.shape)
    inner_rhs = (res_inner.astype(jnp.float32) - scattered).astype(jnp.bfloat16)
    inner_out = jnp.einsum(
        "erb,ecb->erc", inner_rhs, inner_inv, preferred_element_type=jnp.float32
    ).astype(jnp.bfloat16)
    return (inner_out, face_out)


def solution(mesh):
    block = P(AXES, None, None)
    row = P(AXES, None)
    return jax.shard_map(
        body,
        mesh=mesh,
        in_specs=(block, block, block, block, row, block, block, row, P("grp", None), row, row),
        out_specs=(block, block),
        check_vma=False,
    )
```

time: 141 us -> 111 us (0.79)
  blocking collectives: 110 us -> 63 us
  waiting for transfers between devices: 0 us -> 6.7 us
  local copies, waits for them, and re-layouts: 7.45 us -> 11.1 us
  starting transfers between devices: 0 us -> 2.66 us
  matrix products: 20.8 us -> 23.2 us
  other arithmetic: 1.48 us -> 3.26 us
    psum x1 -> x0, blocking collectives: 41.1 us -> none  [body(): coarse_rhs = lax.psum(partial_rhs, ('sub', 'grp'))]
    all_gather x1 -> x0, blocking collectives: 13.1 us -> none  [body(): coarse_sol = lax.all_gather(row_part, 'grp', axis=0, tiled=True)]
    all_to_all x4 -> x5, blocking collectives: 56.1 us -> 63 us  [exchange(): return lax.all_to_all(blocks, axes, split_axis=0, concat_axis=0, tiled=True)]
    all_to_all x0 -> x1, waiting for transfers between devices: none -> 6.7 us  [exchange(): return lax.all_to_all(blocks, axes, split_axis=0, concat_axis=0, tiled=True)]
    all_to_all x0 -> x1, starting transfers between devices: none -> 2.66 us  [exchange(): return lax.all_to_all(blocks, axes, split_axis=0, concat_axis=0, tiled=True)]
    reshape x4 -> x6, local copies, waits for them, and re-layouts: 4.08 us -> 5.95 us  [the longest x2 2.28 us: owner_assemble(): flattened = received.reshape(num_faces, -1)]
  transfers between devices with their start and end apart: 0 -> 1, of which waited for: 0 -> 1; matrix products, arithmetic and copies ran while one was open for 0% -> 1% of each run, Pallas kernels for 0% -> 0%
where the time goes in v1:
time: 111 us
  blocking collectives  63 us (57%)
  matrix products  23.2 us (21%)
  local copies, waits for them, and re-layouts  11.1 us (10%)
  waiting for transfers between devices  6.7 us (6%)
  other arithmetic  3.26 us (3%)
  starting transfers between devices  2.66 us (2%)
    all_to_all x5, blocking collectives, exchange(): return lax.all_to_all(blocks, axes, split_axis=0, concat_axis=0, tiled=True)  63 us
    all_to_all x1, waiting for transfers between devices, exchange(): return lax.all_to_all(blocks, axes, split_axis=0, concat_axis=0, tiled=True)  6.7 us
    dot_general x1, matrix products, body(): jnp.einsum('erb,ecb->erc', inner_rhs, inner_inv, preferred_element_type=j...  4.68 us
    dot_general x1, matrix products, body(): jnp.einsum('erb,ecb->erc', res_inner, inner_inv, preferred_element_type=j...  3.82 us
    dot_general x1, matrix products, body(): coarse_rhs = jnp.dot(every, all_coarse, precision=lax.Precision.HIGHEST)  3.34 us
    all_to_all x1, starting transfers between devices, exchange(): return lax.all_to_all(blocks, axes, split_axis=0, concat_axis=0, tiled=True)  2.66 us
    dot_general x1, matrix products, body(): jnp.einsum('lrb,lcb->lrc', restricted, face_inv, preferred_element_type=j...  2.53 us
    reshape x2, local copies, waits for them, and re-layouts, owner_assemble(): flattened = received.reshape(num_faces, -1)  2.28 us
  transfers between devices with their start and end apart: 1, of which 1 were waited for; matrix products, arithmetic and copies ran while one was open for 1% of the time, Pallas kernels for 0%

profile of v1, /device:TPU:0, one launch (start us, length us, event | category | flops | bytes accessed | tf_op | source)
XLA Modules:
  0.0 110.6 jit_solution(539720037215386459)
XLA Ops:
  0.6 0.8 fusion.25
  2.8 3.8 %convolution_convert_fusion.5 = bf16[64,16,144]{2,1,0:T(8,128)(2,1)S(1)} fusion(bf16[64,16,144]{2,1,0:T(8,128)(2,1)} %param.11, bf16[64,144,144]{2,1,0:T(8,128)(2,1)} %param.13), kind=kOutput, calls=%fused_computation.9 | convolution fusion | flops 42614784 | bytes 3244032 | tf_op jit(solution)/shard_map/erb,ecb->erc/dot_general | solution.py:48
  6.6 1.3 %gather_fusion = bf16[32,16,144]{2,1,0:T(8,128)(2,1)} fusion(bf16[64,16,144]{2,1,0:T(8,128)(2,1)S(1)} %convolution_convert_fusion.5, s32[1024]{0:T(1024)S(1)} %pad_clamp_fusion), kind=kCustom, calls=%fused_computation | custom fusion | bytes 295040 | tf_op jit(solution)/shard_map/gather | solution.py:51
  7.9 1.8 %fusion.4 = bf16[32,16,144]{2,1,0:T(8,128)(2,1)S(1)} fusion(bf16[32,16,144]{2,1,0:T(8,128)(2,1)} %gather_fusion, bf16[32,144,144]{2,1,0:T(8,128)(2,1)S(1)} %copy-done, bf16[32,16,144]{2,1,0:T(8,128)(2,1)} %param.12, f32[32]{0:T(128)S(1)} %fusion.25), kind=kOutput, calls=%fused_computation.15 | convolution fusion | flops 21528576 | bytes 1769600 | tf_op jit(solution)/shard_map/lrb,lcb->lrc/dot_general | solution.py:52
  9.9 17.5 %all_to_all.30 = bf16[32,16,208]{2,1,0:T(8,128)(2,1)} all-to-all(bf16[32,16,208]{2,1,0:T(8,128)(2,1)S(1)} %pad_maximum_fusion), channel_id=1, replica_groups=mesh['sub'=8,'grp'=4] {'sub','grp'}, dimensions={0} | all-to-all | bytes 425984 | tf_op jit(solution)/shard_map/all_to_all | solution.py:11
  27.4 2.0 %reshape.92 = bf16[32,2304]{1,0:T(8,128)(2,1)} reshape(bf16[32,16,144]{2,1,0:T(8,128)(2,1)} %bitcast.44) | data formatting | bytes 294912 | tf_op jit(solution)/shard_map/reshape | solution.py:40
  29.4 1.2 %convolution_convert_fusion.1 = bf16[32,2304]{1,0:T(8,128)(2,1)S(1)} fusion(bf16[32,2304]{1,0:T(8,128)(2,1)} %reshape.92, s32[32]{0:T(128)} %bitcast.45), kind=kOutput, calls=%fused_computation.4 | convolution fusion | flops 2451968 | bytes 295040 | tf_op jit(solution)/shard_map/of,ok->fk/dot_general | solution.py:44
  30.6 1.1 %reshape.93 = bf16[32,16,144]{2,1,0:T(8,128)(2,1)} reshape(bf16[32,2304]{1,0:T(8,128)(2,1)S(1)} %convolution_convert_fusion.1) | data formatting | bytes 294912 | tf_op jit(solution)/shard_map/reshape | solution.py:46
  31.7 12.9 %all_to_all.31 = bf16[32,16,144]{2,1,0:T(8,128)(2,1)S(1)} all-to-all(bf16[32,16,144]{2,1,0:T(8,128)(2,1)} %reshape.93), channel_id=1, replica_groups=mesh['sub'=8,'grp'=4] {'sub','grp'}, dimensions={0} | all-to-all | bytes 294912 | tf_op jit(solution)/shard_map/all_to_all | solution.py:11
  45.3 1.1 convolution_bitcast_fusion.1
  47.2 2.7 %all-to-all-start.2 = ((f32[32,8,128]{2,1,0:T(8,128)}), f32[32,8,128]{2,1,0:T(8,128)S(1)}, u32[]{:S(2)}, u32[]{:S(2)}) async-start(f32[32,8,128]{2,1,0:T(8,128)} %broadcast_in_dim.17), calls=%async_computation.2 | async-start | bytes 262144 | tf_op jit(solution)/shard_map/all_to_all | solution.py:11
  49.9 0.9 slice_convert_fusion
  51.6 6.7 %all-to-all-done.2 = f32[32,8,128]{2,1,0:T(8,128)S(1)} async-done(((f32[32,8,128]{2,1,0:T(8,128)}), f32[32,8,128]{2,1,0:T(8,128)S(1)}, u32[]{:S(2)}, u32[]{:S(2)}) %all-to-all-start.2) | async-done | bytes 131104 | tf_op jit(solution)/shard_map/all_to_all | solution.py:11
  58.3 1.3 %reshape.94 = f32[2048,16]{1,0:T(8,128)} reshape(f32[32,8,128]{2,1,0:T(8,128)S(1)} %all-to-all-done.2) | data formatting | bytes 262144 | tf_op jit(solution)/shard_map/reshape | solution.py:69
  59.5 3.3 %fusion = f32[512,16]{1,0:T(8,128)S(1)} fusion(f32[2048,16]{1,0:T(8,128)} %reshape.94, s32[2048]{0:T(1024)} %add.41), kind=kOutput, calls=%fused_computation.2 | convolution fusion | flops 202375168 | bytes 172032 | tf_op jit(solution)/shard_map/dot_general | solution.py:71
  62.9 1.5 %convolution_bitcast_fusion.2 = f32[128,16]{0,1:T(8,128)S(1)} fusion(f32[512,16]{1,0:T(8,128)S(1)} %fusion, f32[128,512]{1,0:T(8,128)} %param.19), kind=kOutput, calls=%fused_computation.18 | convolution fusion | flops 12582912 | bytes 303104 | tf_op jit(solution)/shard_map/dot_general | solution.py:72
  64.6 8.0 %all_to_all.32 = f32[4,16,128]{2,1,0:T(8,128)S(1)} all-to-all(f32[4,16,128]{2,1,0:T(8,128)S(1)} %broadcast_in_dim.19), channel_id=1, replica_groups=mesh['sub'=8,'grp'=4] {'grp'}, dimensions={0} | all-to-all | bytes 65536 | tf_op jit(solution)/shard_map/all_to_all | solution.py:11
  72.6 0.8 reshape.95
  73.4 1.3 %fusion.6 = bf16[64,16,1]{0,1,2:T(8,128)(2,1)S(1)} fusion(f32[512,16]{1,0:T(8,128)} %reshape.95, s32[64]{0:T(128)S(1)} %bitcast.47), kind=kOutput, calls=%fused_computation.20 | convolution fusion | flops 6325248 | bytes 35072 | tf_op jit(solution)/shard_map/kj,kr->jr/dot_general | solution.py:79
  75.0 2.5 %fusion.5 = bf16[32,16,144]{2,1,0:T(8,128)(2,1)S(1)} fusion(f32[32,16,144]{2,1,0:T(8,128)S(1)} %convolution_bitcast_fusion, bf16[32,144,144]{2,1,0:T(8,128)(2,1)} %param.16, f32[32]{0:T(128)S(1)} %copy-done.5, bf16[32,16,144]{2,1,0:T(8,128)(2,1)} %copy-done.2), kind=kOutput, calls=%fused_computation.16 | convolution fusion | flops 21676032 | bytes 1917056 | tf_op jit(solution)/shard_map/lrb,lcb->lrc/dot_general | solution.py:85
  77.6 11.9 %all_to_all.33 = bf16[32,16,144]{2,1,0:T(8,128)(2,1)S(1)} all-to-all(bf16[32,16,144]{2,1,0:T(8,128)(2,1)S(1)} %fusion.5), channel_id=1, replica_groups=mesh['sub'=8,'grp'=4] {'sub','grp'}, dimensions={0} | all-to-all | bytes 294912 | tf_op jit(solution)/shard_map/all_to_all | solution.py:11
  90.5 12.7 %all_to_all.34 = bf16[32,16,144]{2,1,0:T(8,128)(2,1)S(1)} all-to-all(bf16[32,16,144]{2,1,0:T(8,128)(2,1)S(1)} %reshape.97), channel_id=1, replica_groups=mesh['sub'=8,'grp'=4] {'sub','grp'}, dimensions={0} | all-to-all | bytes 294912 | tf_op jit(solution)/shard_map/all_to_all | solution.py:11
  104.3 0.9 fusion.9
  105.2 4.7 %convolution_convert_fusion.4 = bf16[64,16,144]{2,1,0:T(8,128)(2,1)} fusion(bf16[64,144,144]{2,1,0:T(8,128)(2,1)} %param.13, f32[64,16,144]{2,0,1:T(8,128)S(1)} %fusion.9, bf16[64,16,144]{2,1,0:T(8,128)(2,1)} %param.11), kind=kOutput, calls=%fused_computation.8 | convolution fusion | flops 43057152 | bytes 3833856 | tf_op jit(solution)/shard_map/erb,ecb->erc/dot_general | solution.py:100
  (38 shorter events, 7.0 us)
Async XLA Ops:
  0.6 7.3 %copy-start = (bf16[32,144,144]{2,1,0:T(8,128)(2,1)S(1)}, bf16[32,144,144]{2,1,0:T(8,128)(2,1)}, u32[]{:S(2)}) copy-start(bf16[32,144,144]{2,1,0:T(8,128)(2,1)} %param.14) | copy-start | bytes 3981316
  1.5 6.5 %copy-start.4 = (f32[32]{0:T(128)}, f32[32]{0:T(128)S(1)}, u32[]{:S(2)}) copy-start(f32[32]{0:T(128)S(1)} %fusion.25) | copy-start | bytes 388
  7.9 37.4 %copy-start.1 = (bf16[32,64,144]{2,1,0:T(8,128)(2,1)S(1)}, bf16[32,64,144]{2,1,0:T(8,128)(2,1)}, u32[]{:S(2)}) copy-start(bf16[32,64,144]{2,1,0:T(8,128)(2,1)} %param.17) | copy-start | bytes 1769476
  44.6 0.7 copy-start.2
  47.2 11.0 %all-to-all-start.2 = ((f32[32,8,128]{2,1,0:T(8,128)}), f32[32,8,128]{2,1,0:T(8,128)S(1)}, u32[]{:S(2)}, u32[]{:S(2)}) async-start(f32[32,8,128]{2,1,0:T(8,128)} %broadcast_in_dim.17), calls=%async_computation.2 | async-start | bytes 262144 | tf_op jit(solution)/shard_map/all_to_all | solution.py:11
  51.6 21.9 %copy-start.6 = (s32[1,64]{1,0:T(1,128)S(1)}, s32[1,64]{1,0:T(1,128)}, u32[]{:S(2)}) copy-start(s32[1,64]{1,0:T(1,128)} %param.18) | copy-start | bytes 772
  59.5 15.5 %copy-start.5 = (f32[32]{0:T(128)S(1)}, f32[32]{0:T(128)}, u32[]{:S(2)}) copy-start(f32[32]{0:T(128)} %copy-done.4) | copy-start | bytes 388
  75.0 14.8 %copy-start.3 = (s32[1,32]{1,0:T(1,128)S(1)}, s32[1,32]{1,0:T(1,128)}, u32[]{:S(2)}) copy-start(s32[1,32]{1,0:T(1,128)} %param.20) | copy-start | bytes 388
  103.2 1.1 copy-start.7

commit v2 on v1

v2 whole, which is shorter than its diff:
```python
import functools

import jax
import jax.numpy as jnp
from jax import lax
from jax.experimental import pallas as pl
from jax.experimental.pallas import tpu as pltpu
from jax.sharding import PartitionSpec as P

AXES = ("sub", "grp")
DIGIT = 128
LANES = 128
NT = (((1,), (1,)), ((), ()))
NN = (((1,), (0,)), ((), ()))
F32 = jnp.float32
BF16 = jnp.bfloat16
VMEM = pl.BlockSpec(memory_space=pltpu.VMEM)
SMEM = pl.BlockSpec(memory_space=pltpu.SMEM)
ANY = pl.BlockSpec(memory_space=pl.ANY)
GROUP = 8


def exchange(blocks):
    return lax.all_to_all(blocks, AXES, split_axis=0, concat_axis=0, tiled=True)


def dot(a, b, dims=NN):
    return lax.dot_general(a, b, dims, preferred_element_type=F32)


def omega(sharers, slot):
    count = sharers[0, slot]
    return jnp.where(count > 0, 1.0 / jnp.maximum(count, 1).astype(F32), 0.0)


def split(value):
    high = value.astype(BF16)
    return high, (value - high.astype(F32)).astype(BF16)


def pack(out, slot, value, extra):
    rhs, width = value.shape
    tail = width - LANES
    half = rhs // 2
    out[slot, 0:rhs, :] = value[:, :LANES].astype(BF16)
    end = value[:, LANES:]
    out[slot, rhs : rhs + half, :] = jnp.concatenate(
        [end[:half], end[half:], extra[:, 2 * tail :]], axis=1
    ).astype(BF16)


def unpack(ref, slot, rhs, tail):
    half = rhs // 2
    main = ref[slot, 0:rhs, :].astype(F32)
    last = ref[slot, rhs : rhs + half, :].astype(F32)
    end = jnp.concatenate([last[:, :tail], last[:, tail : 2 * tail]], axis=0)
    return jnp.concatenate([main, end], axis=1)


def loop(count, step, group=GROUP):
    group = min(group, count)

    def body(g, carry):
        for u in range(group):
            step(g * group + u)
        return carry

    lax.fori_loop(0, count // group, body, 0)


def condense_kernel(elem, sharers, cmap, inner, inv, couple, face, out, rin, invs, cps, fac, sems):
    slots, rhs, width = fac.shape
    tail = width - LANES
    chunks = slots // GROUP

    def inner_copy(l):
        return pltpu.make_async_copy(inner.at[elem[0, l]], rin.at[l], sems.at[0, l])

    def inv_copy(l):
        return pltpu.make_async_copy(inv.at[elem[0, l]], invs.at[l], sems.at[1, l])

    def couple_copy(c):
        part = pl.ds(c * GROUP, GROUP)
        return pltpu.make_async_copy(couple.at[part], cps.at[part], sems.at[2, c])

    def face_copy(c):
        part = pl.ds(c * GROUP, GROUP)
        return pltpu.make_async_copy(face.at[part], fac.at[part], sems.at[3, c])

    def start(c, carry):
        for u in range(GROUP):
            inner_copy(c * GROUP + u).start()
            inv_copy(c * GROUP + u).start()
        couple_copy(c).start()
        face_copy(c).start()
        return carry

    lax.fori_loop(0, chunks, start, 0)
    maps = cmap[...]
    digits = jnp.concatenate([maps // DIGIT, maps % DIGIT], axis=0).astype(F32)
    local = digits.shape[1]
    digits = jnp.concatenate([digits, jnp.zeros((rhs // 2 - 2, local), F32)], axis=0)
    extra = jnp.concatenate([jnp.zeros((rhs // 2, LANES - local), F32), digits], axis=1)

    def chunk(c, carry):
        for u in range(GROUP):
            inner_copy(c * GROUP + u).wait()
            inv_copy(c * GROUP + u).wait()
        couple_copy(c).wait()
        face_copy(c).wait()
        for u in range(GROUP):
            l = c * GROUP + u
            near = dot(rin[l], invs[l], NT).astype(BF16)
            value = fac[l].astype(F32) - dot(near, cps[l], NT)
            pack(out, l, omega(sharers, l) * value, extra)
        return carry

    lax.fori_loop(0, chunks, chunk, 0)


def owner_kernel(recv, got, out, sums, rounded):
    slots = got.shape[0]
    owned = sums.shape[0] - 1
    sums[...] = jnp.zeros_like(sums)

    def add(s):
        j = recv[0, s]
        sums[j] += got[s].astype(F32)

    loop(slots, add)
    rounded[...] = sums[...].astype(BF16)
    rounded[owned] = jnp.zeros(rounded.shape[1:], BF16)

    def give(s):
        out[s] = rounded[recv[0, s]]

    loop(slots, give)


def pair_maps(first, d, rhs, local):
    at = LANES - local
    low = first[d, rhs : rhs + rhs // 2, :].astype(F32)
    top = first[d + 1, rhs : rhs + rhs // 2, :].astype(F32)
    low = (low[0:1] * DIGIT + low[1:2])[:, at:]
    top = (top[0:1] * DIGIT + top[1:2])[:, at:]
    return jnp.concatenate([low, top], axis=1)


def columns_kernel(first, cinv, out):
    devices, piece, _ = out.shape
    total = cinv.shape[1]
    local = LANES // 2
    rhs = first.shape[1] * 2 // 3
    start = pl.multiple_of(lax.axis_index("sub") * piece, piece)
    high, low = split(cinv[pl.ds(start, piece), :])
    both = jnp.concatenate([high, low], axis=0)
    place = lax.broadcasted_iota(jnp.int32, (total, LANES), 0).astype(F32)

    def step(p, carry):
        row = pair_maps(first, 2 * p, rhs, local)
        one = jnp.where(place == row, 1.0, 0.0).astype(BF16)
        got = dot(both, one)
        out[2 * p] = jnp.concatenate([got[:piece, :local], got[piece:, :local]], axis=1).astype(BF16)
        out[2 * p + 1] = jnp.concatenate([got[:piece, local:], got[piece:, local:]], axis=1).astype(BF16)
        return carry

    lax.fori_loop(0, devices // 2, step, 0)


def restrict_kernel(sharers, got, basis, cols, out, restricted, total):
    slots, rhs, width = restricted.shape
    tail = width - LANES
    total[...] = jnp.zeros_like(total)

    def body(g, carry):
        part = None
        for u in range(GROUP):
            l = g * GROUP + u
            value = (omega(sharers, l) * unpack(got, l, rhs, tail)).astype(BF16)
            restricted[l] = value
            term = dot(value, basis[l], NT)
            part = term if part is None else part + term
        total[...] += part
        return carry

    lax.fori_loop(0, slots // GROUP, body, 0)
    high, low = split(total[...])
    block = jnp.concatenate([high, low], axis=1)

    def give(d):
        out[d, 0:rhs, :] = block
        out[d, rhs:, :] = cols[d]

    loop(slots, give)


def local_kernel(restricted, inv, out):
    def step(l):
        out[l] = dot(restricted[l], inv[l], NT)

    loop(out.shape[0], step)


def correct_kernel(groups, rows, sharers, got, first, near, basis, out, sums):
    slots, rhs, width = near.shape
    local = basis.shape[1]
    total = sums.shape[1]
    piece = got.shape[1] - rhs
    sums[...] = jnp.zeros_like(sums)
    q = lax.broadcasted_iota(jnp.int32, (total, LANES), 0)
    device = q // piece
    place = ((device % groups) * rows + (device // groups) * piece + q % piece).astype(F32)
    lane = lax.broadcasted_iota(jnp.int32, (rhs, LANES), 1)

    def step(p, carry):
        row = pair_maps(first, 2 * p, rhs, local)
        one = jnp.where(place == row, 1.0, 0.0).astype(BF16)
        a = got[2 * p, 0:rhs, :].astype(F32)
        b = got[2 * p + 1, 0:rhs, :].astype(F32)
        high = jnp.where(lane < local, a, pltpu.roll(b, local, 1))
        low = jnp.where(lane < local, pltpu.roll(a, local, 1), b)
        sums[...] += dot(jnp.concatenate([high, low], axis=0).astype(BF16), one, NT)
        return carry

    lax.fori_loop(0, slots // 2, step, 0)
    high, low = split(sums[0:rhs, :] + sums[rhs:, :])
    columns = got[:, rhs:, :].reshape(total, LANES)
    prod = dot(jnp.concatenate([high, low], axis=0), columns)
    picked = (prod[:rhs, :local] + prod[:rhs, local:] + prod[rhs:, :local]).astype(BF16)
    extra = jnp.zeros((rhs // 2, LANES), F32)

    def finish(l):
        value = dot(picked, basis[l]) + near[l]
        pack(out, l, omega(sharers, l) * value, extra)

    loop(slots, finish)


def inner_kernel(inner, inv, out):
    for u in range(out.shape[0]):
        out[u] = dot(inner[u], inv[u], NT)


def joint_kernel(elem, couple, inv, out):
    def step(l):
        out[l] = dot(couple[l], inv[elem[0, l]], NT).astype(BF16)

    loop(out.shape[0], step, 2)


def extend_kernel(elem, got, joint, base, inner_out, face_out, sums):
    slots, rhs, width = face_out.shape
    tail = width - LANES
    sums[...] = base[...]

    def step(l):
        value = unpack(got, l, rhs, tail).astype(BF16)
        face_out[l] = value
        sums[elem[0, l]] -= dot(value, joint[l])

    loop(slots, step)
    inner_out[...] = sums[...].astype(BF16)


def call(kernel, out_shape, in_specs, scratch=(), flops=0, limit=None, name=None):
    many = isinstance(out_shape, (tuple, list))
    return pl.pallas_call(
        kernel,
        out_shape=out_shape,
        in_specs=in_specs,
        out_specs=tuple(VMEM for _ in out_shape) if many else VMEM,
        scratch_shapes=list(scratch),
        cost_estimate=pl.CostEstimate(flops=flops, bytes_accessed=flops // 16, transcendentals=0),
        compiler_params=pltpu.CompilerParams(vmem_limit_bytes=limit) if limit else None,
        name=name,
    )


def body(
    res_inner,
    res_face,
    inner_inv,
    face_coupling,
    face_elem,
    face_inv,
    coarse_basis,
    coarse_map,
    coarse_inv,
    recv_index,
    sharers,
):
    slots, rhs, width = res_face.shape
    owned = slots // 4
    elements = res_inner.shape[0]
    rows, total = coarse_inv.shape
    groups = total // rows
    piece = rows * groups // slots
    shape = jax.ShapeDtypeStruct
    block_rows = rhs + rhs // 2
    wire = shape((slots, block_rows, LANES), BF16)
    unit = 2 * rhs * width * width

    sent = call(
        condense_kernel,
        wire,
        [SMEM, SMEM, VMEM, ANY, ANY, ANY, ANY],
        [
            pltpu.VMEM((slots, rhs, width), BF16),
            pltpu.VMEM((slots, width, width), BF16),
            pltpu.VMEM((slots, width, width), BF16),
            pltpu.VMEM((slots, rhs, width), BF16),
            pltpu.SemaphoreType.DMA((4, slots)),
        ],
        flops=2 * slots * unit,
        name="condense",
    )(face_elem, sharers, coarse_map, res_inner, inner_inv, face_coupling, res_face)
    first = exchange(sent)

    owner = call(
        owner_kernel,
        wire,
        [SMEM, VMEM],
        [pltpu.VMEM((owned + 1, block_rows, LANES), F32), pltpu.VMEM((owned + 1, block_rows, LANES), BF16)],
        flops=slots * block_rows * LANES,
        name="owner",
    )
    inner_w = pl.pallas_call(
        inner_kernel,
        out_shape=shape((elements, rhs, width), F32),
        grid=(elements // GROUP,),
        in_specs=[
            pl.BlockSpec((GROUP, rhs, width), lambda i: (i, 0, 0)),
            pl.BlockSpec((GROUP, width, width), lambda i: (i, 0, 0)),
        ],
        out_specs=pl.BlockSpec((GROUP, rhs, width), lambda i: (i, 0, 0)),
        cost_estimate=pl.CostEstimate(flops=elements * unit, bytes_accessed=6 << 20, transcendentals=0),
        name="inner",
    )(res_inner, inner_inv)
    joint = call(
        joint_kernel, shape((slots, width, width), BF16), [SMEM, VMEM, VMEM], flops=9 * slots * unit, name="joint"
    )(face_elem, face_coupling, inner_inv)

    gathered = exchange(owner(recv_index, first))
    columns = call(
        columns_kernel,
        shape((slots, piece, LANES), BF16),
        [VMEM, VMEM],
        flops=4 * piece * total * slots * LANES // 2,
        name="columns",
    )(first, coarse_inv)
    coarse, restricted = call(
        restrict_kernel,
        (shape((slots, rhs + piece, LANES), BF16), shape((slots, rhs, width), BF16)),
        [SMEM, VMEM, VMEM, VMEM],
        [pltpu.VMEM((rhs, coarse_map.shape[1]), F32)],
        flops=slots * unit // 2,
        name="restrict",
    )(sharers, gathered, coarse_basis, columns)
    every = exchange(coarse)
    near = call(
        local_kernel, shape((slots, rhs, width), F32), [VMEM, VMEM], flops=slots * unit, name="local"
    )(restricted, face_inv)
    weighted = call(
        functools.partial(correct_kernel, groups, rows),
        wire,
        [SMEM, VMEM, VMEM, VMEM, VMEM],
        [pltpu.VMEM((2 * rhs, total), F32)],
        flops=slots * unit // 2,
        name="correct",
    )(sharers, every, first, near, coarse_basis)
    assembled = exchange(owner(recv_index, exchange(weighted)))
    return call(
        extend_kernel,
        (shape((elements, rhs, width), BF16), shape((slots, rhs, width), BF16)),
        [SMEM, VMEM, VMEM, VMEM],
        [pltpu.VMEM((elements, rhs, width), F32)],
        flops=slots * unit,
        name="extend",
    )(face_elem, assembled, joint, inner_w)


def solution(mesh):
    block = P(AXES, None, None)
    row = P(AXES, None)
    return jax.shard_map(
        body,
        mesh=mesh,
        in_specs=(block, block, block, block, row, block, block, row, P("grp", None), row, row),
        out_specs=(block, block),
        check_vma=False,
    )
```

time: 111 us -> 99.9 us (0.900)
  Pallas kernels: 0 us -> 49.5 us
  blocking collectives: 63 us -> 29.3 us
  matrix products: 23.2 us -> 0 us
  local copies, waits for them, and re-layouts: 11.1 us -> 2.05 us
  starting transfers between devices: 2.66 us -> 7.99 us
  other arithmetic: 3.26 us -> 0 us
  waiting for transfers between devices: 6.7 us -> 9.6 us
    pallas_call x0 -> x10, Pallas kernels: none -> 49.5 us  [the longest x1 7.87 us: body(): call(joint_kernel, shape((slots, width, width), BF16), [SMEM, VMEM, VMEM]...]
    all_to_all x5 -> x2, blocking collectives: 63 us -> 29.3 us  [exchange(): return lax.all_to_all(blocks, AXES, split_axis=0, concat_axis=0, tiled=True)]
    dot_general x13 -> x0, matrix products: 23.2 us -> none  [the longest x1 4.68 us: body(): jnp.einsum('erb,ecb->erc', inner_rhs, inner_inv, preferred_element_type=j...]
    reshape x7 -> x0, local copies, waits for them, and re-layouts: 6.22 us -> none  [the longest x2 2.28 us: owner_assemble(): flattened = received.reshape(num_faces, -1)]
    all_to_all x1 -> x3, starting transfers between devices: 2.66 us -> 7.99 us  [exchange(): return lax.all_to_all(blocks, AXES, split_axis=0, concat_axis=0, tiled=True)]
    all_to_all x1 -> x3, waiting for transfers between devices: 6.7 us -> 9.6 us  [exchange(): return lax.all_to_all(blocks, AXES, split_axis=0, concat_axis=0, tiled=True)]
    select_n x2 -> x0, other arithmetic: 1.47 us -> none  [the longest x1 0.81 us: body(): jnp.where(counts > 0, 1.0 / jnp.maximum(counts, 1).astype(jnp.float32), 0.0)]
    gather x1 -> x0, local copies, waits for them, and re-layouts: 1.29 us -> none  [body(): nearby = inner_w[face_elem[0]]]
  transfers between devices with their start and end apart: 1 -> 3, of which waited for: 1 -> 2; matrix products, arithmetic and copies ran while one was open for 1% -> 0% of each run, Pallas kernels for 0% -> 25%
where the time goes in v2:
time: 99.9 us; the launch traced here: 99.2 us
  Pallas kernels  49.5 us (50%)
  blocking collectives  29.3 us (29%)
  waiting for transfers between devices  9.6 us (10%)
  starting transfers between devices  7.99 us (8%)
  local copies, waits for them, and re-layouts  2.05 us (2%)
    all_to_all x2, blocking collectives, exchange(): return lax.all_to_all(blocks, AXES, split_axis=0, concat_axis=0, tiled=True)  29.3 us
    all_to_all x3, waiting for transfers between devices, exchange(): return lax.all_to_all(blocks, AXES, split_axis=0, concat_axis=0, tiled=True)  9.6 us
    all_to_all x3, starting transfers between devices, exchange(): return lax.all_to_all(blocks, AXES, split_axis=0, concat_axis=0, tiled=True)  7.99 us
    pallas_call x1, Pallas kernels, body(): call(joint_kernel, shape((slots, width, width), BF16), [SMEM, VMEM, VMEM]...  7.87 us
    pallas_call x1, Pallas kernels, body(): call(functools.partial(correct_kernel, groups, rows), wire, [SMEM, VMEM,...  7.2 us
    pallas_call x1, Pallas kernels, body(): pl.pallas_call(inner_kernel, out_shape=shape((elements, rhs, width), F32)...  7.02 us
    pallas_call x1, Pallas kernels, body(): call(condense_kernel, wire, [SMEM, SMEM, VMEM, ANY, ANY, ANY, ANY], [pltp...  6.62 us
    pallas_call x1, Pallas kernels, body(): call(columns_kernel, shape((slots, piece, LANES), BF16), [VMEM, VMEM], fl...  6.3 us
  transfers between devices with their start and end apart: 3, of which 2 were waited for; matrix products, arithmetic and copies ran while one was open for 0% of the time, Pallas kernels for 25%

profile of v2, /device:TPU:0, one launch (start us, length us, event | category | flops | bytes accessed | tf_op | source)
XLA Modules:
  0.0 99.2 jit_solution(2958005320023484952)
XLA Ops:
  0.6 6.6 %condense.1 = bf16[32,24,128]{2,1,0:T(8,128)(2,1)} custom-call(s32[1,32]{1,0:T(1,128)} %elem.5, s32[1,32]{1,0:T(1,128)} %sharers.5, s32[1,64]{1,0:T(1,128)} %cmap.1, bf16[64,16,144]{2,1,0:T(8,128)(2,1)} %inner.5, bf16[64,144,144]{2,1,0:T(8,128)(2,1)} %inv.7, bf16[32,144,144]{2,1,0:T(8,128)(2,1)} %couple.3, bf16[32,16,144]{2,1,0:T(8,128)(2,1)} %face.1), custom_call_target="tpu_custom_call" | custom-call | flops 42467328 | bytes 2654208 | tf_op jit(solution)/shard_map/condense/pallas_call | solution.py:303
  7.3 16.8 %all_to_all.25.got.first = bf16[32,24,128]{2,1,0:T(8,128)(2,1)} all-to-all(bf16[32,24,128]{2,1,0:T(8,128)(2,1)} %condense.1), channel_id=1, replica_groups=mesh['sub'=8,'grp'=4] {'sub','grp'}, dimensions={0} | all-to-all | bytes 393216 | tf_op jit(solution)/shard_map/all_to_all | solution.py:24
  24.0 1.9 %owner.2 = bf16[32,24,128]{2,1,0:T(8,128)(2,1)} custom-call(s32[1,32]{1,0:T(1,128)} %recv.3, bf16[32,24,128]{2,1,0:T(8,128)(2,1)} %all_to_all.25.got.first), custom_call_target="tpu_custom_call" | custom-call | flops 98304 | bytes 6144 | tf_op jit(solution)/shard_map/owner/pallas_call | solution.py:343
  25.9 2.6 %all-to-all-start.1 = ((bf16[32,24,128]{2,1,0:T(8,128)(2,1)}), bf16[32,24,128]{2,1,0:T(8,128)(2,1)S(1)}, u32[]{:S(2)}, u32[]{:S(2)}) async-start(bf16[32,24,128]{2,1,0:T(8,128)(2,1)} %owner.2), calls=%async_computation.1 | async-start | bytes 393216 | tf_op jit(solution)/shard_map/all_to_all | solution.py:24
  28.5 6.3 %columns.1.cols = bf16[32,16,128]{2,1,0:T(8,128)(2,1)} custom-call(bf16[32,24,128]{2,1,0:T(8,128)(2,1)} %all_to_all.25.got.first, f32[128,512]{1,0:T(8,128)} %cinv.1), custom_call_target="tpu_custom_call" | custom-call | flops 67108864 | bytes 4194304 | tf_op jit(solution)/shard_map/columns/pallas_call | solution.py:344
  34.8 3.0 %all-to-all-done.1.got = bf16[32,24,128]{2,1,0:T(8,128)(2,1)S(1)} async-done(((bf16[32,24,128]{2,1,0:T(8,128)(2,1)}), bf16[32,24,128]{2,1,0:T(8,128)(2,1)S(1)}, u32[]{:S(2)}, u32[]{:S(2)}) %all-to-all-start.1) | async-done | bytes 196640 | tf_op jit(solution)/shard_map/all_to_all | solution.py:24
  37.8 0.0 copy-start.1
  37.8 0.7 copy-done.1
  38.5 3.1 %restrict.1 = (bf16[32,32,128]{2,1,0:T(8,128)(2,1)}, bf16[32,16,144]{2,1,0:T(8,128)(2,1)}) custom-call(s32[1,32]{1,0:T(1,128)} %sharers.5, bf16[32,24,128]{2,1,0:T(8,128)(2,1)} %copy-done.1, bf16[32,64,144]{2,1,0:T(8,128)(2,1)} %basis.3, bf16[32,16,128]{2,1,0:T(8,128)(2,1)} %columns.1.cols), custom_call_target="tpu_custom_call" | custom-call | flops 10616832 | bytes 663552 | tf_op jit(solution)/shard_map/restrict/pallas_call | solution.py:351
  41.7 2.8 %all-to-all-start.2 = ((bf16[32,32,128]{2,1,0:T(8,128)(2,1)}), bf16[32,32,128]{2,1,0:T(8,128)(2,1)S(1)}, u32[]{:S(2)}, u32[]{:S(2)}) async-start(bf16[32,32,128]{2,1,0:T(8,128)(2,1)} %get-tuple-element.4), calls=%async_computation.2 | async-start | bytes 524288 | tf_op jit(solution)/shard_map/all_to_all | solution.py:24
  44.5 3.6 %local.1.near = f32[32,16,144]{2,1,0:T(8,128)} custom-call(bf16[32,16,144]{2,1,0:T(8,128)(2,1)} %get-tuple-element.5.restricted, bf16[32,144,144]{2,1,0:T(8,128)(2,1)} %inv.5), custom_call_target="tpu_custom_call" | custom-call | flops 21233664 | bytes 1327104 | tf_op jit(solution)/shard_map/local/pallas_call | solution.py:360
  48.1 6.6 %all-to-all-done.2.got = bf16[32,32,128]{2,1,0:T(8,128)(2,1)S(1)} async-done(((bf16[32,32,128]{2,1,0:T(8,128)(2,1)}), bf16[32,32,128]{2,1,0:T(8,128)(2,1)S(1)}, u32[]{:S(2)}, u32[]{:S(2)}) %all-to-all-start.2) | async-done | bytes 262176 | tf_op jit(solution)/shard_map/all_to_all | solution.py:24
  54.7 0.0 copy-start
  54.7 0.7 copy-done
  55.4 7.2 %correct.1 = bf16[32,24,128]{2,1,0:T(8,128)(2,1)} custom-call(s32[1,32]{1,0:T(1,128)} %sharers.5, bf16[32,32,128]{2,1,0:T(8,128)(2,1)} %copy-done, bf16[32,24,128]{2,1,0:T(8,128)(2,1)} %all_to_all.25.got.first, f32[32,16,144]{2,1,0:T(8,128)} %local.1.near, bf16[32,64,144]{2,1,0:T(8,128)(2,1)} %basis.3), custom_call_target="tpu_custom_call" | custom-call | flops 10616832 | bytes 663552 | tf_op jit(solution)/shard_map/correct/pallas_call | solution.py:363
  62.6 12.6 %all_to_all.26.got = bf16[32,24,128]{2,1,0:T(8,128)(2,1)} all-to-all(bf16[32,24,128]{2,1,0:T(8,128)(2,1)} %correct.1), channel_id=1, replica_groups=mesh['sub'=8,'grp'=4] {'sub','grp'}, dimensions={0} | all-to-all | bytes 393216 | tf_op jit(solution)/shard_map/all_to_all | solution.py:24
  75.2 1.9 %owner.3 = bf16[32,24,128]{2,1,0:T(8,128)(2,1)} custom-call(s32[1,32]{1,0:T(1,128)} %recv.3, bf16[32,24,128]{2,1,0:T(8,128)(2,1)} %all_to_all.26.got), custom_call_target="tpu_custom_call" | custom-call | flops 98304 | bytes 6144 | tf_op jit(solution)/shard_map/owner/pallas_call | solution.py:371
  77.1 2.6 %all-to-all-start.4 = ((bf16[32,24,128]{2,1,0:T(8,128)(2,1)}), bf16[32,24,128]{2,1,0:T(8,128)(2,1)S(1)}, u32[]{:S(2)}, u32[]{:S(2)}) async-start(bf16[32,24,128]{2,1,0:T(8,128)(2,1)} %owner.3), calls=%async_computation.4 | async-start | bytes 393216 | tf_op jit(solution)/shard_map/all_to_all | solution.py:24
  79.7 7.0 %inner.4.base = f32[64,16,144]{2,1,0:T(8,128)} custom-call(bf16[64,16,144]{2,1,0:T(8,128)(2,1)} %inner.5, bf16[64,144,144]{2,1,0:T(8,128)(2,1)} %inv.7), custom_call_target="tpu_custom_call" | custom-call | flops 42467328 | bytes 6291456 | tf_op jit(solution)/shard_map/inner/pallas_call | solution.py:327
  86.7 7.9 %joint.1 = bf16[32,144,144]{2,1,0:T(8,128)(2,1)} custom-call(s32[1,32]{1,0:T(1,128)} %elem.5, bf16[32,144,144]{2,1,0:T(8,128)(2,1)} %couple.3, bf16[64,144,144]{2,1,0:T(8,128)(2,1)} %inv.7), custom_call_target="tpu_custom_call" | custom-call | flops 191102976 | bytes 11943936 | tf_op jit(solution)/shard_map/joint/pallas_call | solution.py:339
  94.6 0.0 all-to-all-done.4.got
  94.6 0.0 copy-start.2
  94.6 0.7 copy-done.2
  95.3 3.9 %extend.1 = (bf16[64,16,144]{2,1,0:T(8,128)(2,1)}, bf16[32,16,144]{2,1,0:T(8,128)(2,1)}) custom-call(s32[1,32]{1,0:T(1,128)} %elem.5, bf16[32,24,128]{2,1,0:T(8,128)(2,1)} %copy-done.2, bf16[32,144,144]{2,1,0:T(8,128)(2,1)} %joint.1, f32[64,16,144]{2,1,0:T(8,128)} %inner.4.base), custom_call_target="tpu_custom_call" | custom-call | flops 21233664 | bytes 1327104 | tf_op jit(solution)/shard_map/extend/pallas_call | solution.py:372
Async XLA Ops:
  25.9 11.9 %all-to-all-start.1 = ((bf16[32,24,128]{2,1,0:T(8,128)(2,1)}), bf16[32,24,128]{2,1,0:T(8,128)(2,1)S(1)}, u32[]{:S(2)}, u32[]{:S(2)}) async-start(bf16[32,24,128]{2,1,0:T(8,128)(2,1)} %owner.2), calls=%async_computation.1 | async-start | bytes 393216 | tf_op jit(solution)/shard_map/all_to_all | solution.py:24
  37.8 0.7 copy-start.1
  41.7 13.1 %all-to-all-start.2 = ((bf16[32,32,128]{2,1,0:T(8,128)(2,1)}), bf16[32,32,128]{2,1,0:T(8,128)(2,1)S(1)}, u32[]{:S(2)}, u32[]{:S(2)}) async-start(bf16[32,32,128]{2,1,0:T(8,128)(2,1)} %get-tuple-element.4), calls=%async_computation.2 | async-start | bytes 524288 | tf_op jit(solution)/shard_map/all_to_all | solution.py:24
  54.7 0.7 copy-start
  77.1 17.5 %all-to-all-start.4 = ((bf16[32,24,128]{2,1,0:T(8,128)(2,1)}), bf16[32,24,128]{2,1,0:T(8,128)(2,1)S(1)}, u32[]{:S(2)}, u32[]{:S(2)}) async-start(bf16[32,24,128]{2,1,0:T(8,128)(2,1)} %owner.3), calls=%async_computation.4 | async-start | bytes 393216 | tf_op jit(solution)/shard_map/all_to_all | solution.py:24
  94.6 0.7 copy-start.2

commit v3 on v2

v3 whole, which is shorter than its diff:
```python
import functools

import jax
import jax.numpy as jnp
from jax import lax
from jax.experimental import pallas as pl
from jax.experimental.pallas import tpu as pltpu
from jax.sharding import PartitionSpec as P

AXES = ("sub", "grp")
DIGIT = 128
LANES = 128
NT = (((1,), (1,)), ((), ()))
NN = (((1,), (0,)), ((), ()))
F32 = jnp.float32
BF16 = jnp.bfloat16
VMEM = pl.BlockSpec(memory_space=pltpu.VMEM)
SMEM = pl.BlockSpec(memory_space=pltpu.SMEM)
HBM = pl.BlockSpec(memory_space=pltpu.HBM)
CHUNK = 16


def exchange(blocks):
    return lax.all_to_all(blocks, AXES, split_axis=0, concat_axis=0, tiled=True)


def dot(a, b, dims=NN):
    return lax.dot_general(a, b, dims, preferred_element_type=F32)


def omega(sharers, slot):
    count = sharers[0, slot]
    return jnp.where(count > 0, 1.0 / jnp.maximum(count, 1).astype(F32), 0.0)


def split(value):
    high = value.astype(BF16)
    return high, (value - high.astype(F32)).astype(BF16)


def pack(out, slot, value, extra):
    rhs, width = value.shape
    tail = width - LANES
    half = rhs // 2
    out[slot, 0:rhs, :] = value[:, :LANES].astype(BF16)
    end = value[:, LANES:]
    out[slot, rhs : rhs + half, :] = jnp.concatenate(
        [end[:half], end[half:], extra[:, 2 * tail :]], axis=1
    ).astype(BF16)


def unpack(ref, slot, rhs, tail):
    half = rhs // 2
    main = ref[slot, 0:rhs, :].astype(F32)
    last = ref[slot, rhs : rhs + half, :].astype(F32)
    end = jnp.concatenate([last[:, :tail], last[:, tail : 2 * tail]], axis=0)
    return jnp.concatenate([main, end], axis=1)


def loop(count, step, group=16):
    group = min(group, count)

    def body(g, carry):
        for u in range(group):
            step(g * group + u)
        return carry

    lax.fori_loop(0, count // group, body, 0)


def condense_kernel(
    elem_in, sharers_in, cmap, inner, inv, couple, face, out, elem, sharers, rin, invs, cps, fac, sems, small
):
    slots, rhs, width = fac.shape
    tail = width - LANES
    chunks = slots // CHUNK

    def inner_copy(l):
        return pltpu.make_async_copy(inner.at[elem[0, l]], rin.at[l], sems.at[0, l])

    def inv_copy(l):
        return pltpu.make_async_copy(inv.at[elem[0, l]], invs.at[l], sems.at[1, l])

    def couple_copy(c):
        part = pl.ds(c * CHUNK, CHUNK)
        return pltpu.make_async_copy(couple.at[part], cps.at[part], sems.at[2, c])

    def face_copy(c):
        part = pl.ds(c * CHUNK, CHUNK)
        return pltpu.make_async_copy(face.at[part], fac.at[part], sems.at[3, c])

    elem_copy = pltpu.make_async_copy(elem_in, elem, small.at[0])
    sharers_copy = pltpu.make_async_copy(sharers_in, sharers, small.at[1])
    elem_copy.start()
    sharers_copy.start()
    elem_copy.wait()

    def start(c, carry):
        for u in range(CHUNK):
            inner_copy(c * CHUNK + u).start()
            inv_copy(c * CHUNK + u).start()
        couple_copy(c).start()
        face_copy(c).start()
        return carry

    lax.fori_loop(0, chunks, start, 0)
    maps = cmap[...]
    digits = jnp.concatenate([maps // DIGIT, maps % DIGIT], axis=0).astype(F32)
    local = digits.shape[1]
    digits = jnp.concatenate([digits, jnp.zeros((rhs // 2 - 2, local), F32)], axis=0)
    extra = jnp.concatenate([jnp.zeros((rhs // 2, LANES - local), F32), digits], axis=1)
    sharers_copy.wait()

    def chunk(c, carry):
        for u in range(CHUNK):
            inner_copy(c * CHUNK + u).wait()
            inv_copy(c * CHUNK + u).wait()
        couple_copy(c).wait()
        face_copy(c).wait()
        for u in range(CHUNK):
            l = c * CHUNK + u
            near = dot(rin[l], invs[l], NT).astype(BF16)
            value = fac[l].astype(F32) - dot(near, cps[l], NT)
            pack(out, l, omega(sharers, l) * value, extra)
        return carry

    lax.fori_loop(0, chunks, chunk, 0)


def assemble(recv, got, out, sums, rounded):
    slots = got.shape[0]
    rows = sums.shape[1]
    owned = sums.shape[0] - 1
    sums[...] = jnp.zeros_like(sums)

    def add(s):
        j = recv[0, s]
        sums[j] += got[s, :rows, :].astype(F32)

    loop(slots, add)
    rounded[...] = sums[...].astype(BF16)
    rounded[owned] = jnp.zeros(rounded.shape[1:], BF16)

    def give(s):
        out[s, :rows, :] = rounded[recv[0, s]]

    loop(slots, give)


def pair_digits(first, d, rhs, local):
    at = LANES - local
    low = first[d, rhs : rhs + rhs // 2, :].astype(F32)
    top = first[d + 1, rhs : rhs + rhs // 2, :].astype(F32)
    both = jnp.concatenate([low[:, at:], top[:, at:]], axis=1).astype(jnp.int32)
    return both[0:1], both[1:2]


def take_lanes(ref, tile, lane):
    rows, total = ref.shape
    lane = jnp.broadcast_to(lane, (rows, LANES))
    tile = jnp.broadcast_to(tile, (rows, LANES))
    taken = None
    for t in range(total // LANES):
        part = jnp.take_along_axis(ref[:, t * LANES : (t + 1) * LANES], lane, axis=1)
        taken = part if taken is None else jnp.where(tile == t, part, taken)
    return taken


def owner_kernel(recv, got, out, sums, rounded):
    assemble(recv, got, out, sums, rounded)


def first_owner_kernel(recv, got, cinv, out, sums, rounded, strip):
    slots, height, _ = out.shape
    head = got.shape[1]
    piece = height - head
    rhs = head * 2 // 3
    local = LANES // 2
    assemble(recv, got, out, sums, rounded)
    start = pl.multiple_of(lax.axis_index("sub") * piece, piece)
    strip[...] = cinv[pl.ds(start, piece), :]
    left = lax.broadcasted_iota(jnp.int32, (piece, LANES), 1) < local

    def step(p):
        taken = take_lanes(strip, *pair_digits(got, 2 * p, rhs, local))
        high = taken.astype(BF16).astype(F32)
        low = taken - high
        out[2 * p, head:, :] = jnp.where(left, high, pltpu.roll(low, local, 1)).astype(BF16)
        out[2 * p + 1, head:, :] = jnp.where(left, pltpu.roll(high, local, 1), low).astype(BF16)

    loop(slots // 2, step, 8)


def restrict_kernel(sharers, got, basis, out, restricted, total):
    slots, rhs, width = restricted.shape
    tail = width - LANES
    group = min(slots, 16)
    total[...] = jnp.zeros_like(total)

    def body(g, carry):
        part = None
        for u in range(group):
            l = g * group + u
            value = (omega(sharers, l) * unpack(got, l, rhs, tail)).astype(BF16)
            restricted[l] = value
            term = dot(value, basis[l], NT)
            part = term if part is None else part + term
        total[...] += part
        return carry

    lax.fori_loop(0, slots // group, body, 0)
    high, low = split(total[...])
    block = jnp.concatenate([high, low], axis=1)

    def give(d):
        out[d] = block

    loop(slots, give)


def turn_columns(groups, rows, got, head, piece, turned):
    local, total = turned.shape
    for t in range(total // LANES):
        parts = []
        for k in range(t * LANES, (t + 1) * LANES, piece):
            device = (k % rows) // piece * groups + k // rows
            parts.append(got[device, head:, :].astype(F32))
        part = jnp.concatenate(parts, axis=0)
        part = part + pltpu.roll(part, local, 1)
        turned[:, t * LANES : (t + 1) * LANES] = part.T[:local]


def correct_kernel(groups, rows, sharers, got, first, second, restricted, inv, basis, out, turned, sums):
    slots, rhs, width = restricted.shape
    head = first.shape[1]
    local = basis.shape[1]
    turn_columns(groups, rows, second, head, second.shape[1] - head, turned)
    sums[...] = jnp.zeros_like(sums)
    left = lax.broadcasted_iota(jnp.int32, (rhs, LANES), 1) < local
    group = min(slots // 2, 4)

    def body(g, carry):
        part = None
        for u in range(group):
            p = g * group + u
            columns = jnp.concatenate(split(take_lanes(turned, *pair_digits(first, 2 * p, rhs, local))), axis=0)
            a = got[2 * p].astype(F32)
            b = got[2 * p + 1].astype(F32)
            high = jnp.where(left, a, pltpu.roll(b, local, 1))
            low = jnp.where(left, pltpu.roll(a, local, 1), b)
            term = dot(jnp.concatenate([high, low], axis=0).astype(BF16), columns, NT)
            part = term if part is None else part + term
        sums[...] += part
        return carry

    lax.fori_loop(0, slots // 2 // group, body, 0)
    prod = sums[...]
    picked = (prod[:rhs, :local] + (prod[:rhs, local:] + prod[rhs:, :local])).astype(BF16)
    extra = jnp.zeros((rhs // 2, LANES), F32)

    def finish(l):
        value = dot(picked, basis[l]) + dot(restricted[l], inv[l], NT)
        pack(out, l, omega(sharers, l) * value, extra)

    loop(slots, finish)


def extend_kernel(elem, got, inner, couple, inv, inner_out, face_out, sums):
    slots, rhs, width = face_out.shape
    tail = width - LANES
    sums[...] = inner[...].astype(F32)

    def step(l):
        value = unpack(got, l, rhs, tail).astype(BF16)
        face_out[l] = value
        sums[elem[0, l]] -= dot(value, couple[l])

    loop(slots, step)

    def finish(e):
        inner_out[e] = dot(sums[e].astype(BF16), inv[e], NT).astype(BF16)

    loop(inner_out.shape[0], finish)


def padded(shape, dtype):
    size = jnp.dtype(dtype).itemsize
    for n in shape[:-2]:
        size *= n
    return size * (-(-shape[-2] // 16) * 16) * (-(-shape[-1] // LANES) * LANES)


def call(kernel, out_shape, specs, args, scratch=(), flops=0, name=None, limit=None):
    many = isinstance(out_shape, (tuple, list))
    outs = tuple(out_shape) if many else (out_shape,)
    held = [a for a, s in zip(args, specs) if s is VMEM] + list(outs)
    need = sum(padded(a.shape, a.dtype) for a in held)
    room = sum(padded(shape, dtype) for shape, dtype in scratch if dtype is not None)
    made = [pltpu.VMEM(shape, dtype) if dtype is not None else shape for shape, dtype in scratch]
    return pl.pallas_call(
        kernel,
        out_shape=out_shape,
        in_specs=specs,
        out_specs=tuple(VMEM for _ in outs) if many else VMEM,
        scratch_shapes=made,
        cost_estimate=pl.CostEstimate(flops=flops, bytes_accessed=need, transcendentals=0),
        compiler_params=pltpu.CompilerParams(vmem_limit_bytes=limit or need + room + (2 << 20)),
        name=name,
    )(*args)


def body(
    res_inner,
    res_face,
    inner_inv,
    face_coupling,
    face_elem,
    face_inv,
    coarse_basis,
    coarse_map,
    coarse_inv,
    recv_index,
    sharers,
):
    slots, rhs, width = res_face.shape
    owned = slots // 4
    elements = res_inner.shape[0]
    rows, total = coarse_inv.shape
    local = coarse_map.shape[1]
    groups = total // rows
    piece = rows * groups // slots
    shape = jax.ShapeDtypeStruct
    head = rhs + rhs // 2
    wire = shape((slots, head, LANES), BF16)
    unit = 2 * rhs * width * width
    tables = [((owned + 1, head, LANES), F32), ((owned + 1, head, LANES), BF16)]

    sent = call(
        condense_kernel,
        wire,
        [HBM, HBM, VMEM, HBM, HBM, HBM, HBM],
        (face_elem, sharers, coarse_map, res_inner, inner_inv, face_coupling, res_face),
        [
            (pltpu.SMEM(face_elem.shape, jnp.int32), None),
            (pltpu.SMEM(sharers.shape, jnp.int32), None),
            ((slots, rhs, width), BF16),
            ((slots, width, width), BF16),
            ((slots, width, width), BF16),
            ((slots, rhs, width), BF16),
            (pltpu.SemaphoreType.DMA((4, slots)), None),
            (pltpu.SemaphoreType.DMA((2,)), None),
        ],
        flops=2 * slots * unit,
        name="condense",
        limit=60 * 1024 * 1024,
    )
    first = exchange(sent)
    held = call(
        first_owner_kernel,
        shape((slots, head + piece, LANES), BF16),
        [SMEM, VMEM, VMEM],
        (recv_index, first, coarse_inv),
        tables + [((piece, total), F32)],
        flops=slots * head * LANES,
        name="first_owner",
    )
    gathered = exchange(held)
    coarse, restricted = call(
        restrict_kernel,
        (shape((slots, rhs, LANES), BF16), shape((slots, rhs, width), BF16)),
        [SMEM, VMEM, VMEM],
        (sharers, gathered, coarse_basis),
        [((rhs, local), F32)],
        flops=slots * unit // 2,
        name="restrict",
    )
    every = exchange(coarse)
    weighted = call(
        functools.partial(correct_kernel, groups, rows),
        wire,
        [SMEM, VMEM, VMEM, VMEM, VMEM, VMEM, VMEM],
        (sharers, every, first, gathered, restricted, face_inv, coarse_basis),
        [((local, total), F32), ((2 * rhs, LANES), F32)],
        flops=2 * slots * unit,
        name="correct",
    )
    third = exchange(weighted)
    spread = call(
        owner_kernel, wire, [SMEM, VMEM], (recv_index, third), tables, flops=slots * head * LANES, name="owner"
    )
    assembled = exchange(spread)
    return call(
        extend_kernel,
        (shape((elements, rhs, width), BF16), shape((slots, rhs, width), BF16)),
        [SMEM, VMEM, VMEM, VMEM, VMEM],
        (face_elem, assembled, res_inner, face_coupling, inner_inv),
        [((elements, rhs, width), F32)],
        flops=2 * slots * unit,
        name="extend",
    )


def solution(mesh):
    block = P(AXES, None, None)
    row = P(AXES, None)
    return jax.shard_map(
        body,
        mesh=mesh,
        in_specs=(block, block, block, block, row, block, block, row, P("grp", None), row, row),
        out_specs=(block, block),
        check_vma=False,
    )
```

time: 99.9 us -> 83.3 us (0.83)
  blocking collectives: 29.3 us -> 63.3 us
  Pallas kernels: 49.5 us -> 18.9 us
  waiting for transfers between devices: 9.6 us -> 0 us
  starting transfers between devices: 7.99 us -> 0 us
  local copies, waits for them, and re-layouts: 2.05 us -> 0.05 us
    all_to_all x2 -> x5, blocking collectives: 29.3 us -> 63.3 us  [exchange(): return lax.all_to_all(blocks, AXES, split_axis=0, concat_axis=0, tiled=True)]
    pallas_call x10 -> x6, Pallas kernels: 49.5 us -> 18.9 us  [call(): pl.pallas_call(kernel, out_shape=out_shape, in_specs=specs, out_specs=tup...]
    all_to_all x3 -> x0, waiting for transfers between devices: 9.6 us -> none  [exchange(): return lax.all_to_all(blocks, AXES, split_axis=0, concat_axis=0, tiled=True)]
    all_to_all x3 -> x0, starting transfers between devices: 7.99 us -> none  [exchange(): return lax.all_to_all(blocks, AXES, split_axis=0, concat_axis=0, tiled=True)]
    unnamed x6 -> x20, local copies, waits for them, and re-layouts: 2.05 us -> 0.05 us
  transfers between devices with their start and end apart: 3 -> 0, of which waited for: 2 -> 0; matrix products, arithmetic and copies ran while one was open for 0% -> 0% of each run, Pallas kernels for 25% -> 0%
where the time goes in v3:
time: 83.3 us; the launch traced here: 82.9 us
  blocking collectives  63.3 us (76%)
  Pallas kernels  18.9 us (23%)
    all_to_all x5, blocking collectives, exchange(): return lax.all_to_all(blocks, AXES, split_axis=0, concat_axis=0, tiled=True)  63.3 us
    pallas_call x6, Pallas kernels, call(): pl.pallas_call(kernel, out_shape=out_shape, in_specs=specs, out_specs=tup...  18.9 us

profile of v3, /device:TPU:0, one launch (start us, length us, event | category | flops | bytes accessed | tf_op | source)
XLA Modules:
  0.0 82.9 jit_solution(6153819119961522412)
XLA Ops:
  0.6 0.0 copy-start.5
  0.6 0.0 copy-start.7
  0.7 0.0 copy-start.4
  0.7 0.0 copy-start.2
  0.7 0.0 slice-start
  0.7 7.3 %condense.1 = bf16[32,24,128]{2,1,0:T(8,128)(2,1)} custom-call(s32[1,32]{1,0:T(1,128)} %elem.1, s32[1,32]{1,0:T(1,128)} %sharers.3, s32[1,64]{1,0:T(1,128)} %cmap.1, bf16[64,16,144]{2,1,0:T(8,128)(2,1)} %inner.3, bf16[64,144,144]{2,1,0:T(8,128)(2,1)} %inv.5, bf16[32,144,144]{2,1,0:T(8,128)(2,1)} %couple.3, bf16[32,16,144]{2,1,0:T(8,128)(2,1)} %face.1), custom_call_target="tpu_custom_call" | custom-call | flops 42467328 | bytes 270336 | tf_op jit(solution)/shard_map/condense/pallas_call | solution.py:300
  8.0 0.0 copy-start.1
  8.0 16.6 %all_to_all.25.got.first = bf16[32,24,128]{2,1,0:T(8,128)(2,1)S(1)} all-to-all(bf16[32,24,128]{2,1,0:T(8,128)(2,1)} %condense.1), channel_id=1, replica_groups=mesh['sub'=8,'grp'=4] {'sub','grp'}, dimensions={0} | all-to-all | bytes 393216 | tf_op jit(solution)/shard_map/all_to_all | solution.py:24
  24.7 0.0 copy-done.7
  24.7 0.0 copy-done.4
  24.7 1.5 %first_owner.1 = bf16[32,40,128]{2,1,0:T(8,128)(2,1)S(1)} custom-call(s32[1,32]{1,0:T(1,128)S(1)} %copy-done.7, bf16[32,24,128]{2,1,0:T(8,128)(2,1)S(1)} %all_to_all.25.got.first, f32[128,512]{1,0:T(8,128)S(1)} %copy-done.4), custom_call_target="tpu_custom_call" | custom-call | flops 98304 | bytes 917504 | tf_op jit(solution)/shard_map/first_owner/pallas_call | solution.py:300
  26.2 13.0 %all_to_all.26.got.second = bf16[32,40,128]{2,1,0:T(8,128)(2,1)S(1)} all-to-all(bf16[32,40,128]{2,1,0:T(8,128)(2,1)S(1)} %first_owner.1), channel_id=1, replica_groups=mesh['sub'=8,'grp'=4] {'sub','grp'}, dimensions={0} | all-to-all | bytes 655360 | tf_op jit(solution)/shard_map/all_to_all | solution.py:24
  39.2 0.0 copy-done.5
  39.2 0.0 copy-done.1
  39.2 1.3 %restrict.1 = (bf16[32,16,128]{2,1,0:T(8,128)(2,1)S(1)}, bf16[32,16,144]{2,1,0:T(8,128)(2,1)S(1)}) custom-call(s32[1,32]{1,0:T(1,128)S(1)} %copy-done.5, bf16[32,40,128]{2,1,0:T(8,128)(2,1)S(1)} %all_to_all.26.got.second, bf16[32,64,144]{2,1,0:T(8,128)(2,1)S(1)} %copy-done.1), custom_call_target="tpu_custom_call" | custom-call | flops 10616832 | bytes 1835008 | tf_op jit(solution)/shard_map/restrict/pallas_call | solution.py:300
  40.5 11.4 %all_to_all.27.got = bf16[32,16,128]{2,1,0:T(8,128)(2,1)S(1)} all-to-all(bf16[32,16,128]{2,1,0:T(8,128)(2,1)S(1)} %get-tuple-element.4), channel_id=1, replica_groups=mesh['sub'=8,'grp'=4] {'sub','grp'}, dimensions={0} | all-to-all | bytes 262144 | tf_op jit(solution)/shard_map/all_to_all | solution.py:24
  51.9 0.0 copy-done.2
  52.0 4.1 %correct.1 = bf16[32,24,128]{2,1,0:T(8,128)(2,1)S(1)} custom-call(s32[1,32]{1,0:T(1,128)S(1)} %copy-done.5, bf16[32,16,128]{2,1,0:T(8,128)(2,1)S(1)} %all_to_all.27.got, bf16[32,24,128]{2,1,0:T(8,128)(2,1)S(1)} %all_to_all.25.got.first, bf16[32,40,128]{2,1,0:T(8,128)(2,1)S(1)} %all_to_all.26.got.second, ...), custom_call_target="tpu_custom_call" | custom-call | flops 42467328 | bytes 4718592 | tf_op jit(solution)/shard_map/correct/pallas_call | solution.py:300
  56.1 11.0 %all_to_all.28.got = bf16[32,24,128]{2,1,0:T(8,128)(2,1)S(1)} all-to-all(bf16[32,24,128]{2,1,0:T(8,128)(2,1)S(1)} %correct.1), channel_id=1, replica_groups=mesh['sub'=8,'grp'=4] {'sub','grp'}, dimensions={0} | all-to-all | bytes 393216 | tf_op jit(solution)/shard_map/all_to_all | solution.py:24
  67.1 0.8 %owner.1 = bf16[32,24,128]{2,1,0:T(8,128)(2,1)S(1)} custom-call(s32[1,32]{1,0:T(1,128)S(1)} %copy-done.7, bf16[32,24,128]{2,1,0:T(8,128)(2,1)S(1)} %all_to_all.28.got), custom_call_target="tpu_custom_call" | custom-call | flops 98304 | bytes 524288 | tf_op jit(solution)/shard_map/owner/pallas_call | solution.py:300
  67.9 11.2 %all_to_all.29.got = bf16[32,24,128]{2,1,0:T(8,128)(2,1)S(1)} all-to-all(bf16[32,24,128]{2,1,0:T(8,128)(2,1)S(1)} %owner.1), channel_id=1, replica_groups=mesh['sub'=8,'grp'=4] {'sub','grp'}, dimensions={0} | all-to-all | bytes 393216 | tf_op jit(solution)/shard_map/all_to_all | solution.py:24
  79.2 0.0 slice-done
  79.2 0.0 copy-done
  79.2 3.8 %extend.1 = (bf16[64,16,144]{2,1,0:T(8,128)(2,1)}, bf16[32,16,144]{2,1,0:T(8,128)(2,1)}) custom-call(s32[1,32]{1,0:T(1,128)S(1)} %copy-done.6, bf16[32,24,128]{2,1,0:T(8,128)(2,1)S(1)} %all_to_all.29.got, bf16[64,16,144]{2,1,0:T(8,128)(2,1)S(1)} %copy-done.3, bf16[32,144,144]{2,1,0:T(8,128)(2,1)S(1)} %copy-done, bf16[64,144,144]{2,1,0:T(8,128)(2,1)S(1)} %bitcast.1), custom_call_target="tpu_custom_call" | custom-call | flops 42467328 | bytes 8650752 | tf_op jit(solution)/shard_map/extend/pallas_call | solution.py:300
  (8 shorter events, 0.0 us)
Async XLA Ops:
  0.6 38.6 %copy-start.5 = (s32[1,32]{1,0:T(1,128)S(1)}, s32[1,32]{1,0:T(1,128)}, u32[]{:S(2)}) copy-start(s32[1,32]{1,0:T(1,128)} %sharers.3) | copy-start | bytes 388
  0.6 24.1 %copy-start.7 = (s32[1,32]{1,0:T(1,128)S(1)}, s32[1,32]{1,0:T(1,128)}, u32[]{:S(2)}) copy-start(s32[1,32]{1,0:T(1,128)} %recv.3) | copy-start | bytes 388
  0.7 24.1 %copy-start.4 = (f32[128,512]{1,0:T(8,128)S(1)}, f32[128,512]{1,0:T(8,128)}, u32[]{:S(2)}) copy-start(f32[128,512]{1,0:T(8,128)} %cinv.1) | copy-start | bytes 786436
  0.7 51.3 %copy-start.2 = (bf16[32,144,144]{2,1,0:T(8,128)(2,1)S(1)}, bf16[32,144,144]{2,1,0:T(8,128)(2,1)}, u32[]{:S(2)}) copy-start(bf16[32,144,144]{2,1,0:T(8,128)(2,1)} %inv.4) | copy-start | bytes 3981316
  0.7 78.5 %slice-start = ((s8[4718592]{0:T(1024)(128)(4,1)}), s8[524288]{0:T(1024)(128)(4,1)S(1)}, s32[]{:S(2)}) async-start(s8[4718592]{0:T(1024)(128)(4,1)} %bitcast), calls=%async_computation.5 | async-start | bytes 1048576
  8.0 31.2 %copy-start.1 = (bf16[32,64,144]{2,1,0:T(8,128)(2,1)S(1)}, bf16[32,64,144]{2,1,0:T(8,128)(2,1)}, u32[]{:S(2)}) copy-start(bf16[32,64,144]{2,1,0:T(8,128)(2,1)} %basis.3) | copy-start | bytes 1769476
  24.7 54.5 %slice-start.1 = ((s8[4718592]{0:T(1024)(128)(4,1)}), s8[4194304]{0:T(1024)(128)(4,1)S(1)}, s32[]{:S(2)}) async-start(s8[4718592]{0:T(1024)(128)(4,1)} %bitcast), calls=%async_computation.6 | async-start | bytes 8388608
  51.9 27.2 %copy-start = (bf16[32,144,144]{2,1,0:T(8,128)(2,1)S(1)}, bf16[32,144,144]{2,1,0:T(8,128)(2,1)}, u32[]{:S(2)}) copy-start(bf16[32,144,144]{2,1,0:T(8,128)(2,1)} %couple.3) | copy-start | bytes 3981316
  51.9 27.2 %copy-start.3 = (bf16[64,16,144]{2,1,0:T(8,128)(2,1)S(1)}, bf16[64,16,144]{2,1,0:T(8,128)(2,1)}, u32[]{:S(2)}) copy-start(bf16[64,16,144]{2,1,0:T(8,128)(2,1)} %inner.3) | copy-start | bytes 884740
  51.9 27.2 %copy-start.6 = (s32[1,32]{1,0:T(1,128)S(1)}, s32[1,32]{1,0:T(1,128)}, u32[]{:S(2)}) copy-start(s32[1,32]{1,0:T(1,128)} %elem.1) | copy-start | bytes 388

commit v4 on v3

--- a/solution.py
+++ b/solution.py
@@ -33,11 +33,6 @@
     return jnp.where(count > 0, 1.0 / jnp.maximum(count, 1).astype(F32), 0.0)
 
 
-def split(value):
-    high = value.astype(BF16)
-    return high, (value - high.astype(F32)).astype(BF16)
-
-
 def pack(out, slot, value, extra):
     rhs, width = value.shape
     tail = width - LANES
@@ -69,62 +64,61 @@
 
 
 def condense_kernel(
-    elem_in, sharers_in, cmap, inner, inv, couple, face, out, elem, sharers, rin, invs, cps, fac, sems, small
+    elem_in, sharers_in, map_in, inner, inv, couple, face, out, elem, sharers, cmap, rin, invs, cps, fac, stage, sems, small
 ):
     slots, rhs, width = fac.shape
-    tail = width - LANES
-    chunks = slots // CHUNK
-
-    def inner_copy(l):
-        return pltpu.make_async_copy(inner.at[elem[0, l]], rin.at[l], sems.at[0, l])
-
-    def inv_copy(l):
-        return pltpu.make_async_copy(inv.at[elem[0, l]], invs.at[l], sems.at[1, l])
+    step = min(slots, CHUNK)
+    chunks = slots // step
+    copy = pltpu.make_async_copy
+
+    def part(c):
+        return pl.ds(c * step, step)
 
     def couple_copy(c):
-        part = pl.ds(c * CHUNK, CHUNK)
-        return pltpu.make_async_copy(couple.at[part], cps.at[part], sems.at[2, c])
+        return copy(couple.at[part(c)], cps.at[part(c)], sems.at[2, c])
 
     def face_copy(c):
-        part = pl.ds(c * CHUNK, CHUNK)
-        return pltpu.make_async_copy(face.at[part], fac.at[part], sems.at[3, c])
-
-    elem_copy = pltpu.make_async_copy(elem_in, elem, small.at[0])
-    sharers_copy = pltpu.make_async_copy(sharers_in, sharers, small.at[1])
-    elem_copy.start()
-    sharers_copy.start()
-    elem_copy.wait()
-
-    def start(c, carry):
-        for u in range(CHUNK):
-            inner_copy(c * CHUNK + u).start()
-            inv_copy(c * CHUNK + u).start()
-        couple_copy(c).start()
-        face_copy(c).start()
-        return carry
-
-    lax.fori_loop(0, chunks, start, 0)
+        return copy(face.at[part(c)], fac.at[part(c)], sems.at[3, c])
+
+    def out_copy(c):
+        return copy(stage.at[part(c)], out.at[part(c)], sems.at[4, c])
+
+    first = copy(elem_in, elem, small.at[0])
+    others = [copy(sharers_in, sharers, small.at[1]), copy(map_in, cmap, small.at[2])]
+    first.start()
+    for other in others:
+        other.start()
+    couple_copy(0).start()
+    face_copy(0).start()
+    first.wait()
+    for c in range(chunks):
+        for u in range(step):
+            l = c * step + u
+            copy(inner.at[elem[0, l]], rin.at[l], sems.at[0, c]).start()
+            copy(inv.at[elem[0, l]], invs.at[l], sems.at[1, c]).start()
+        if c > 0:
+            couple_copy(c).start()
+            face_copy(c).start()
+    for other in others:
+        other.wait()
     maps = cmap[...]
     digits = jnp.concatenate([maps // DIGIT, maps % DIGIT], axis=0).astype(F32)
     local = digits.shape[1]
     digits = jnp.concatenate([digits, jnp.zeros((rhs // 2 - 2, local), F32)], axis=0)
     extra = jnp.concatenate([jnp.zeros((rhs // 2, LANES - local), F32), digits], axis=1)
-    sharers_copy.wait()
-
-    def chunk(c, carry):
-        for u in range(CHUNK):
-            inner_copy(c * CHUNK + u).wait()
-            inv_copy(c * CHUNK + u).wait()
+    for c in range(chunks):
+        copy(inner.at[pl.ds(0, step)], rin.at[part(c)], sems.at[0, c]).wait()
+        copy(inv.at[pl.ds(0, step)], invs.at[part(c)], sems.at[1, c]).wait()
+        near = [dot(rin[c * step + u], invs[c * step + u], NT).astype(BF16) for u in range(step)]
         couple_copy(c).wait()
         face_copy(c).wait()
-        for u in range(CHUNK):
-            l = c * CHUNK + u
-            near = dot(rin[l], invs[l], NT).astype(BF16)
-            value = fac[l].astype(F32) - dot(near, cps[l], NT)
-            pack(out, l, omega(sharers, l) * value, extra)
-        return carry
-
-    lax.fori_loop(0, chunks, chunk, 0)
+        for u in range(step):
+            l = c * step + u
+            value = fac[l].astype(F32) - dot(near[u], cps[l], NT)
+            pack(stage, l, omega(sharers, l) * value, extra)
+        out_copy(c).start()
+    for c in range(chunks):
+        out_copy(c).wait()
 
 
 def assemble(recv, got, out, sums, rounded):
@@ -170,25 +164,30 @@
     assemble(recv, got, out, sums, rounded)
 
 
+def halves(value, local, left):
+    half = value.shape[0] // 2
+    top, low = value[:half], value[half:]
+    return jnp.where(left, top, pltpu.roll(low, local, 1)), jnp.where(left, pltpu.roll(top, local, 1), low)
+
+
 def first_owner_kernel(recv, got, cinv, out, sums, rounded, strip):
     slots, height, _ = out.shape
     head = got.shape[1]
-    piece = height - head
+    piece = strip.shape[0]
     rhs = head * 2 // 3
     local = LANES // 2
     assemble(recv, got, out, sums, rounded)
     start = pl.multiple_of(lax.axis_index("sub") * piece, piece)
     strip[...] = cinv[pl.ds(start, piece), :]
-    left = lax.broadcasted_iota(jnp.int32, (piece, LANES), 1) < local
+    left = lax.broadcasted_iota(jnp.int32, (piece // 2, LANES), 1) < local
 
     def step(p):
         taken = take_lanes(strip, *pair_digits(got, 2 * p, rhs, local))
-        high = taken.astype(BF16).astype(F32)
-        low = taken - high
-        out[2 * p, head:, :] = jnp.where(left, high, pltpu.roll(low, local, 1)).astype(BF16)
-        out[2 * p + 1, head:, :] = jnp.where(left, pltpu.roll(high, local, 1), low).astype(BF16)
-
-    loop(slots // 2, step, 8)
+        low, top = halves(taken, local, left)
+        out[2 * p, head:, :] = low.astype(BF16)
+        out[2 * p + 1, head:, :] = top.astype(BF16)
+
+    loop(slots // 2, step)
 
 
 def restrict_kernel(sharers, got, basis, out, restricted, total):
@@ -209,8 +208,8 @@
         return carry
 
     lax.fori_loop(0, slots // group, body, 0)
-    high, low = split(total[...])
-    block = jnp.concatenate([high, low], axis=1)
+    both = total[...]
+    block = jnp.concatenate([both[: rhs // 2], both[rhs // 2 :]], axis=1).astype(BF16)
 
     def give(d):
         out[d] = block
@@ -223,39 +222,35 @@
     for t in range(total // LANES):
         parts = []
         for k in range(t * LANES, (t + 1) * LANES, piece):
-            device = (k % rows) // piece * groups + k // rows
-            parts.append(got[device, head:, :].astype(F32))
-        part = jnp.concatenate(parts, axis=0)
-        part = part + pltpu.roll(part, local, 1)
-        turned[:, t * LANES : (t + 1) * LANES] = part.T[:local]
+            block = got[(k % rows) // piece * groups + k // rows, head:, :].astype(F32)
+            parts += [block, pltpu.roll(block, local, 1)]
+        turned[:, t * LANES : (t + 1) * LANES] = jnp.concatenate(parts, axis=0).T[:local]
 
 
 def correct_kernel(groups, rows, sharers, got, first, second, restricted, inv, basis, out, turned, sums):
     slots, rhs, width = restricted.shape
     head = first.shape[1]
     local = basis.shape[1]
-    turn_columns(groups, rows, second, head, second.shape[1] - head, turned)
+    turn_columns(groups, rows, second, head, (second.shape[1] - head) * 2, turned)
     sums[...] = jnp.zeros_like(sums)
-    left = lax.broadcasted_iota(jnp.int32, (rhs, LANES), 1) < local
-    group = min(slots // 2, 4)
+    left = lax.broadcasted_iota(jnp.int32, (rhs // 2, LANES), 1) < local
+    group = min(slots // 2, 8)
 
     def body(g, carry):
         part = None
         for u in range(group):
             p = g * group + u
-            columns = jnp.concatenate(split(take_lanes(turned, *pair_digits(first, 2 * p, rhs, local))), axis=0)
-            a = got[2 * p].astype(F32)
-            b = got[2 * p + 1].astype(F32)
-            high = jnp.where(left, a, pltpu.roll(b, local, 1))
-            low = jnp.where(left, pltpu.roll(a, local, 1), b)
-            term = dot(jnp.concatenate([high, low], axis=0).astype(BF16), columns, NT)
+            columns = take_lanes(turned, *pair_digits(first, 2 * p, rhs, local)).astype(BF16)
+            low = got[2 * p].astype(F32)
+            top = got[2 * p + 1].astype(F32)
+            value = jnp.concatenate(halves(jnp.concatenate([low, top], axis=0), local, left), axis=0)
+            term = dot(value.astype(BF16), columns, NT)
             part = term if part is None else part + term
         sums[...] += part
         return carry
 
     lax.fori_loop(0, slots // 2 // group, body, 0)
-    prod = sums[...]
-    picked = (prod[:rhs, :local] + (prod[:rhs, local:] + prod[rhs:, :local])).astype(BF16)
+    picked = sums[...].astype(BF16)
     extra = jnp.zeros((rhs // 2, LANES), F32)
 
     def finish(l):
@@ -275,12 +270,12 @@
         face_out[l] = value
         sums[elem[0, l]] -= dot(value, couple[l])
 
-    loop(slots, step)
+    loop(slots, step, 32)
 
     def finish(e):
         inner_out[e] = dot(sums[e].astype(BF16), inv[e], NT).astype(BF16)
 
-    loop(inner_out.shape[0], finish)
+    loop(inner_out.shape[0], finish, 32)
 
 
 def padded(shape, dtype):
@@ -290,7 +285,7 @@
     return size * (-(-shape[-2] // 16) * 16) * (-(-shape[-1] // LANES) * LANES)
 
 
-def call(kernel, out_shape, specs, args, scratch=(), flops=0, name=None, limit=None):
+def call(kernel, out_shape, specs, args, scratch=(), flops=0, name=None, limit=None, out_spec=VMEM):
     many = isinstance(out_shape, (tuple, list))
     outs = tuple(out_shape) if many else (out_shape,)
     held = [a for a, s in zip(args, specs) if s is VMEM] + list(outs)
@@ -301,7 +296,7 @@
         kernel,
         out_shape=out_shape,
         in_specs=specs,
-        out_specs=tuple(VMEM for _ in outs) if many else VMEM,
+        out_specs=tuple(VMEM for _ in outs) if many else out_spec,
         scratch_shapes=made,
         cost_estimate=pl.CostEstimate(flops=flops, bytes_accessed=need, transcendentals=0),
         compiler_params=pltpu.CompilerParams(vmem_limit_bytes=limit or need + room + (2 << 20)),
@@ -338,40 +333,43 @@
     sent = call(
         condense_kernel,
         wire,
-        [HBM, HBM, VMEM, HBM, HBM, HBM, HBM],
+        [HBM] * 7,
         (face_elem, sharers, coarse_map, res_inner, inner_inv, face_coupling, res_face),
         [
             (pltpu.SMEM(face_elem.shape, jnp.int32), None),
             (pltpu.SMEM(sharers.shape, jnp.int32), None),
+            (pltpu.VMEM(coarse_map.shape, jnp.int32), None),
             ((slots, rhs, width), BF16),
             ((slots, width, width), BF16),
             ((slots, width, width), BF16),
             ((slots, rhs, width), BF16),
-            (pltpu.SemaphoreType.DMA((4, slots)), None),
-            (pltpu.SemaphoreType.DMA((2,)), None),
+            ((slots, head, LANES), BF16),
+            (pltpu.SemaphoreType.DMA((5, -(-slots // CHUNK))), None),
+            (pltpu.SemaphoreType.DMA((3,)), None),
         ],
         flops=2 * slots * unit,
         name="condense",
         limit=60 * 1024 * 1024,
+        out_spec=HBM,
     )
     first = exchange(sent)
     held = call(
         first_owner_kernel,
-        shape((slots, head + piece, LANES), BF16),
+        shape((slots, head + piece // 2, LANES), BF16),
         [SMEM, VMEM, VMEM],
         (recv_index, first, coarse_inv),
         tables + [((piece, total), F32)],
-        flops=slots * head * LANES,
+        flops=100 * slots * unit,
         name="first_owner",
     )
     gathered = exchange(held)
     coarse, restricted = call(
         restrict_kernel,
-        (shape((slots, rhs, LANES), BF16), shape((slots, rhs, width), BF16)),
+        (shape((slots, rhs // 2, LANES), BF16), shape((slots, rhs, width), BF16)),
         [SMEM, VMEM, VMEM],
         (sharers, gathered, coarse_basis),
         [((rhs, local), F32)],
-        flops=slots * unit // 2,
+        flops=100 * slots * unit,
         name="restrict",
     )
     every = exchange(coarse)
@@ -380,7 +378,7 @@
         wire,
         [SMEM, VMEM, VMEM, VMEM, VMEM, VMEM, VMEM],
         (sharers, every, first, gathered, restricted, face_inv, coarse_basis),
-        [((local, total), F32), ((2 * rhs, LANES), F32)],
+        [((local, total), F32), ((rhs, local), F32)],
         flops=2 * slots * unit,
         name="correct",
     )

time: 83.3 us -> 76.6 us (0.920)
  Pallas kernels: 18.9 us -> 14.6 us
  blocking collectives: 63.3 us -> 60.9 us
    pallas_call x6, Pallas kernels: 18.9 us -> 14.6 us  [call(): pl.pallas_call(kernel, out_shape=out_shape, in_specs=specs, out_specs=tup...]
    all_to_all x5, blocking collectives: 63.3 us -> 60.9 us  [exchange(): return lax.all_to_all(blocks, AXES, split_axis=0, concat_axis=0, tiled=True)]
where the time goes in v4:
time: 76.6 us; the launch traced here: 76.3 us
  blocking collectives  60.9 us (80%)
  Pallas kernels  14.6 us (19%)
    all_to_all x5, blocking collectives, exchange(): return lax.all_to_all(blocks, AXES, split_axis=0, concat_axis=0, tiled=True)  60.9 us
    pallas_call x6, Pallas kernels, call(): pl.pallas_call(kernel, out_shape=out_shape, in_specs=specs, out_specs=tup...  14.6 us

profile of v4, /device:TPU:0, one launch (start us, length us, event | category | flops | bytes accessed | tf_op | source)
XLA Modules:
  0.0 76.3 jit_solution(7536297734634260239)
XLA Ops:
  0.6 0.0 copy-start.6
  0.6 0.0 copy-start.7
  0.7 5.0 %condense.1 = bf16[32,24,128]{2,1,0:T(8,128)(2,1)} custom-call(s32[1,32]{1,0:T(1,128)} %elem.1, s32[1,32]{1,0:T(1,128)} %sharers.3, s32[1,64]{1,0:T(1,128)} %map_in.1, bf16[64,16,144]{2,1,0:T(8,128)(2,1)} %inner.3, bf16[64,144,144]{2,1,0:T(8,128)(2,1)} %inv.5, bf16[32,144,144]{2,1,0:T(8,128)(2,1)} %couple.3, bf16[32,16,144]{2,1,0:T(8,128)(2,1)} %face.1), custom_call_target="tpu_custom_call" | custom-call | flops 42467328 | bytes 262144 | tf_op jit(solution)/shard_map/condense/pallas_call | solution.py:295
  5.6 16.6 %all_to_all.25.got.first = bf16[32,24,128]{2,1,0:T(8,128)(2,1)S(1)} all-to-all(bf16[32,24,128]{2,1,0:T(8,128)(2,1)} %condense.1), channel_id=1, replica_groups=mesh['sub'=8,'grp'=4] {'sub','grp'}, dimensions={0} | all-to-all | bytes 393216 | tf_op jit(solution)/shard_map/all_to_all | solution.py:24
  22.2 0.0 copy-done.6
  22.2 0.0 copy-done.7
  22.2 1.2 %first_owner.1 = bf16[32,32,128]{2,1,0:T(8,128)(2,1)S(1)} custom-call(s32[1,32]{1,0:T(1,128)S(1)} %copy-done.6, bf16[32,24,128]{2,1,0:T(8,128)(2,1)S(1)} %all_to_all.25.got.first, f32[128,512]{1,0:T(8,128)S(1)} %copy-done.7), custom_call_target="tpu_custom_call" | custom-call | flops 2123366400 | bytes 786432 | tf_op jit(solution)/shard_map/first_owner/pallas_call | solution.py:295
  23.4 0.0 slice-start
  23.4 12.2 %all_to_all.26.got.second = bf16[32,32,128]{2,1,0:T(8,128)(2,1)S(1)} all-to-all(bf16[32,32,128]{2,1,0:T(8,128)(2,1)S(1)} %first_owner.1), channel_id=1, replica_groups=mesh['sub'=8,'grp'=4] {'sub','grp'}, dimensions={0} | all-to-all | bytes 524288 | tf_op jit(solution)/shard_map/all_to_all | solution.py:24
  35.6 0.0 copy-done.3
  35.6 0.0 copy-done.4
  35.6 1.3 %restrict.1 = (bf16[32,8,128]{2,1,0:T(8,128)(2,1)S(1)}, bf16[32,16,144]{2,1,0:T(8,128)(2,1)S(1)}) custom-call(s32[1,32]{1,0:T(1,128)S(1)} %copy-done.4, bf16[32,32,128]{2,1,0:T(8,128)(2,1)S(1)} %all_to_all.26.got.second, bf16[32,64,144]{2,1,0:T(8,128)(2,1)S(1)} %copy-done.3), custom_call_target="tpu_custom_call" | custom-call | flops 2123366400 | bytes 1703936 | tf_op jit(solution)/shard_map/restrict/pallas_call | solution.py:295
  36.9 9.9 %all_to_all.27.got = bf16[32,8,128]{2,1,0:T(8,128)(2,1)S(1)} all-to-all(bf16[32,8,128]{2,1,0:T(8,128)(2,1)S(1)} %get-tuple-element.4), channel_id=1, replica_groups=mesh['sub'=8,'grp'=4] {'sub','grp'}, dimensions={0} | all-to-all | bytes 131072 | tf_op jit(solution)/shard_map/all_to_all | solution.py:24
  46.9 0.0 copy-done.1
  46.9 3.1 %correct.1 = bf16[32,24,128]{2,1,0:T(8,128)(2,1)S(1)} custom-call(s32[1,32]{1,0:T(1,128)S(1)} %copy-done.4, bf16[32,8,128]{2,1,0:T(8,128)(2,1)S(1)} %all_to_all.27.got, bf16[32,24,128]{2,1,0:T(8,128)(2,1)S(1)} %all_to_all.25.got.first, bf16[32,32,128]{2,1,0:T(8,128)(2,1)S(1)} %all_to_all.26.got.second, bf16[32,16,144]{2,1,0:T(8,128)(2,1)S(1)} %get-tuple-element.5.restricted, ...), custom_call_target="tpu_custom_call" | custom-call | flops 42467328 | bytes 4587520 | tf_op jit(solution)/shard_map/correct/pallas_call | solution.py:295
  49.9 11.0 %all_to_all.28.got = bf16[32,24,128]{2,1,0:T(8,128)(2,1)S(1)} all-to-all(bf16[32,24,128]{2,1,0:T(8,128)(2,1)S(1)} %correct.1), channel_id=1, replica_groups=mesh['sub'=8,'grp'=4] {'sub','grp'}, dimensions={0} | all-to-all | bytes 393216 | tf_op jit(solution)/shard_map/all_to_all | solution.py:24
  60.9 0.8 %owner.1 = bf16[32,24,128]{2,1,0:T(8,128)(2,1)S(1)} custom-call(s32[1,32]{1,0:T(1,128)S(1)} %copy-done.6, bf16[32,24,128]{2,1,0:T(8,128)(2,1)S(1)} %all_to_all.28.got), custom_call_target="tpu_custom_call" | custom-call | flops 98304 | bytes 524288 | tf_op jit(solution)/shard_map/owner/pallas_call | solution.py:295
  61.8 11.2 %all_to_all.29.got = bf16[32,24,128]{2,1,0:T(8,128)(2,1)S(1)} all-to-all(bf16[32,24,128]{2,1,0:T(8,128)(2,1)S(1)} %owner.1), channel_id=1, replica_groups=mesh['sub'=8,'grp'=4] {'sub','grp'}, dimensions={0} | all-to-all | bytes 393216 | tf_op jit(solution)/shard_map/all_to_all | solution.py:24
  73.0 0.0 slice-done
  73.0 0.0 slice-done.1
  73.0 0.0 copy-done
  73.0 0.0 copy-done.2
  73.0 0.0 copy-done.5
  73.0 3.3 %extend.1 = (bf16[64,16,144]{2,1,0:T(8,128)(2,1)}, bf16[32,16,144]{2,1,0:T(8,128)(2,1)}) custom-call(s32[1,32]{1,0:T(1,128)S(1)} %copy-done.5, bf16[32,24,128]{2,1,0:T(8,128)(2,1)S(1)} %all_to_all.29.got, bf16[64,16,144]{2,1,0:T(8,128)(2,1)S(1)} %copy-done.2, bf16[32,144,144]{2,1,0:T(8,128)(2,1)S(1)} %copy-done, bf16[64,144,144]{2,1,0:T(8,128)(2,1)S(1)} %bitcast.1), custom_call_target="tpu_custom_call" | custom-call | flops 42467328 | bytes 8650752 | tf_op jit(solution)/shard_map/extend/pallas_call | solution.py:295
  (8 shorter events, 0.0 us)
Async XLA Ops:
  0.6 21.6 %copy-start.6 = (s32[1,32]{1,0:T(1,128)S(1)}, s32[1,32]{1,0:T(1,128)}, u32[]{:S(2)}) copy-start(s32[1,32]{1,0:T(1,128)} %recv.3) | copy-start | bytes 388
  0.6 21.6 %copy-start.7 = (f32[128,512]{1,0:T(8,128)S(1)}, f32[128,512]{1,0:T(8,128)}, u32[]{:S(2)}) copy-start(f32[128,512]{1,0:T(8,128)} %cinv.1) | copy-start | bytes 786436
  22.2 13.4 %copy-start.3 = (bf16[32,64,144]{2,1,0:T(8,128)(2,1)S(1)}, bf16[32,64,144]{2,1,0:T(8,128)(2,1)}, u32[]{:S(2)}) copy-start(bf16[32,64,144]{2,1,0:T(8,128)(2,1)} %basis.3) | copy-start | bytes 1769476
  22.2 13.4 %copy-start.4 = (s32[1,32]{1,0:T(1,128)S(1)}, s32[1,32]{1,0:T(1,128)}, u32[]{:S(2)}) copy-start(s32[1,32]{1,0:T(1,128)} %sharers.3) | copy-start | bytes 388
  23.4 49.6 %slice-start = ((s8[4718592]{0:T(1024)(128)(4,1)}), s8[4194304]{0:T(1024)(128)(4,1)S(1)}, s32[]{:S(2)}) async-start(s8[4718592]{0:T(1024)(128)(4,1)} %bitcast), calls=%async_computation.5 | async-start | bytes 8388608
  35.6 11.2 %copy-start.1 = (bf16[32,144,144]{2,1,0:T(8,128)(2,1)S(1)}, bf16[32,144,144]{2,1,0:T(8,128)(2,1)}, u32[]{:S(2)}) copy-start(bf16[32,144,144]{2,1,0:T(8,128)(2,1)} %inv.4) | copy-start | bytes 3981316
  35.6 37.4 %slice-start.1 = ((s8[4718592]{0:T(1024)(128)(4,1)}), s8[524288]{0:T(1024)(128)(4,1)S(1)}, s32[]{:S(2)}) async-start(s8[4718592]{0:T(1024)(128)(4,1)} %bitcast), calls=%async_computation.6 | async-start | bytes 1048576
  46.9 26.1 %copy-start = (bf16[32,144,144]{2,1,0:T(8,128)(2,1)S(1)}, bf16[32,144,144]{2,1,0:T(8,128)(2,1)}, u32[]{:S(2)}) copy-start(bf16[32,144,144]{2,1,0:T(8,128)(2,1)} %couple.3) | copy-start | bytes 3981316
  46.9 26.1 %copy-start.2 = (bf16[64,16,144]{2,1,0:T(8,128)(2,1)S(1)}, bf16[64,16,144]{2,1,0:T(8,128)(2,1)}, u32[]{:S(2)}) copy-start(bf16[64,16,144]{2,1,0:T(8,128)(2,1)} %inner.3) | copy-start | bytes 884740
  46.9 26.1 %copy-start.5 = (s32[1,32]{1,0:T(1,128)S(1)}, s32[1,32]{1,0:T(1,128)}, u32[]{:S(2)}) copy-start(s32[1,32]{1,0:T(1,128)} %elem.1) | copy-start | bytes 388

commit v5 on v4

--- a/solution.py
+++ b/solution.py
@@ -18,6 +18,7 @@
 SMEM = pl.BlockSpec(memory_space=pltpu.SMEM)
 HBM = pl.BlockSpec(memory_space=pltpu.HBM)
 CHUNK = 16
+ROWS = 4
 
 
 def exchange(blocks):
@@ -34,22 +35,19 @@
 
 
 def pack(out, slot, value, extra):
-    rhs, width = value.shape
-    tail = width - LANES
-    half = rhs // 2
-    out[slot, 0:rhs, :] = value[:, :LANES].astype(BF16)
-    end = value[:, LANES:]
-    out[slot, rhs : rhs + half, :] = jnp.concatenate(
-        [end[:half], end[half:], extra[:, 2 * tail :]], axis=1
-    ).astype(BF16)
+    count = value.shape[0] // ROWS
+    value_rows = [value[ROWS * j : ROWS * (j + 1)] for j in range(count)]
+    for j in range(count):
+        out[slot, j] = value_rows[j][:, :LANES].astype(BF16)
+    out[slot, count] = jnp.concatenate([v[:, LANES:] for v in value_rows] + [extra], axis=1).astype(BF16)
 
 
 def unpack(ref, slot, rhs, tail):
-    half = rhs // 2
-    main = ref[slot, 0:rhs, :].astype(F32)
-    last = ref[slot, rhs : rhs + half, :].astype(F32)
-    end = jnp.concatenate([last[:, :tail], last[:, tail : 2 * tail]], axis=0)
-    return jnp.concatenate([main, end], axis=1)
+    count = rhs // ROWS
+    main = [ref[slot, j].astype(F32) for j in range(count)]
+    last = ref[slot, count].astype(F32)
+    end = [last[:, j * tail : (j + 1) * tail] for j in range(count)]
+    return jnp.concatenate([jnp.concatenate(main, axis=0), jnp.concatenate(end, axis=0)], axis=1)
 
 
 def loop(count, step, group=16):
@@ -104,8 +102,9 @@
     maps = cmap[...]
     digits = jnp.concatenate([maps // DIGIT, maps % DIGIT], axis=0).astype(F32)
     local = digits.shape[1]
-    digits = jnp.concatenate([digits, jnp.zeros((rhs // 2 - 2, local), F32)], axis=0)
-    extra = jnp.concatenate([jnp.zeros((rhs // 2, LANES - local), F32), digits], axis=1)
+    spare = LANES - rhs // ROWS * (width - LANES)
+    digits = jnp.concatenate([digits, jnp.zeros((ROWS - 2, local), F32)], axis=0)
+    extra = jnp.concatenate([jnp.zeros((ROWS, spare - local), F32), digits], axis=1) if spare > local else digits
     for c in range(chunks):
         copy(inner.at[pl.ds(0, step)], rin.at[part(c)], sems.at[0, c]).wait()
         copy(inv.at[pl.ds(0, step)], invs.at[part(c)], sems.at[1, c]).wait()
@@ -129,23 +128,24 @@
 
     def add(s):
         j = recv[0, s]
-        sums[j] += got[s, :rows, :].astype(F32)
+        sums[j] += got[s, :rows].astype(F32)
 
     loop(slots, add)
     rounded[...] = sums[...].astype(BF16)
     rounded[owned] = jnp.zeros(rounded.shape[1:], BF16)
 
     def give(s):
-        out[s, :rows, :] = rounded[recv[0, s]]
+        out[s, :rows] = rounded[recv[0, s]]
 
     loop(slots, give)
 
 
-def pair_digits(first, d, rhs, local):
+def pair_digits(first, d, local):
+    last = first.shape[1] - 1
     at = LANES - local
-    low = first[d, rhs : rhs + rhs // 2, :].astype(F32)
-    top = first[d + 1, rhs : rhs + rhs // 2, :].astype(F32)
-    both = jnp.concatenate([low[:, at:], top[:, at:]], axis=1).astype(jnp.int32)
+    low = first[d, last].astype(F32)
+    top = first[d + 1, last].astype(F32)
+    both = jnp.concatenate([low[:2, at:], top[:2, at:]], axis=1).astype(jnp.int32)
     return both[0:1], both[1:2]
 
 
@@ -171,10 +171,9 @@
 
 
 def first_owner_kernel(recv, got, cinv, out, sums, rounded, strip):
-    slots, height, _ = out.shape
+    slots, height, _, _ = out.shape
     head = got.shape[1]
     piece = strip.shape[0]
-    rhs = head * 2 // 3
     local = LANES // 2
     assemble(recv, got, out, sums, rounded)
     start = pl.multiple_of(lax.axis_index("sub") * piece, piece)
@@ -182,10 +181,11 @@
     left = lax.broadcasted_iota(jnp.int32, (piece // 2, LANES), 1) < local
 
     def step(p):
-        taken = take_lanes(strip, *pair_digits(got, 2 * p, rhs, local))
+        taken = take_lanes(strip, *pair_digits(got, 2 * p, local))
         low, top = halves(taken, local, left)
-        out[2 * p, head:, :] = low.astype(BF16)
-        out[2 * p + 1, head:, :] = top.astype(BF16)
+        for j in range(height - head):
+            out[2 * p, head + j] = low[ROWS * j : ROWS * (j + 1)].astype(BF16)
+            out[2 * p + 1, head + j] = top[ROWS * j : ROWS * (j + 1)].astype(BF16)
 
     loop(slots // 2, step)
 
@@ -217,12 +217,15 @@
     loop(slots, give)
 
 
-def turn_columns(groups, rows, got, head, piece, turned):
+def turn_columns(groups, rows, got, head, turned):
     local, total = turned.shape
+    piece = (got.shape[1] - head) * ROWS * 2
     for t in range(total // LANES):
         parts = []
         for k in range(t * LANES, (t + 1) * LANES, piece):
-            block = got[(k % rows) // piece * groups + k // rows, head:, :].astype(F32)
+            device = (k % rows) // piece * groups + k // rows
+            block = [got[device, j].astype(F32) for j in range(head, got.shape[1])]
+            block = jnp.concatenate(block, axis=0)
             parts += [block, pltpu.roll(block, local, 1)]
         turned[:, t * LANES : (t + 1) * LANES] = jnp.concatenate(parts, axis=0).T[:local]
 
@@ -231,7 +234,7 @@
     slots, rhs, width = restricted.shape
     head = first.shape[1]
     local = basis.shape[1]
-    turn_columns(groups, rows, second, head, (second.shape[1] - head) * 2, turned)
+    turn_columns(groups, rows, second, head, turned)
     sums[...] = jnp.zeros_like(sums)
     left = lax.broadcasted_iota(jnp.int32, (rhs // 2, LANES), 1) < local
     group = min(slots // 2, 8)
@@ -240,7 +243,7 @@
         part = None
         for u in range(group):
             p = g * group + u
-            columns = take_lanes(turned, *pair_digits(first, 2 * p, rhs, local)).astype(BF16)
+            columns = take_lanes(turned, *pair_digits(first, 2 * p, local)).astype(BF16)
             low = got[2 * p].astype(F32)
             top = got[2 * p + 1].astype(F32)
             value = jnp.concatenate(halves(jnp.concatenate([low, top], axis=0), local, left), axis=0)
@@ -251,7 +254,7 @@
 
     lax.fori_loop(0, slots // 2 // group, body, 0)
     picked = sums[...].astype(BF16)
-    extra = jnp.zeros((rhs // 2, LANES), F32)
+    extra = jnp.zeros((ROWS, LANES - rhs // ROWS * (width - LANES)), F32)
 
     def finish(l):
         value = dot(picked, basis[l]) + dot(restricted[l], inv[l], NT)
@@ -282,7 +285,8 @@
     size = jnp.dtype(dtype).itemsize
     for n in shape[:-2]:
         size *= n
-    return size * (-(-shape[-2] // 16) * 16) * (-(-shape[-1] // LANES) * LANES)
+    high = shape[-2] if shape[-2] < 8 else -(-shape[-2] // 16) * 16
+    return size * high * (-(-shape[-1] // LANES) * LANES)
 
 
 def call(kernel, out_shape, specs, args, scratch=(), flops=0, name=None, limit=None, out_spec=VMEM):
@@ -325,10 +329,10 @@
     groups = total // rows
     piece = rows * groups // slots
     shape = jax.ShapeDtypeStruct
-    head = rhs + rhs // 2
-    wire = shape((slots, head, LANES), BF16)
+    head = rhs // ROWS + 1
+    wire = shape((slots, head, ROWS, LANES), BF16)
     unit = 2 * rhs * width * width
-    tables = [((owned + 1, head, LANES), F32), ((owned + 1, head, LANES), BF16)]
+    tables = [((owned + 1, head, ROWS, LANES), F32), ((owned + 1, head, ROWS, LANES), BF16)]
 
     sent = call(
         condense_kernel,
@@ -343,7 +347,7 @@
             ((slots, width, width), BF16),
             ((slots, width, width), BF16),
             ((slots, rhs, width), BF16),
-            ((slots, head, LANES), BF16),
+            (wire.shape, BF16),
             (pltpu.SemaphoreType.DMA((5, -(-slots // CHUNK))), None),
             (pltpu.SemaphoreType.DMA((3,)), None),
         ],
@@ -355,7 +359,7 @@
     first = exchange(sent)
     held = call(
         first_owner_kernel,
-        shape((slots, head + piece // 2, LANES), BF16),
+        shape((slots, head + piece // (2 * ROWS), ROWS, LANES), BF16),
         [SMEM, VMEM, VMEM],
         (recv_index, first, coarse_inv),
         tables + [((piece, total), F32)],
@@ -384,7 +388,7 @@
     )
     third = exchange(weighted)
     spread = call(
-        owner_kernel, wire, [SMEM, VMEM], (recv_index, third), tables, flops=slots * head * LANES, name="owner"
+        owner_kernel, wire, [SMEM, VMEM], (recv_index, third), tables, flops=slots * width * LANES, name="owner"
     )
     assembled = exchange(spread)
     return call(

time: 76.6 us -> 74.4 us (0.971)
  blocking collectives: 60.9 us -> 58.6 us
    all_to_all x5, blocking collectives: 60.9 us -> 58.6 us  [exchange(): return lax.all_to_all(blocks, AXES, split_axis=0, concat_axis=0, tiled=True)]
where the time goes in v5:
time: 74.4 us; the launch traced here: 74.2 us
  blocking collectives  58.6 us (79%)
  Pallas kernels  14.7 us (20%)
    all_to_all x5, blocking collectives, exchange(): return lax.all_to_all(blocks, AXES, split_axis=0, concat_axis=0, tiled=True)  58.6 us
    pallas_call x6, Pallas kernels, call(): pl.pallas_call(kernel, out_shape=out_shape, in_specs=specs, out_specs=tup...  14.7 us

profile of v5, /device:TPU:0, one launch (start us, length us, event | category | flops | bytes accessed | tf_op | source)
XLA Modules:
  0.0 74.2 jit_solution(3060547578439659240)
XLA Ops:
  0.6 0.0 copy-start.6
  0.6 0.0 copy-start.7
  0.7 5.0 %condense.1 = bf16[32,5,4,128]{3,2,1,0:T(4,128)(2,1)} custom-call(s32[1,32]{1,0:T(1,128)} %elem.1, s32[1,32]{1,0:T(1,128)} %sharers.3, s32[1,64]{1,0:T(1,128)} %map_in.1, bf16[64,16,144]{2,1,0:T(8,128)(2,1)} %inner.3, bf16[64,144,144]{2,1,0:T(8,128)(2,1)} %inv.5, bf16[32,144,144]{2,1,0:T(8,128)(2,1)} %couple.3, bf16[32,16,144]{2,1,0:T(8,128)(2,1)} %face.1), custom_call_target="tpu_custom_call" | custom-call | flops 42467328 | bytes 163840 | tf_op jit(solution)/shard_map/condense/pallas_call | solution.py:299
  5.7 16.1 %all_to_all.25.got.first = bf16[32,5,4,128]{3,2,1,0:T(4,128)(2,1)S(1)} all-to-all(bf16[32,5,4,128]{3,2,1,0:T(4,128)(2,1)} %condense.1), channel_id=1, replica_groups=mesh['sub'=8,'grp'=4] {'sub','grp'}, dimensions={0} | all-to-all | bytes 327680 | tf_op jit(solution)/shard_map/all_to_all | solution.py:25
  21.8 0.0 copy-done.6
  21.8 0.0 copy-done.7
  21.8 1.2 %first_owner.1 = bf16[32,7,4,128]{3,2,1,0:T(4,128)(2,1)S(1)} custom-call(s32[1,32]{1,0:T(1,128)S(1)} %copy-done.6, bf16[32,5,4,128]{3,2,1,0:T(4,128)(2,1)S(1)} %all_to_all.25.got.first, f32[128,512]{1,0:T(8,128)S(1)} %copy-done.7), custom_call_target="tpu_custom_call" | custom-call | flops 2123366400 | bytes 655360 | tf_op jit(solution)/shard_map/first_owner/pallas_call | solution.py:299
  23.0 0.0 slice-start
  23.0 11.7 %all_to_all.26.got.second = bf16[32,7,4,128]{3,2,1,0:T(4,128)(2,1)S(1)} all-to-all(bf16[32,7,4,128]{3,2,1,0:T(4,128)(2,1)S(1)} %first_owner.1), channel_id=1, replica_groups=mesh['sub'=8,'grp'=4] {'sub','grp'}, dimensions={0} | all-to-all | bytes 458752 | tf_op jit(solution)/shard_map/all_to_all | solution.py:25
  34.7 0.0 copy-done.3
  34.7 0.0 copy-done.4
  34.8 1.3 %restrict.1 = (bf16[32,8,128]{2,1,0:T(8,128)(2,1)S(1)}, bf16[32,16,144]{2,1,0:T(8,128)(2,1)S(1)}) custom-call(s32[1,32]{1,0:T(1,128)S(1)} %copy-done.4, bf16[32,7,4,128]{3,2,1,0:T(4,128)(2,1)S(1)} %all_to_all.26.got.second, bf16[32,64,144]{2,1,0:T(8,128)(2,1)S(1)} %copy-done.3), custom_call_target="tpu_custom_call" | custom-call | flops 2123366400 | bytes 1671168 | tf_op jit(solution)/shard_map/restrict/pallas_call | solution.py:299
  36.1 9.7 %all_to_all.27.got = bf16[32,8,128]{2,1,0:T(8,128)(2,1)S(1)} all-to-all(bf16[32,8,128]{2,1,0:T(8,128)(2,1)S(1)} %get-tuple-element.4), channel_id=1, replica_groups=mesh['sub'=8,'grp'=4] {'sub','grp'}, dimensions={0} | all-to-all | bytes 131072 | tf_op jit(solution)/shard_map/all_to_all | solution.py:25
  45.8 0.0 copy-done.1
  45.8 3.1 %correct.1 = bf16[32,5,4,128]{3,2,1,0:T(4,128)(2,1)S(1)} custom-call(s32[1,32]{1,0:T(1,128)S(1)} %copy-done.4, bf16[32,8,128]{2,1,0:T(8,128)(2,1)S(1)} %all_to_all.27.got, bf16[32,5,4,128]{3,2,1,0:T(4,128)(2,1)S(1)} %all_to_all.25.got.first, bf16[32,7,4,128]{3,2,1,0:T(4,128)(2,1)S(1)} %all_to_all.26.got.second, ...), custom_call_target="tpu_custom_call" | custom-call | flops 42467328 | bytes 4358144 | tf_op jit(solution)/shard_map/correct/pallas_call | solution.py:299
  48.9 10.5 %all_to_all.28.got = bf16[32,5,4,128]{3,2,1,0:T(4,128)(2,1)S(1)} all-to-all(bf16[32,5,4,128]{3,2,1,0:T(4,128)(2,1)S(1)} %correct.1), channel_id=1, replica_groups=mesh['sub'=8,'grp'=4] {'sub','grp'}, dimensions={0} | all-to-all | bytes 327680 | tf_op jit(solution)/shard_map/all_to_all | solution.py:25
  59.4 0.9 %owner.1 = bf16[32,5,4,128]{3,2,1,0:T(4,128)(2,1)S(1)} custom-call(s32[1,32]{1,0:T(1,128)S(1)} %copy-done.6, bf16[32,5,4,128]{3,2,1,0:T(4,128)(2,1)S(1)} %all_to_all.28.got), custom_call_target="tpu_custom_call" | custom-call | flops 589824 | bytes 327680 | tf_op jit(solution)/shard_map/owner/pallas_call | solution.py:299
  60.3 10.6 %all_to_all.29.got = bf16[32,5,4,128]{3,2,1,0:T(4,128)(2,1)S(1)} all-to-all(bf16[32,5,4,128]{3,2,1,0:T(4,128)(2,1)S(1)} %owner.1), channel_id=1, replica_groups=mesh['sub'=8,'grp'=4] {'sub','grp'}, dimensions={0} | all-to-all | bytes 327680 | tf_op jit(solution)/shard_map/all_to_all | solution.py:25
  70.8 0.0 slice-done
  70.8 0.0 slice-done.1
  70.8 0.0 copy-done
  70.8 0.0 copy-done.2
  70.8 0.0 copy-done.5
  70.8 3.3 %extend.1 = (bf16[64,16,144]{2,1,0:T(8,128)(2,1)}, bf16[32,16,144]{2,1,0:T(8,128)(2,1)}) custom-call(s32[1,32]{1,0:T(1,128)S(1)} %copy-done.5, bf16[32,5,4,128]{3,2,1,0:T(4,128)(2,1)S(1)} %all_to_all.29.got, bf16[64,16,144]{2,1,0:T(8,128)(2,1)S(1)} %copy-done.2, bf16[32,144,144]{2,1,0:T(8,128)(2,1)S(1)} %copy-done, bf16[64,144,144]{2,1,0:T(8,128)(2,1)S(1)} %bitcast.1), custom_call_target="tpu_custom_call" | custom-call | flops 42467328 | bytes 8552448 | tf_op jit(solution)/shard_map/extend/pallas_call | solution.py:299
  (8 shorter events, 0.0 us)
Async XLA Ops:
  0.6 21.1 %copy-start.6 = (s32[1,32]{1,0:T(1,128)S(1)}, s32[1,32]{1,0:T(1,128)}, u32[]{:S(2)}) copy-start(s32[1,32]{1,0:T(1,128)} %recv.3) | copy-start | bytes 388
  0.6 21.1 %copy-start.7 = (f32[128,512]{1,0:T(8,128)S(1)}, f32[128,512]{1,0:T(8,128)}, u32[]{:S(2)}) copy-start(f32[128,512]{1,0:T(8,128)} %cinv.1) | copy-start | bytes 786436
  21.8 13.0 %copy-start.3 = (bf16[32,64,144]{2,1,0:T(8,128)(2,1)S(1)}, bf16[32,64,144]{2,1,0:T(8,128)(2,1)}, u32[]{:S(2)}) copy-start(bf16[32,64,144]{2,1,0:T(8,128)(2,1)} %basis.3) | copy-start | bytes 1769476
  21.8 13.0 %copy-start.4 = (s32[1,32]{1,0:T(1,128)S(1)}, s32[1,32]{1,0:T(1,128)}, u32[]{:S(2)}) copy-start(s32[1,32]{1,0:T(1,128)} %sharers.3) | copy-start | bytes 388
  23.0 47.8 %slice-start = ((s8[4718592]{0:T(1024)(128)(4,1)}), s8[4194304]{0:T(1024)(128)(4,1)S(1)}, s32[]{:S(2)}) async-start(s8[4718592]{0:T(1024)(128)(4,1)} %bitcast), calls=%async_computation.5 | async-start | bytes 8388608
  34.8 11.0 %copy-start.1 = (bf16[32,144,144]{2,1,0:T(8,128)(2,1)S(1)}, bf16[32,144,144]{2,1,0:T(8,128)(2,1)}, u32[]{:S(2)}) copy-start(bf16[32,144,144]{2,1,0:T(8,128)(2,1)} %inv.4) | copy-start | bytes 3981316
  34.8 36.1 %slice-start.1 = ((s8[4718592]{0:T(1024)(128)(4,1)}), s8[524288]{0:T(1024)(128)(4,1)S(1)}, s32[]{:S(2)}) async-start(s8[4718592]{0:T(1024)(128)(4,1)} %bitcast), calls=%async_computation.6 | async-start | bytes 1048576
  45.8 25.0 %copy-start = (bf16[32,144,144]{2,1,0:T(8,128)(2,1)S(1)}, bf16[32,144,144]{2,1,0:T(8,128)(2,1)}, u32[]{:S(2)}) copy-start(bf16[32,144,144]{2,1,0:T(8,128)(2,1)} %couple.3) | copy-start | bytes 3981316
  45.8 25.0 %copy-start.2 = (bf16[64,16,144]{2,1,0:T(8,128)(2,1)S(1)}, bf16[64,16,144]{2,1,0:T(8,128)(2,1)}, u32[]{:S(2)}) copy-start(bf16[64,16,144]{2,1,0:T(8,128)(2,1)} %inner.3) | copy-start | bytes 884740
  45.8 25.1 %copy-start.5 = (s32[1,32]{1,0:T(1,128)S(1)}, s32[1,32]{1,0:T(1,128)}, u32[]{:S(2)}) copy-start(s32[1,32]{1,0:T(1,128)} %elem.1) | copy-start | bytes 388

commit v6 on v5

--- a/solution.py
+++ b/solution.py
@@ -62,7 +62,7 @@
 
 
 def condense_kernel(
-    elem_in, sharers_in, map_in, inner, inv, couple, face, out, elem, sharers, cmap, rin, invs, cps, fac, stage, sems, small
+    elem_in, sharers_in, map_in, inner, inv, couple, face, out, elem, sharers, cmap, rin, invs, cps, fac, sems, small
 ):
     slots, rhs, width = fac.shape
     step = min(slots, CHUNK)
@@ -77,9 +77,6 @@
 
     def face_copy(c):
         return copy(face.at[part(c)], fac.at[part(c)], sems.at[3, c])
-
-    def out_copy(c):
-        return copy(stage.at[part(c)], out.at[part(c)], sems.at[4, c])
 
     first = copy(elem_in, elem, small.at[0])
     others = [copy(sharers_in, sharers, small.at[1]), copy(map_in, cmap, small.at[2])]
@@ -114,10 +111,7 @@
         for u in range(step):
             l = c * step + u
             value = fac[l].astype(F32) - dot(near[u], cps[l], NT)
-            pack(stage, l, omega(sharers, l) * value, extra)
-        out_copy(c).start()
-    for c in range(chunks):
-        out_copy(c).wait()
+            pack(out, l, omega(sharers, l) * value, extra)
 
 
 def assemble(recv, got, out, sums, rounded):
@@ -130,14 +124,14 @@
         j = recv[0, s]
         sums[j] += got[s, :rows].astype(F32)
 
-    loop(slots, add)
+    loop(slots, add, 32)
     rounded[...] = sums[...].astype(BF16)
     rounded[owned] = jnp.zeros(rounded.shape[1:], BF16)
 
     def give(s):
         out[s, :rows] = rounded[recv[0, s]]
 
-    loop(slots, give)
+    loop(slots, give, 32)
 
 
 def pair_digits(first, d, local):
@@ -193,7 +187,7 @@
 def restrict_kernel(sharers, got, basis, out, restricted, total):
     slots, rhs, width = restricted.shape
     tail = width - LANES
-    group = min(slots, 16)
+    group = min(slots, 32)
     total[...] = jnp.zeros_like(total)
 
     def body(g, carry):
@@ -214,7 +208,7 @@
     def give(d):
         out[d] = block
 
-    loop(slots, give)
+    loop(slots, give, 32)
 
 
 def turn_columns(groups, rows, got, head, turned):
@@ -237,7 +231,7 @@
     turn_columns(groups, rows, second, head, turned)
     sums[...] = jnp.zeros_like(sums)
     left = lax.broadcasted_iota(jnp.int32, (rhs // 2, LANES), 1) < local
-    group = min(slots // 2, 8)
+    group = min(slots // 2, 16)
 
     def body(g, carry):
         part = None
@@ -260,25 +254,35 @@
         value = dot(picked, basis[l]) + dot(restricted[l], inv[l], NT)
         pack(out, l, omega(sharers, l) * value, extra)
 
-    loop(slots, finish)
-
-
-def extend_kernel(elem, got, inner, couple, inv, inner_out, face_out, sums):
-    slots, rhs, width = face_out.shape
+    loop(slots, finish, 32)
+
+
+def extend_kernel(elem, got, inner, couple, inv, inner_out, face_out, sums, faces, inners, sems):
+    slots, rhs, width = faces.shape
+    elements = inners.shape[0]
     tail = width - LANES
     sums[...] = inner[...].astype(F32)
 
     def step(l):
         value = unpack(got, l, rhs, tail).astype(BF16)
-        face_out[l] = value
+        faces[l] = value
         sums[elem[0, l]] -= dot(value, couple[l])
 
     loop(slots, step, 32)
-
-    def finish(e):
-        inner_out[e] = dot(sums[e].astype(BF16), inv[e], NT).astype(BF16)
-
-    loop(inner_out.shape[0], finish, 32)
+    copies = [pltpu.make_async_copy(faces, face_out, sems.at[0])]
+    copies[0].start()
+    part = elements // 2
+    for c in range(2):
+
+        def finish(e):
+            inners[c * part + e] = dot(sums[c * part + e].astype(BF16), inv[c * part + e], NT).astype(BF16)
+
+        loop(part, finish, 32)
+        span = pl.ds(c * part, part)
+        copies.append(pltpu.make_async_copy(inners.at[span], inner_out.at[span], sems.at[1 + c]))
+        copies[-1].start()
+    for each in copies:
+        each.wait()
 
 
 def padded(shape, dtype):
@@ -300,7 +304,7 @@
         kernel,
         out_shape=out_shape,
         in_specs=specs,
-        out_specs=tuple(VMEM for _ in outs) if many else out_spec,
+        out_specs=tuple(out_spec for _ in outs) if many else out_spec,
         scratch_shapes=made,
         cost_estimate=pl.CostEstimate(flops=flops, bytes_accessed=need, transcendentals=0),
         compiler_params=pltpu.CompilerParams(vmem_limit_bytes=limit or need + room + (2 << 20)),
@@ -338,7 +342,10 @@
         condense_kernel,
         wire,
         [HBM] * 7,
-        (face_elem, sharers, coarse_map, res_inner, inner_inv, face_coupling, res_face),
+        tuple(
+            pltpu.with_memory_space_constraint(x, pltpu.HBM)
+            for x in (face_elem, sharers, coarse_map, res_inner, inner_inv, face_coupling, res_face)
+        ),
         [
             (pltpu.SMEM(face_elem.shape, jnp.int32), None),
             (pltpu.SMEM(sharers.shape, jnp.int32), None),
@@ -347,14 +354,11 @@
             ((slots, width, width), BF16),
             ((slots, width, width), BF16),
             ((slots, rhs, width), BF16),
-            (wire.shape, BF16),
-            (pltpu.SemaphoreType.DMA((5, -(-slots // CHUNK))), None),
+            (pltpu.SemaphoreType.DMA((4, -(-slots // CHUNK))), None),
             (pltpu.SemaphoreType.DMA((3,)), None),
         ],
         flops=2 * slots * unit,
         name="condense",
-        limit=60 * 1024 * 1024,
-        out_spec=HBM,
     )
     first = exchange(sent)
     held = call(
@@ -396,9 +400,15 @@
         (shape((elements, rhs, width), BF16), shape((slots, rhs, width), BF16)),
         [SMEM, VMEM, VMEM, VMEM, VMEM],
         (face_elem, assembled, res_inner, face_coupling, inner_inv),
-        [((elements, rhs, width), F32)],
+        [
+            ((elements, rhs, width), F32),
+            ((slots, rhs, width), BF16),
+            ((elements, rhs, width), BF16),
+            (pltpu.SemaphoreType.DMA((3,)), None),
+        ],
         flops=2 * slots * unit,
         name="extend",
+        out_spec=HBM,
     )
 
 

time: 74.4 us -> 72.2 us (0.970)
  Pallas kernels: 14.7 us -> 12.7 us
    pallas_call x6, Pallas kernels: 14.7 us -> 12.7 us  [call(): pl.pallas_call(kernel, out_shape=out_shape, in_specs=specs, out_specs=tup...]
where the time goes in v6:
time: 72.2 us; the launch traced here: 72 us
  blocking collectives  58.5 us (81%)
  Pallas kernels  12.7 us (18%)
  between operations  0.73 us (1%)
    all_to_all x5, blocking collectives, exchange(): return lax.all_to_all(blocks, AXES, split_axis=0, concat_axis=0, tiled=True)  58.5 us
    pallas_call x6, Pallas kernels, call(): pl.pallas_call(kernel, out_shape=out_shape, in_specs=specs, out_specs=tup...  12.7 us

profile of v6, /device:TPU:0, one launch (start us, length us, event | category | flops | bytes accessed | tf_op | source)
XLA Modules:
  0.0 72.0 jit_solution(3887783540669435083)
XLA Ops:
  0.6 0.0 copy-start.6
  0.6 0.0 copy-start.7
  0.7 4.2 %condense.1 = bf16[32,5,4,128]{3,2,1,0:T(4,128)(2,1)S(1)} custom-call(s32[1,32]{1,0:T(1,128)} %elem.1, s32[1,32]{1,0:T(1,128)} %sharers.3, s32[1,64]{1,0:T(1,128)} %map_in.1, bf16[64,16,144]{2,1,0:T(8,128)(2,1)} %inner.3, bf16[64,144,144]{2,1,0:T(8,128)(2,1)} %inv.5, bf16[32,144,144]{2,1,0:T(8,128)(2,1)} %couple.3, bf16[32,16,144]{2,1,0:T(8,128)(2,1)} %face.1), custom_call_target="tpu_custom_call" | custom-call | flops 42467328 | bytes 163840 | tf_op jit(solution)/shard_map/condense/pallas_call | solution.py:303
  4.9 16.0 %all_to_all.25.got.first = bf16[32,5,4,128]{3,2,1,0:T(4,128)(2,1)S(1)} all-to-all(bf16[32,5,4,128]{3,2,1,0:T(4,128)(2,1)S(1)} %condense.1), channel_id=1, replica_groups=mesh['sub'=8,'grp'=4] {'sub','grp'}, dimensions={0} | all-to-all | bytes 327680 | tf_op jit(solution)/shard_map/all_to_all | solution.py:25
  20.9 0.0 copy-done.6
  20.9 0.0 copy-done.7
  20.9 0.9 %first_owner.1 = bf16[32,7,4,128]{3,2,1,0:T(4,128)(2,1)S(1)} custom-call(s32[1,32]{1,0:T(1,128)S(1)} %copy-done.6, bf16[32,5,4,128]{3,2,1,0:T(4,128)(2,1)S(1)} %all_to_all.25.got.first, f32[128,512]{1,0:T(8,128)S(1)} %copy-done.7), custom_call_target="tpu_custom_call" | custom-call | flops 2123366400 | bytes 655360 | tf_op jit(solution)/shard_map/first_owner/pallas_call | solution.py:303
  21.8 0.0 slice-start
  21.9 11.7 %all_to_all.26.got.second = bf16[32,7,4,128]{3,2,1,0:T(4,128)(2,1)S(1)} all-to-all(bf16[32,7,4,128]{3,2,1,0:T(4,128)(2,1)S(1)} %first_owner.1), channel_id=1, replica_groups=mesh['sub'=8,'grp'=4] {'sub','grp'}, dimensions={0} | all-to-all | bytes 458752 | tf_op jit(solution)/shard_map/all_to_all | solution.py:25
  33.6 0.0 copy-done.3
  33.6 0.0 copy-done.4
  33.6 1.1 %restrict.1 = (bf16[32,8,128]{2,1,0:T(8,128)(2,1)S(1)}, bf16[32,16,144]{2,1,0:T(8,128)(2,1)S(1)}) custom-call(s32[1,32]{1,0:T(1,128)S(1)} %copy-done.4, bf16[32,7,4,128]{3,2,1,0:T(4,128)(2,1)S(1)} %all_to_all.26.got.second, bf16[32,64,144]{2,1,0:T(8,128)(2,1)S(1)} %copy-done.3), custom_call_target="tpu_custom_call" | custom-call | flops 2123366400 | bytes 1671168 | tf_op jit(solution)/shard_map/restrict/pallas_call | solution.py:303
  34.7 9.7 %all_to_all.27.got = bf16[32,8,128]{2,1,0:T(8,128)(2,1)S(1)} all-to-all(bf16[32,8,128]{2,1,0:T(8,128)(2,1)S(1)} %get-tuple-element.4), channel_id=1, replica_groups=mesh['sub'=8,'grp'=4] {'sub','grp'}, dimensions={0} | all-to-all | bytes 131072 | tf_op jit(solution)/shard_map/all_to_all | solution.py:25
  44.4 0.0 copy-done.1
  44.4 2.5 %correct.1 = bf16[32,5,4,128]{3,2,1,0:T(4,128)(2,1)S(1)} custom-call(s32[1,32]{1,0:T(1,128)S(1)} %copy-done.4, bf16[32,8,128]{2,1,0:T(8,128)(2,1)S(1)} %all_to_all.27.got, bf16[32,5,4,128]{3,2,1,0:T(4,128)(2,1)S(1)} %all_to_all.25.got.first, bf16[32,7,4,128]{3,2,1,0:T(4,128)(2,1)S(1)} %all_to_all.26.got.second, ...), custom_call_target="tpu_custom_call" | custom-call | flops 42467328 | bytes 4358144 | tf_op jit(solution)/shard_map/correct/pallas_call | solution.py:303
  46.9 10.5 %all_to_all.28.got = bf16[32,5,4,128]{3,2,1,0:T(4,128)(2,1)S(1)} all-to-all(bf16[32,5,4,128]{3,2,1,0:T(4,128)(2,1)S(1)} %correct.1), channel_id=1, replica_groups=mesh['sub'=8,'grp'=4] {'sub','grp'}, dimensions={0} | all-to-all | bytes 327680 | tf_op jit(solution)/shard_map/all_to_all | solution.py:25
  57.5 0.8 %owner.1 = bf16[32,5,4,128]{3,2,1,0:T(4,128)(2,1)S(1)} custom-call(s32[1,32]{1,0:T(1,128)S(1)} %copy-done.6, bf16[32,5,4,128]{3,2,1,0:T(4,128)(2,1)S(1)} %all_to_all.28.got), custom_call_target="tpu_custom_call" | custom-call | flops 589824 | bytes 327680 | tf_op jit(solution)/shard_map/owner/pallas_call | solution.py:303
  58.3 10.6 %all_to_all.29.got = bf16[32,5,4,128]{3,2,1,0:T(4,128)(2,1)S(1)} all-to-all(bf16[32,5,4,128]{3,2,1,0:T(4,128)(2,1)S(1)} %owner.1), channel_id=1, replica_groups=mesh['sub'=8,'grp'=4] {'sub','grp'}, dimensions={0} | all-to-all | bytes 327680 | tf_op jit(solution)/shard_map/all_to_all | solution.py:25
  68.9 0.0 slice-done
  68.9 0.0 slice-done.1
  68.9 0.0 copy-done
  68.9 0.0 copy-done.2
  68.9 0.0 copy-done.5
  68.9 3.1 %extend.1 = (bf16[64,16,144]{2,1,0:T(8,128)(2,1)}, bf16[32,16,144]{2,1,0:T(8,128)(2,1)}) custom-call(s32[1,32]{1,0:T(1,128)S(1)} %copy-done.5, bf16[32,5,4,128]{3,2,1,0:T(4,128)(2,1)S(1)} %all_to_all.29.got, bf16[64,16,144]{2,1,0:T(8,128)(2,1)S(1)} %copy-done.2, bf16[32,144,144]{2,1,0:T(8,128)(2,1)S(1)} %copy-done, bf16[64,144,144]{2,1,0:T(8,128)(2,1)S(1)} %bitcast.1), custom_call_target="tpu_custom_call" | custom-call | flops 42467328 | bytes 8552448 | tf_op jit(solution)/shard_map/extend/pallas_call | solution.py:303
  (8 shorter events, 0.0 us)
Async XLA Ops:
  0.6 20.3 %copy-start.6 = (s32[1,32]{1,0:T(1,128)S(1)}, s32[1,32]{1,0:T(1,128)}, u32[]{:S(2)}) copy-start(s32[1,32]{1,0:T(1,128)} %recv.3) | copy-start | bytes 388
  0.6 20.2 %copy-start.7 = (f32[128,512]{1,0:T(8,128)S(1)}, f32[128,512]{1,0:T(8,128)}, u32[]{:S(2)}) copy-start(f32[128,512]{1,0:T(8,128)} %cinv.1) | copy-start | bytes 786436
  20.9 12.7 %copy-start.3 = (bf16[32,64,144]{2,1,0:T(8,128)(2,1)S(1)}, bf16[32,64,144]{2,1,0:T(8,128)(2,1)}, u32[]{:S(2)}) copy-start(bf16[32,64,144]{2,1,0:T(8,128)(2,1)} %basis.3) | copy-start | bytes 1769476
  20.9 12.7 %copy-start.4 = (s32[1,32]{1,0:T(1,128)S(1)}, s32[1,32]{1,0:T(1,128)}, u32[]{:S(2)}) copy-start(s32[1,32]{1,0:T(1,128)} %sharers.3) | copy-start | bytes 388
  21.8 47.0 %slice-start = ((s8[4718592]{0:T(1024)(128)(4,1)}), s8[4194304]{0:T(1024)(128)(4,1)S(1)}, s32[]{:S(2)}) async-start(s8[4718592]{0:T(1024)(128)(4,1)} %bitcast), calls=%async_computation.5 | async-start | bytes 8388608
  33.6 10.8 %copy-start.1 = (bf16[32,144,144]{2,1,0:T(8,128)(2,1)S(1)}, bf16[32,144,144]{2,1,0:T(8,128)(2,1)}, u32[]{:S(2)}) copy-start(bf16[32,144,144]{2,1,0:T(8,128)(2,1)} %inv.4) | copy-start | bytes 3981316
  33.6 35.3 %slice-start.1 = ((s8[4718592]{0:T(1024)(128)(4,1)}), s8[524288]{0:T(1024)(128)(4,1)S(1)}, s32[]{:S(2)}) async-start(s8[4718592]{0:T(1024)(128)(4,1)} %bitcast), calls=%async_computation.6 | async-start | bytes 1048576
  44.4 24.5 %copy-start = (bf16[32,144,144]{2,1,0:T(8,128)(2,1)S(1)}, bf16[32,144,144]{2,1,0:T(8,128)(2,1)}, u32[]{:S(2)}) copy-start(bf16[32,144,144]{2,1,0:T(8,128)(2,1)} %couple.3) | copy-start | bytes 3981316
  44.4 24.5 %copy-start.2 = (bf16[64,16,144]{2,1,0:T(8,128)(2,1)S(1)}, bf16[64,16,144]{2,1,0:T(8,128)(2,1)}, u32[]{:S(2)}) copy-start(bf16[64,16,144]{2,1,0:T(8,128)(2,1)} %inner.3) | copy-start | bytes 884740
  44.4 24.5 %copy-start.5 = (s32[1,32]{1,0:T(1,128)S(1)}, s32[1,32]{1,0:T(1,128)}, u32[]{:S(2)}) copy-start(s32[1,32]{1,0:T(1,128)} %elem.1) | copy-start | bytes 388

commit v7 on v6

--- a/solution.py
+++ b/solution.py
@@ -15,10 +15,10 @@
 F32 = jnp.float32
 BF16 = jnp.bfloat16
 VMEM = pl.BlockSpec(memory_space=pltpu.VMEM)
-SMEM = pl.BlockSpec(memory_space=pltpu.SMEM)
 HBM = pl.BlockSpec(memory_space=pltpu.HBM)
 CHUNK = 16
 ROWS = 4
+GROUP = 32
 
 
 def exchange(blocks):
@@ -59,6 +59,23 @@
         return carry
 
     lax.fori_loop(0, count // group, body, 0)
+
+
+def table_loop(table, step):
+    rows, group = table.shape
+
+    def body(g, carry):
+        row = table[pl.ds(g, 1), :]
+        for u in range(group):
+            step(g * group + u, row[0, u])
+        return carry
+
+    lax.fori_loop(0, rows, body, 0)
+
+
+def weights(sharers, g):
+    count = sharers[pl.ds(g, 1), :]
+    return jnp.where(count > 0, 1.0 / jnp.maximum(count, 1).astype(F32), 0.0)
 
 
 def condense_kernel(
@@ -115,23 +132,21 @@
 
 
 def assemble(recv, got, out, sums, rounded):
-    slots = got.shape[0]
     rows = sums.shape[1]
     owned = sums.shape[0] - 1
     sums[...] = jnp.zeros_like(sums)
 
-    def add(s):
-        j = recv[0, s]
+    def add(s, j):
         sums[j] += got[s, :rows].astype(F32)
 
-    loop(slots, add, 32)
+    table_loop(recv, add)
     rounded[...] = sums[...].astype(BF16)
     rounded[owned] = jnp.zeros(rounded.shape[1:], BF16)
 
-    def give(s):
-        out[s, :rows] = rounded[recv[0, s]]
-
-    loop(slots, give, 32)
+    def give(s, j):
+        out[s, :rows] = rounded[j]
+
+    table_loop(recv, give)
 
 
 def pair_digits(first, d, local):
@@ -169,7 +184,6 @@
     head = got.shape[1]
     piece = strip.shape[0]
     local = LANES // 2
-    assemble(recv, got, out, sums, rounded)
     start = pl.multiple_of(lax.axis_index("sub") * piece, piece)
     strip[...] = cinv[pl.ds(start, piece), :]
     left = lax.broadcasted_iota(jnp.int32, (piece // 2, LANES), 1) < local
@@ -182,26 +196,28 @@
             out[2 * p + 1, head + j] = top[ROWS * j : ROWS * (j + 1)].astype(BF16)
 
     loop(slots // 2, step)
+    assemble(recv, got, out, sums, rounded)
 
 
 def restrict_kernel(sharers, got, basis, out, restricted, total):
     slots, rhs, width = restricted.shape
     tail = width - LANES
-    group = min(slots, 32)
+    groups, group = sharers.shape
     total[...] = jnp.zeros_like(total)
 
     def body(g, carry):
         part = None
+        weight = weights(sharers, g)
         for u in range(group):
             l = g * group + u
-            value = (omega(sharers, l) * unpack(got, l, rhs, tail)).astype(BF16)
+            value = (weight[:, u : u + 1] * unpack(got, l, rhs, tail)).astype(BF16)
             restricted[l] = value
             term = dot(value, basis[l], NT)
             part = term if part is None else part + term
         total[...] += part
         return carry
 
-    lax.fori_loop(0, slots // group, body, 0)
+    lax.fori_loop(0, groups, body, 0)
     both = total[...]
     block = jnp.concatenate([both[: rhs // 2], both[rhs // 2 :]], axis=1).astype(BF16)
 
@@ -250,11 +266,15 @@
     picked = sums[...].astype(BF16)
     extra = jnp.zeros((ROWS, LANES - rhs // ROWS * (width - LANES)), F32)
 
-    def finish(l):
-        value = dot(picked, basis[l]) + dot(restricted[l], inv[l], NT)
-        pack(out, l, omega(sharers, l) * value, extra)
-
-    loop(slots, finish, 32)
+    def finish(g, carry):
+        weight = weights(sharers, g)
+        for u in range(sharers.shape[1]):
+            l = g * sharers.shape[1] + u
+            value = dot(picked, basis[l]) + dot(restricted[l], inv[l], NT)
+            pack(out, l, weight[:, u : u + 1] * value, extra)
+        return carry
+
+    lax.fori_loop(0, sharers.shape[0], finish, 0)
 
 
 def extend_kernel(elem, got, inner, couple, inv, inner_out, face_out, sums, faces, inners, sems):
@@ -263,12 +283,12 @@
     tail = width - LANES
     sums[...] = inner[...].astype(F32)
 
-    def step(l):
+    def step(l, e):
         value = unpack(got, l, rhs, tail).astype(BF16)
         faces[l] = value
-        sums[elem[0, l]] -= dot(value, couple[l])
-
-    loop(slots, step, 32)
+        sums[e] -= dot(value, couple[l])
+
+    table_loop(elem, step)
     copies = [pltpu.make_async_copy(faces, face_out, sems.at[0])]
     copies[0].start()
     part = elements // 2
@@ -336,6 +356,9 @@
     head = rhs // ROWS + 1
     wire = shape((slots, head, ROWS, LANES), BF16)
     unit = 2 * rhs * width * width
+    recv_table, sharers_table, elem_table = (
+        x.reshape(-1, min(slots, GROUP)) for x in (recv_index, sharers, face_elem)
+    )
     tables = [((owned + 1, head, ROWS, LANES), F32), ((owned + 1, head, ROWS, LANES), BF16)]
 
     sent = call(
@@ -364,8 +387,8 @@
     held = call(
         first_owner_kernel,
         shape((slots, head + piece // (2 * ROWS), ROWS, LANES), BF16),
-        [SMEM, VMEM, VMEM],
-        (recv_index, first, coarse_inv),
+        [VMEM, VMEM, VMEM],
+        (recv_table, first, coarse_inv),
         tables + [((piece, total), F32)],
         flops=100 * slots * unit,
         name="first_owner",
@@ -374,8 +397,8 @@
     coarse, restricted = call(
         restrict_kernel,
         (shape((slots, rhs // 2, LANES), BF16), shape((slots, rhs, width), BF16)),
-        [SMEM, VMEM, VMEM],
-        (sharers, gathered, coarse_basis),
+        [VMEM, VMEM, VMEM],
+        (sharers_table, gathered, coarse_basis),
         [((rhs, local), F32)],
         flops=100 * slots * unit,
         name="restrict",
@@ -384,22 +407,22 @@
     weighted = call(
         functools.partial(correct_kernel, groups, rows),
         wire,
-        [SMEM, VMEM, VMEM, VMEM, VMEM, VMEM, VMEM],
-        (sharers, every, first, gathered, restricted, face_inv, coarse_basis),
+        [VMEM] * 7,
+        (sharers_table, every, first, gathered, restricted, face_inv, coarse_basis),
         [((local, total), F32), ((rhs, local), F32)],
         flops=2 * slots * unit,
         name="correct",
     )
     third = exchange(weighted)
     spread = call(
-        owner_kernel, wire, [SMEM, VMEM], (recv_index, third), tables, flops=slots * width * LANES, name="owner"
+        owner_kernel, wire, [VMEM, VMEM], (recv_table, third), tables, flops=slots * width * LANES, name="owner"
     )
     assembled = exchange(spread)
     return call(
         extend_kernel,
         (shape((elements, rhs, width), BF16), shape((slots, rhs, width), BF16)),
-        [SMEM, VMEM, VMEM, VMEM, VMEM],
-        (face_elem, assembled, res_inner, face_coupling, inner_inv),
+        [VMEM] * 5,
+        (elem_table, assembled, res_inner, face_coupling, inner_inv),
         [
             ((elements, rhs, width), F32),
             ((slots, rhs, width), BF16),

time: 72.2 us -> 70 us (0.970)
  Pallas kernels: 12.7 us -> 10.4 us
    pallas_call x6, Pallas kernels: 12.7 us -> 10.4 us  [call(): pl.pallas_call(kernel, out_shape=out_shape, in_specs=specs, out_specs=tup...]
where the time goes in v7:
time: 70 us; the launch traced here: 69.7 us
  blocking collectives  58.5 us (84%)
  Pallas kernels  10.4 us (15%)
  between operations  0.73 us (1%)
    all_to_all x5, blocking collectives, exchange(): return lax.all_to_all(blocks, AXES, split_axis=0, concat_axis=0, tiled=True)  58.5 us
    pallas_call x6, Pallas kernels, call(): pl.pallas_call(kernel, out_shape=out_shape, in_specs=specs, out_specs=tup...  10.4 us

profile of v7, /device:TPU:0, one launch (start us, length us, event | category | flops | bytes accessed | tf_op | source)
XLA Modules:
  0.0 69.7 jit_solution(16036006770266306594)
XLA Ops:
  0.6 0.0 copy-start.6
  0.6 0.0 copy-start.7
  0.7 4.2 %condense.1 = bf16[32,5,4,128]{3,2,1,0:T(4,128)(2,1)S(1)} custom-call(s32[1,32]{1,0:T(1,128)} %elem.1, s32[1,32]{1,0:T(1,128)} %sharers.3, s32[1,64]{1,0:T(1,128)} %map_in.1, bf16[64,16,144]{2,1,0:T(8,128)(2,1)} %inner.3, bf16[64,144,144]{2,1,0:T(8,128)(2,1)} %inv.5, bf16[32,144,144]{2,1,0:T(8,128)(2,1)} %couple.3, bf16[32,16,144]{2,1,0:T(8,128)(2,1)} %face.1), custom_call_target="tpu_custom_call" | custom-call | flops 42467328 | bytes 163840 | tf_op jit(solution)/shard_map/condense/pallas_call | solution.py:323
  4.9 16.0 %all_to_all.25.got.first = bf16[32,5,4,128]{3,2,1,0:T(4,128)(2,1)S(1)} all-to-all(bf16[32,5,4,128]{3,2,1,0:T(4,128)(2,1)S(1)} %condense.1), channel_id=1, replica_groups=mesh['sub'=8,'grp'=4] {'sub','grp'}, dimensions={0} | all-to-all | bytes 327680 | tf_op jit(solution)/shard_map/all_to_all | solution.py:25
  20.9 0.0 copy-done.6
  20.9 0.0 copy-done.7
  20.9 0.6 first_owner.1
  21.5 0.0 slice-start
  21.5 11.7 %all_to_all.26.got.second = bf16[32,7,4,128]{3,2,1,0:T(4,128)(2,1)S(1)} all-to-all(bf16[32,7,4,128]{3,2,1,0:T(4,128)(2,1)S(1)} %first_owner.1), channel_id=1, replica_groups=mesh['sub'=8,'grp'=4] {'sub','grp'}, dimensions={0} | all-to-all | bytes 458752 | tf_op jit(solution)/shard_map/all_to_all | solution.py:25
  33.3 0.0 copy-done.3
  33.3 0.0 copy-done.4
  33.3 0.5 restrict.1
  33.8 9.7 %all_to_all.27.got = bf16[32,8,128]{2,1,0:T(8,128)(2,1)S(1)} all-to-all(bf16[32,8,128]{2,1,0:T(8,128)(2,1)S(1)} %get-tuple-element.4), channel_id=1, replica_groups=mesh['sub'=8,'grp'=4] {'sub','grp'}, dimensions={0} | all-to-all | bytes 131072 | tf_op jit(solution)/shard_map/all_to_all | solution.py:25
  43.5 0.0 copy-done.1
  43.5 2.1 %correct.1 = bf16[32,5,4,128]{3,2,1,0:T(4,128)(2,1)S(1)} custom-call(s32[1,32]{1,0:T(1,128)S(1)} %copy-done.4, bf16[32,8,128]{2,1,0:T(8,128)(2,1)S(1)} %all_to_all.27.got, bf16[32,5,4,128]{3,2,1,0:T(4,128)(2,1)S(1)} %all_to_all.25.got.first, bf16[32,7,4,128]{3,2,1,0:T(4,128)(2,1)S(1)} %all_to_all.26.got.second, ...), custom_call_target="tpu_custom_call" | custom-call | flops 42467328 | bytes 4358656 | tf_op jit(solution)/shard_map/correct/pallas_call | solution.py:323
  45.6 10.5 %all_to_all.28.got = bf16[32,5,4,128]{3,2,1,0:T(4,128)(2,1)S(1)} all-to-all(bf16[32,5,4,128]{3,2,1,0:T(4,128)(2,1)S(1)} %correct.1), channel_id=1, replica_groups=mesh['sub'=8,'grp'=4] {'sub','grp'}, dimensions={0} | all-to-all | bytes 327680 | tf_op jit(solution)/shard_map/all_to_all | solution.py:25
  56.1 0.4 owner.1
  56.5 10.6 %all_to_all.29.got = bf16[32,5,4,128]{3,2,1,0:T(4,128)(2,1)S(1)} all-to-all(bf16[32,5,4,128]{3,2,1,0:T(4,128)(2,1)S(1)} %owner.1), channel_id=1, replica_groups=mesh['sub'=8,'grp'=4] {'sub','grp'}, dimensions={0} | all-to-all | bytes 327680 | tf_op jit(solution)/shard_map/all_to_all | solution.py:25
  67.1 0.0 slice-done
  67.1 0.0 slice-done.1
  67.1 0.0 copy-done
  67.1 0.0 copy-done.2
  67.1 0.0 copy-done.5
  67.1 2.6 %extend.1 = (bf16[64,16,144]{2,1,0:T(8,128)(2,1)}, bf16[32,16,144]{2,1,0:T(8,128)(2,1)}) custom-call(s32[1,32]{1,0:T(1,128)S(1)} %copy-done.5, bf16[32,5,4,128]{3,2,1,0:T(4,128)(2,1)S(1)} %all_to_all.29.got, bf16[64,16,144]{2,1,0:T(8,128)(2,1)S(1)} %copy-done.2, bf16[32,144,144]{2,1,0:T(8,128)(2,1)S(1)} %copy-done, bf16[64,144,144]{2,1,0:T(8,128)(2,1)S(1)} %bitcast.1), custom_call_target="tpu_custom_call" | custom-call | flops 42467328 | bytes 8552960 | tf_op jit(solution)/shard_map/extend/pallas_call | solution.py:323
  (8 shorter events, 0.0 us)
Async XLA Ops:
  0.6 20.3 %copy-start.6 = (s32[1,32]{1,0:T(1,128)S(1)}, s32[1,32]{1,0:T(1,128)}, u32[]{:S(2)}) copy-start(s32[1,32]{1,0:T(1,128)} %recv.3) | copy-start | bytes 388
  0.6 20.2 %copy-start.7 = (f32[128,512]{1,0:T(8,128)S(1)}, f32[128,512]{1,0:T(8,128)}, u32[]{:S(2)}) copy-start(f32[128,512]{1,0:T(8,128)} %cinv.1) | copy-start | bytes 786436
  20.9 12.4 %copy-start.3 = (bf16[32,64,144]{2,1,0:T(8,128)(2,1)S(1)}, bf16[32,64,144]{2,1,0:T(8,128)(2,1)}, u32[]{:S(2)}) copy-start(bf16[32,64,144]{2,1,0:T(8,128)(2,1)} %basis.3) | copy-start | bytes 1769476
  20.9 12.4 %copy-start.4 = (s32[1,32]{1,0:T(1,128)S(1)}, s32[1,32]{1,0:T(1,128)}, u32[]{:S(2)}) copy-start(s32[1,32]{1,0:T(1,128)} %sharers.3) | copy-start | bytes 388
  21.5 45.6 %slice-start = ((s8[4718592]{0:T(1024)(128)(4,1)}), s8[4194304]{0:T(1024)(128)(4,1)S(1)}, s32[]{:S(2)}) async-start(s8[4718592]{0:T(1024)(128)(4,1)} %bitcast), calls=%async_computation.5 | async-start | bytes 8388608
  33.3 10.3 %copy-start.1 = (bf16[32,144,144]{2,1,0:T(8,128)(2,1)S(1)}, bf16[32,144,144]{2,1,0:T(8,128)(2,1)}, u32[]{:S(2)}) copy-start(bf16[32,144,144]{2,1,0:T(8,128)(2,1)} %inv.4) | copy-start | bytes 3981316
  33.3 33.8 %slice-start.1 = ((s8[4718592]{0:T(1024)(128)(4,1)}), s8[524288]{0:T(1024)(128)(4,1)S(1)}, s32[]{:S(2)}) async-start(s8[4718592]{0:T(1024)(128)(4,1)} %bitcast), calls=%async_computation.6 | async-start | bytes 1048576
  43.5 23.6 %copy-start = (bf16[32,144,144]{2,1,0:T(8,128)(2,1)S(1)}, bf16[32,144,144]{2,1,0:T(8,128)(2,1)}, u32[]{:S(2)}) copy-start(bf16[32,144,144]{2,1,0:T(8,128)(2,1)} %couple.3) | copy-start | bytes 3981316
  43.5 23.6 %copy-start.2 = (bf16[64,16,144]{2,1,0:T(8,128)(2,1)S(1)}, bf16[64,16,144]{2,1,0:T(8,128)(2,1)}, u32[]{:S(2)}) copy-start(bf16[64,16,144]{2,1,0:T(8,128)(2,1)} %inner.3) | copy-start | bytes 884740
  43.5 23.6 %copy-start.5 = (s32[1,32]{1,0:T(1,128)S(1)}, s32[1,32]{1,0:T(1,128)}, u32[]{:S(2)}) copy-start(s32[1,32]{1,0:T(1,128)} %elem.1) | copy-start | bytes 388

commit v8 on v7

--- a/solution.py
+++ b/solution.py
@@ -17,7 +17,7 @@
 VMEM = pl.BlockSpec(memory_space=pltpu.VMEM)
 HBM = pl.BlockSpec(memory_space=pltpu.HBM)
 CHUNK = 16
-ROWS = 4
+ROWS = 2
 GROUP = 32
 
 
@@ -34,12 +34,12 @@
     return jnp.where(count > 0, 1.0 / jnp.maximum(count, 1).astype(F32), 0.0)
 
 
-def pack(out, slot, value, extra):
+def pack(out, slot, value):
     count = value.shape[0] // ROWS
     value_rows = [value[ROWS * j : ROWS * (j + 1)] for j in range(count)]
     for j in range(count):
         out[slot, j] = value_rows[j][:, :LANES].astype(BF16)
-    out[slot, count] = jnp.concatenate([v[:, LANES:] for v in value_rows] + [extra], axis=1).astype(BF16)
+    out[slot, count] = jnp.concatenate([v[:, LANES:] for v in value_rows], axis=1).astype(BF16)
 
 
 def unpack(ref, slot, rhs, tail):
@@ -116,9 +116,8 @@
     maps = cmap[...]
     digits = jnp.concatenate([maps // DIGIT, maps % DIGIT], axis=0).astype(F32)
     local = digits.shape[1]
-    spare = LANES - rhs // ROWS * (width - LANES)
-    digits = jnp.concatenate([digits, jnp.zeros((ROWS - 2, local), F32)], axis=0)
-    extra = jnp.concatenate([jnp.zeros((ROWS, spare - local), F32), digits], axis=1) if spare > local else digits
+    digits = jnp.concatenate([jnp.zeros((ROWS, LANES - local), F32), digits], axis=1).astype(BF16)
+    last = out.shape[1] - 1
     for c in range(chunks):
         copy(inner.at[pl.ds(0, step)], rin.at[part(c)], sems.at[0, c]).wait()
         copy(inv.at[pl.ds(0, step)], invs.at[part(c)], sems.at[1, c]).wait()
@@ -128,7 +127,8 @@
         for u in range(step):
             l = c * step + u
             value = fac[l].astype(F32) - dot(near[u], cps[l], NT)
-            pack(out, l, omega(sharers, l) * value, extra)
+            pack(out, l, omega(sharers, l) * value)
+            out[l, last] = digits
 
 
 def assemble(recv, got, out, sums, rounded):
@@ -181,7 +181,7 @@
 
 def first_owner_kernel(recv, got, cinv, out, sums, rounded, strip):
     slots, height, _, _ = out.shape
-    head = got.shape[1]
+    head = sums.shape[1]
     piece = strip.shape[0]
     local = LANES // 2
     start = pl.multiple_of(lax.axis_index("sub") * piece, piece)
@@ -240,9 +240,9 @@
         turned[:, t * LANES : (t + 1) * LANES] = jnp.concatenate(parts, axis=0).T[:local]
 
 
-def correct_kernel(groups, rows, sharers, got, first, second, restricted, inv, basis, out, turned, sums):
+def correct_kernel(groups, rows, sharers, got, first, second, restricted, inv, basis, out, turned, sums, near):
     slots, rhs, width = restricted.shape
-    head = first.shape[1]
+    head = first.shape[1] - 1
     local = basis.shape[1]
     turn_columns(groups, rows, second, head, turned)
     sums[...] = jnp.zeros_like(sums)
@@ -259,19 +259,19 @@
             value = jnp.concatenate(halves(jnp.concatenate([low, top], axis=0), local, left), axis=0)
             term = dot(value.astype(BF16), columns, NT)
             part = term if part is None else part + term
+            for l in (2 * p, 2 * p + 1):
+                near[l] = dot(restricted[l], inv[l], NT)
         sums[...] += part
         return carry
 
     lax.fori_loop(0, slots // 2 // group, body, 0)
     picked = sums[...].astype(BF16)
-    extra = jnp.zeros((ROWS, LANES - rhs // ROWS * (width - LANES)), F32)
-
     def finish(g, carry):
         weight = weights(sharers, g)
         for u in range(sharers.shape[1]):
             l = g * sharers.shape[1] + u
-            value = dot(picked, basis[l]) + dot(restricted[l], inv[l], NT)
-            pack(out, l, weight[:, u : u + 1] * value, extra)
+            value = dot(picked, basis[l]) + near[l]
+            pack(out, l, weight[:, u : u + 1] * value)
         return carry
 
     lax.fori_loop(0, sharers.shape[0], finish, 0)
@@ -363,7 +363,7 @@
 
     sent = call(
         condense_kernel,
-        wire,
+        shape((slots, head + 1, ROWS, LANES), BF16),
         [HBM] * 7,
         tuple(
             pltpu.with_memory_space_constraint(x, pltpu.HBM)
@@ -409,7 +409,7 @@
         wire,
         [VMEM] * 7,
         (sharers_table, every, first, gathered, restricted, face_inv, coarse_basis),
-        [((local, total), F32), ((rhs, local), F32)],
+        [((local, total), F32), ((rhs, local), F32), ((slots, rhs, width), F32)],
         flops=2 * slots * unit,
         name="correct",
     )

time: 70 us -> 69.4 us (level)
  blocking collectives: 58.5 us -> 57.7 us
    all_to_all x5, blocking collectives: 58.5 us -> 57.7 us  [exchange(): return lax.all_to_all(blocks, AXES, split_axis=0, concat_axis=0, tiled=True)]
where the time goes in v8:
time: 69.4 us; the launch traced here: 69.1 us
  blocking collectives  57.7 us (83%)
  Pallas kernels  10.6 us (15%)
  between operations  0.73 us (1%)
    all_to_all x5, blocking collectives, exchange(): return lax.all_to_all(blocks, AXES, split_axis=0, concat_axis=0, tiled=True)  57.7 us
    pallas_call x6, Pallas kernels, call(): pl.pallas_call(kernel, out_shape=out_shape, in_specs=specs, out_specs=tup...  10.6 us

profile of v8, /device:TPU:0, one launch (start us, length us, event | category | flops | bytes accessed | tf_op | source)
XLA Modules:
  0.0 69.1 jit_solution(7608781701897915251)
XLA Ops:
  0.6 0.0 copy-start.6
  0.6 0.0 copy-start.7
  0.7 4.3 %condense.1 = bf16[32,10,2,128]{3,2,1,0:T(2,128)(2,1)S(1)} custom-call(s32[1,32]{1,0:T(1,128)} %elem.1, s32[1,32]{1,0:T(1,128)} %sharers.3, s32[1,64]{1,0:T(1,128)} %map_in.1, bf16[64,16,144]{2,1,0:T(8,128)(2,1)} %inner.3, bf16[64,144,144]{2,1,0:T(8,128)(2,1)} %inv.5, bf16[32,144,144]{2,1,0:T(8,128)(2,1)} %couple.3, bf16[32,16,144]{2,1,0:T(8,128)(2,1)} %face.1), custom_call_target="tpu_custom_call" | custom-call | flops 42467328 | bytes 163840 | tf_op jit(solution)/shard_map/condense/pallas_call | solution.py:323
  4.9 16.0 %all_to_all.25.got.first = bf16[32,10,2,128]{3,2,1,0:T(2,128)(2,1)S(1)} all-to-all(bf16[32,10,2,128]{3,2,1,0:T(2,128)(2,1)S(1)} %condense.1), channel_id=1, replica_groups=mesh['sub'=8,'grp'=4] {'sub','grp'}, dimensions={0} | all-to-all | bytes 327680 | tf_op jit(solution)/shard_map/all_to_all | solution.py:25
  20.9 0.0 copy-done.6
  20.9 0.0 copy-done.7
  20.9 0.6 first_owner.1
  21.5 0.0 slice-start
  21.6 11.5 %all_to_all.26.got.second = bf16[32,13,2,128]{3,2,1,0:T(2,128)(2,1)S(1)} all-to-all(bf16[32,13,2,128]{3,2,1,0:T(2,128)(2,1)S(1)} %first_owner.1), channel_id=1, replica_groups=mesh['sub'=8,'grp'=4] {'sub','grp'}, dimensions={0} | all-to-all | bytes 425984 | tf_op jit(solution)/shard_map/all_to_all | solution.py:25
  33.1 0.0 copy-done.3
  33.1 0.0 copy-done.4
  33.1 0.6 restrict.1
  33.6 9.6 %all_to_all.27.got = bf16[32,8,128]{2,1,0:T(8,128)(2,1)S(1)} all-to-all(bf16[32,8,128]{2,1,0:T(8,128)(2,1)S(1)} %get-tuple-element.4), channel_id=1, replica_groups=mesh['sub'=8,'grp'=4] {'sub','grp'}, dimensions={0} | all-to-all | bytes 131072 | tf_op jit(solution)/shard_map/all_to_all | solution.py:25
  43.2 0.0 copy-done.1
  43.2 2.2 %correct.1 = bf16[32,9,2,128]{3,2,1,0:T(2,128)(2,1)S(1)} custom-call(s32[1,32]{1,0:T(1,128)S(1)} %copy-done.4, bf16[32,8,128]{2,1,0:T(8,128)(2,1)S(1)} %all_to_all.27.got, bf16[32,10,2,128]{3,2,1,0:T(2,128)(2,1)S(1)} %all_to_all.25.got.first, bf16[32,13,2,128]{3,2,1,0:T(2,128)(2,1)S(1)} %all_to_all.26.got.second, ...), custom_call_target="tpu_custom_call" | custom-call | flops 42467328 | bytes 4325888 | tf_op jit(solution)/shard_map/correct/pallas_call | solution.py:323
  45.4 10.3 %all_to_all.28.got = bf16[32,9,2,128]{3,2,1,0:T(2,128)(2,1)S(1)} all-to-all(bf16[32,9,2,128]{3,2,1,0:T(2,128)(2,1)S(1)} %correct.1), channel_id=1, replica_groups=mesh['sub'=8,'grp'=4] {'sub','grp'}, dimensions={0} | all-to-all | bytes 294912 | tf_op jit(solution)/shard_map/all_to_all | solution.py:25
  55.7 0.4 owner.1
  56.1 10.3 %all_to_all.29.got = bf16[32,9,2,128]{3,2,1,0:T(2,128)(2,1)S(1)} all-to-all(bf16[32,9,2,128]{3,2,1,0:T(2,128)(2,1)S(1)} %owner.1), channel_id=1, replica_groups=mesh['sub'=8,'grp'=4] {'sub','grp'}, dimensions={0} | all-to-all | bytes 294912 | tf_op jit(solution)/shard_map/all_to_all | solution.py:25
  66.5 0.0 slice-done
  66.5 0.0 slice-done.1
  66.5 0.0 copy-done
  66.5 0.0 copy-done.2
  66.5 0.0 copy-done.5
  66.5 2.6 %extend.1 = (bf16[64,16,144]{2,1,0:T(8,128)(2,1)}, bf16[32,16,144]{2,1,0:T(8,128)(2,1)}) custom-call(s32[1,32]{1,0:T(1,128)S(1)} %copy-done.5, bf16[32,9,2,128]{3,2,1,0:T(2,128)(2,1)S(1)} %all_to_all.29.got, bf16[64,16,144]{2,1,0:T(8,128)(2,1)S(1)} %copy-done.2, bf16[32,144,144]{2,1,0:T(8,128)(2,1)S(1)} %copy-done, bf16[64,144,144]{2,1,0:T(8,128)(2,1)S(1)} %bitcast.1), custom_call_target="tpu_custom_call" | custom-call | flops 42467328 | bytes 8536576 | tf_op jit(solution)/shard_map/extend/pallas_call | solution.py:323
  (8 shorter events, 0.0 us)
Async XLA Ops:
  0.6 20.3 %copy-start.6 = (s32[1,32]{1,0:T(1,128)S(1)}, s32[1,32]{1,0:T(1,128)}, u32[]{:S(2)}) copy-start(s32[1,32]{1,0:T(1,128)} %recv.3) | copy-start | bytes 388
  0.6 20.3 %copy-start.7 = (f32[128,512]{1,0:T(8,128)S(1)}, f32[128,512]{1,0:T(8,128)}, u32[]{:S(2)}) copy-start(f32[128,512]{1,0:T(8,128)} %cinv.1) | copy-start | bytes 786436
  20.9 12.1 %copy-start.3 = (bf16[32,64,144]{2,1,0:T(8,128)(2,1)S(1)}, bf16[32,64,144]{2,1,0:T(8,128)(2,1)}, u32[]{:S(2)}) copy-start(bf16[32,64,144]{2,1,0:T(8,128)(2,1)} %basis.3) | copy-start | bytes 1769476
  20.9 12.1 %copy-start.4 = (s32[1,32]{1,0:T(1,128)S(1)}, s32[1,32]{1,0:T(1,128)}, u32[]{:S(2)}) copy-start(s32[1,32]{1,0:T(1,128)} %sharers.3) | copy-start | bytes 388
  21.5 44.9 %slice-start = ((s8[4718592]{0:T(1024)(128)(4,1)}), s8[4194304]{0:T(1024)(128)(4,1)S(1)}, s32[]{:S(2)}) async-start(s8[4718592]{0:T(1024)(128)(4,1)} %bitcast), calls=%async_computation.5 | async-start | bytes 8388608
  33.1 10.2 %copy-start.1 = (bf16[32,144,144]{2,1,0:T(8,128)(2,1)S(1)}, bf16[32,144,144]{2,1,0:T(8,128)(2,1)}, u32[]{:S(2)}) copy-start(bf16[32,144,144]{2,1,0:T(8,128)(2,1)} %inv.4) | copy-start | bytes 3981316
  33.1 33.4 %slice-start.1 = ((s8[4718592]{0:T(1024)(128)(4,1)}), s8[524288]{0:T(1024)(128)(4,1)S(1)}, s32[]{:S(2)}) async-start(s8[4718592]{0:T(1024)(128)(4,1)} %bitcast), calls=%async_computation.6 | async-start | bytes 1048576
  43.2 23.2 %copy-start = (bf16[32,144,144]{2,1,0:T(8,128)(2,1)S(1)}, bf16[32,144,144]{2,1,0:T(8,128)(2,1)}, u32[]{:S(2)}) copy-start(bf16[32,144,144]{2,1,0:T(8,128)(2,1)} %couple.3) | copy-start | bytes 3981316
  43.2 23.2 %copy-start.2 = (bf16[64,16,144]{2,1,0:T(8,128)(2,1)S(1)}, bf16[64,16,144]{2,1,0:T(8,128)(2,1)}, u32[]{:S(2)}) copy-start(bf16[64,16,144]{2,1,0:T(8,128)(2,1)} %inner.3) | copy-start | bytes 884740
  43.2 23.2 %copy-start.5 = (s32[1,32]{1,0:T(1,128)S(1)}, s32[1,32]{1,0:T(1,128)}, u32[]{:S(2)}) copy-start(s32[1,32]{1,0:T(1,128)} %elem.1) | copy-start | bytes 388

commit v9 on v8

--- a/solution.py
+++ b/solution.py
@@ -34,19 +34,37 @@
     return jnp.where(count > 0, 1.0 / jnp.maximum(count, 1).astype(F32), 0.0)
 
 
-def pack(out, slot, value):
+def tail_order(count, fold):
+    spans = [[k] for k in range(count)]
+    while fold and len(spans) > 1:
+        half = len(spans) // 2
+        spans = [a + b for a, b in zip(spans[:half], spans[half:])]
+    return spans[0] if fold else list(range(count))
+
+
+def pack(out, slot, value, fold):
     count = value.shape[0] // ROWS
-    value_rows = [value[ROWS * j : ROWS * (j + 1)] for j in range(count)]
     for j in range(count):
-        out[slot, j] = value_rows[j][:, :LANES].astype(BF16)
-    out[slot, count] = jnp.concatenate([v[:, LANES:] for v in value_rows], axis=1).astype(BF16)
-
-
-def unpack(ref, slot, rhs, tail):
+        out[slot, j] = value[ROWS * j : ROWS * (j + 1), :LANES].astype(BF16)
+    end = value[:, LANES:]
+    if fold:
+        while end.shape[0] > ROWS:
+            half = end.shape[0] // 2
+            end = jnp.concatenate([end[:half], end[half:]], axis=1)
+    else:
+        end = jnp.concatenate([end[ROWS * j : ROWS * (j + 1)] for j in range(count)], axis=1)
+    out[slot, count] = end.astype(BF16)
+
+
+def unpack(ref, slot, rhs, tail, fold):
     count = rhs // ROWS
     main = [ref[slot, j].astype(F32) for j in range(count)]
     last = ref[slot, count].astype(F32)
-    end = [last[:, j * tail : (j + 1) * tail] for j in range(count)]
+    order = tail_order(count, fold)
+    end = []
+    for k in range(count):
+        at = order.index(k) * tail
+        end.append(last[:, at : at + tail])
     return jnp.concatenate([jnp.concatenate(main, axis=0), jnp.concatenate(end, axis=0)], axis=1)
 
 
@@ -127,7 +145,7 @@
         for u in range(step):
             l = c * step + u
             value = fac[l].astype(F32) - dot(near[u], cps[l], NT)
-            pack(out, l, omega(sharers, l) * value)
+            pack(out, l, omega(sharers, l) * value, False)
             out[l, last] = digits
 
 
@@ -210,7 +228,7 @@
         weight = weights(sharers, g)
         for u in range(group):
             l = g * group + u
-            value = (weight[:, u : u + 1] * unpack(got, l, rhs, tail)).astype(BF16)
+            value = (weight[:, u : u + 1] * unpack(got, l, rhs, tail, False)).astype(BF16)
             restricted[l] = value
             term = dot(value, basis[l], NT)
             part = term if part is None else part + term
@@ -271,7 +289,7 @@
         for u in range(sharers.shape[1]):
             l = g * sharers.shape[1] + u
             value = dot(picked, basis[l]) + near[l]
-            pack(out, l, weight[:, u : u + 1] * value)
+            pack(out, l, weight[:, u : u + 1] * value, True)
         return carry
 
     lax.fori_loop(0, sharers.shape[0], finish, 0)
@@ -284,7 +302,7 @@
     sums[...] = inner[...].astype(F32)
 
     def step(l, e):
-        value = unpack(got, l, rhs, tail).astype(BF16)
+        value = unpack(got, l, rhs, tail, True).astype(BF16)
         faces[l] = value
         sums[e] -= dot(value, couple[l])
 

time: 69.4 us -> 69.1 us (level)
  no operation moved by 1% of the time
where the time goes in v9:
time: 69.1 us; the launch traced here: 68.9 us
  blocking collectives  57.7 us (84%)
  Pallas kernels  10.4 us (15%)
  between operations  0.73 us (1%)
    all_to_all x5, blocking collectives, exchange(): return lax.all_to_all(blocks, AXES, split_axis=0, concat_axis=0, tiled=True)  57.7 us
    pallas_call x6, Pallas kernels, call(): pl.pallas_call(kernel, out_shape=out_shape, in_specs=specs, out_specs=tup...  10.4 us

profile of v9, /device:TPU:0, one launch (start us, length us, event | category | flops | bytes accessed | tf_op | source)
XLA Modules:
  0.0 68.9 jit_solution(3294360325539771481)
XLA Ops:
  0.6 0.0 copy-start.6
  0.6 0.0 copy-start.7
  0.7 4.3 %condense.1 = bf16[32,10,2,128]{3,2,1,0:T(2,128)(2,1)S(1)} custom-call(s32[1,32]{1,0:T(1,128)} %elem.1, s32[1,32]{1,0:T(1,128)} %sharers.3, s32[1,64]{1,0:T(1,128)} %map_in.1, bf16[64,16,144]{2,1,0:T(8,128)(2,1)} %inner.3, bf16[64,144,144]{2,1,0:T(8,128)(2,1)} %inv.5, bf16[32,144,144]{2,1,0:T(8,128)(2,1)} %couple.3, bf16[32,16,144]{2,1,0:T(8,128)(2,1)} %face.1), custom_call_target="tpu_custom_call" | custom-call | flops 42467328 | bytes 163840 | tf_op jit(solution)/shard_map/condense/pallas_call | solution.py:341
  4.9 16.0 %all_to_all.25.got.first = bf16[32,10,2,128]{3,2,1,0:T(2,128)(2,1)S(1)} all-to-all(bf16[32,10,2,128]{3,2,1,0:T(2,128)(2,1)S(1)} %condense.1), channel_id=1, replica_groups=mesh['sub'=8,'grp'=4] {'sub','grp'}, dimensions={0} | all-to-all | bytes 327680 | tf_op jit(solution)/shard_map/all_to_all | solution.py:25
  20.9 0.0 copy-done.6
  20.9 0.0 copy-done.7
  20.9 0.6 first_owner.1
  21.5 0.0 slice-start
  21.6 11.5 %all_to_all.26.got.second = bf16[32,13,2,128]{3,2,1,0:T(2,128)(2,1)S(1)} all-to-all(bf16[32,13,2,128]{3,2,1,0:T(2,128)(2,1)S(1)} %first_owner.1), channel_id=1, replica_groups=mesh['sub'=8,'grp'=4] {'sub','grp'}, dimensions={0} | all-to-all | bytes 425984 | tf_op jit(solution)/shard_map/all_to_all | solution.py:25
  33.1 0.0 copy-done.3
  33.1 0.0 copy-done.4
  33.1 0.6 restrict.1
  33.6 9.6 %all_to_all.27.got = bf16[32,8,128]{2,1,0:T(8,128)(2,1)S(1)} all-to-all(bf16[32,8,128]{2,1,0:T(8,128)(2,1)S(1)} %get-tuple-element.4), channel_id=1, replica_groups=mesh['sub'=8,'grp'=4] {'sub','grp'}, dimensions={0} | all-to-all | bytes 131072 | tf_op jit(solution)/shard_map/all_to_all | solution.py:25
  43.2 0.0 copy-done.1
  43.2 1.9 %correct.1 = bf16[32,9,2,128]{3,2,1,0:T(2,128)(2,1)S(1)} custom-call(s32[1,32]{1,0:T(1,128)S(1)} %copy-done.4, bf16[32,8,128]{2,1,0:T(8,128)(2,1)S(1)} %all_to_all.27.got, bf16[32,10,2,128]{3,2,1,0:T(2,128)(2,1)S(1)} %all_to_all.25.got.first, bf16[32,13,2,128]{3,2,1,0:T(2,128)(2,1)S(1)} %all_to_all.26.got.second, ...), custom_call_target="tpu_custom_call" | custom-call | flops 42467328 | bytes 4325888 | tf_op jit(solution)/shard_map/correct/pallas_call | solution.py:341
  45.2 10.3 %all_to_all.28.got = bf16[32,9,2,128]{3,2,1,0:T(2,128)(2,1)S(1)} all-to-all(bf16[32,9,2,128]{3,2,1,0:T(2,128)(2,1)S(1)} %correct.1), channel_id=1, replica_groups=mesh['sub'=8,'grp'=4] {'sub','grp'}, dimensions={0} | all-to-all | bytes 294912 | tf_op jit(solution)/shard_map/all_to_all | solution.py:25
  55.5 0.4 owner.1
  55.9 10.3 %all_to_all.29.got = bf16[32,9,2,128]{3,2,1,0:T(2,128)(2,1)S(1)} all-to-all(bf16[32,9,2,128]{3,2,1,0:T(2,128)(2,1)S(1)} %owner.1), channel_id=1, replica_groups=mesh['sub'=8,'grp'=4] {'sub','grp'}, dimensions={0} | all-to-all | bytes 294912 | tf_op jit(solution)/shard_map/all_to_all | solution.py:25
  66.2 0.0 slice-done
  66.2 0.0 slice-done.1
  66.2 0.0 copy-done
  66.2 0.0 copy-done.2
  66.3 0.0 copy-done.5
  66.3 2.6 %extend.1 = (bf16[64,16,144]{2,1,0:T(8,128)(2,1)}, bf16[32,16,144]{2,1,0:T(8,128)(2,1)}) custom-call(s32[1,32]{1,0:T(1,128)S(1)} %copy-done.5, bf16[32,9,2,128]{3,2,1,0:T(2,128)(2,1)S(1)} %all_to_all.29.got, bf16[64,16,144]{2,1,0:T(8,128)(2,1)S(1)} %copy-done.2, bf16[32,144,144]{2,1,0:T(8,128)(2,1)S(1)} %copy-done, bf16[64,144,144]{2,1,0:T(8,128)(2,1)S(1)} %bitcast.1), custom_call_target="tpu_custom_call" | custom-call | flops 42467328 | bytes 8536576 | tf_op jit(solution)/shard_map/extend/pallas_call | solution.py:341
  (8 shorter events, 0.0 us)
Async XLA Ops:
  0.6 20.3 %copy-start.6 = (s32[1,32]{1,0:T(1,128)S(1)}, s32[1,32]{1,0:T(1,128)}, u32[]{:S(2)}) copy-start(s32[1,32]{1,0:T(1,128)} %recv.3) | copy-start | bytes 388
  0.6 20.3 %copy-start.7 = (f32[128,512]{1,0:T(8,128)S(1)}, f32[128,512]{1,0:T(8,128)}, u32[]{:S(2)}) copy-start(f32[128,512]{1,0:T(8,128)} %cinv.1) | copy-start | bytes 786436
  20.9 12.1 %copy-start.3 = (bf16[32,64,144]{2,1,0:T(8,128)(2,1)S(1)}, bf16[32,64,144]{2,1,0:T(8,128)(2,1)}, u32[]{:S(2)}) copy-start(bf16[32,64,144]{2,1,0:T(8,128)(2,1)} %basis.3) | copy-start | bytes 1769476
  20.9 12.1 %copy-start.4 = (s32[1,32]{1,0:T(1,128)S(1)}, s32[1,32]{1,0:T(1,128)}, u32[]{:S(2)}) copy-start(s32[1,32]{1,0:T(1,128)} %sharers.3) | copy-start | bytes 388
  21.5 44.7 %slice-start = ((s8[4718592]{0:T(1024)(128)(4,1)}), s8[4194304]{0:T(1024)(128)(4,1)S(1)}, s32[]{:S(2)}) async-start(s8[4718592]{0:T(1024)(128)(4,1)} %bitcast), calls=%async_computation.5 | async-start | bytes 8388608
  33.1 10.2 %copy-start.1 = (bf16[32,144,144]{2,1,0:T(8,128)(2,1)S(1)}, bf16[32,144,144]{2,1,0:T(8,128)(2,1)}, u32[]{:S(2)}) copy-start(bf16[32,144,144]{2,1,0:T(8,128)(2,1)} %inv.4) | copy-start | bytes 3981316
  33.1 33.2 %slice-start.1 = ((s8[4718592]{0:T(1024)(128)(4,1)}), s8[524288]{0:T(1024)(128)(4,1)S(1)}, s32[]{:S(2)}) async-start(s8[4718592]{0:T(1024)(128)(4,1)} %bitcast), calls=%async_computation.6 | async-start | bytes 1048576
  43.2 23.0 %copy-start = (bf16[32,144,144]{2,1,0:T(8,128)(2,1)S(1)}, bf16[32,144,144]{2,1,0:T(8,128)(2,1)}, u32[]{:S(2)}) copy-start(bf16[32,144,144]{2,1,0:T(8,128)(2,1)} %couple.3) | copy-start | bytes 3981316
  43.2 23.0 %copy-start.2 = (bf16[64,16,144]{2,1,0:T(8,128)(2,1)S(1)}, bf16[64,16,144]{2,1,0:T(8,128)(2,1)}, u32[]{:S(2)}) copy-start(bf16[64,16,144]{2,1,0:T(8,128)(2,1)} %inner.3) | copy-start | bytes 884740
  43.2 23.0 %copy-start.5 = (s32[1,32]{1,0:T(1,128)S(1)}, s32[1,32]{1,0:T(1,128)}, u32[]{:S(2)}) copy-start(s32[1,32]{1,0:T(1,128)} %elem.1) | copy-start | bytes 388

commit v10 on v9

--- a/solution.py
+++ b/solution.py
@@ -309,8 +309,9 @@
     table_loop(elem, step)
     copies = [pltpu.make_async_copy(faces, face_out, sems.at[0])]
     copies[0].start()
-    part = elements // 2
-    for c in range(2):
+    parts = sems.shape[0] - 1
+    part = elements // parts
+    for c in range(parts):
 
         def finish(e):
             inners[c * part + e] = dot(sums[c * part + e].astype(BF16), inv[c * part + e], NT).astype(BF16)
@@ -445,7 +446,7 @@
             ((elements, rhs, width), F32),
             ((slots, rhs, width), BF16),
             ((elements, rhs, width), BF16),
-            (pltpu.SemaphoreType.DMA((3,)), None),
+            (pltpu.SemaphoreType.DMA((5,)), None),
         ],
         flops=2 * slots * unit,
         name="extend",

time: 69.1 us -> 69.1 us (level)
  no operation moved by 1% of the time
where the time goes in v10:
time: 69.1 us; the launch traced here: 68.9 us
  blocking collectives  57.7 us (84%)
  Pallas kernels  10.4 us (15%)
  between operations  0.73 us (1%)
    all_to_all x5, blocking collectives, exchange(): return lax.all_to_all(blocks, AXES, split_axis=0, concat_axis=0, tiled=True)  57.7 us
    pallas_call x6, Pallas kernels, call(): pl.pallas_call(kernel, out_shape=out_shape, in_specs=specs, out_specs=tup...  10.4 us

profile of v10, /device:TPU:0, one launch (start us, length us, event | category | flops | bytes accessed | tf_op | source)
XLA Modules:
  0.0 68.9 jit_solution(4416539547701035509)
XLA Ops:
  0.6 0.0 copy-start.6
  0.6 0.0 copy-start.7
  0.7 4.3 %condense.1 = bf16[32,10,2,128]{3,2,1,0:T(2,128)(2,1)S(1)} custom-call(s32[1,32]{1,0:T(1,128)} %elem.1, s32[1,32]{1,0:T(1,128)} %sharers.3, s32[1,64]{1,0:T(1,128)} %map_in.1, bf16[64,16,144]{2,1,0:T(8,128)(2,1)} %inner.3, bf16[64,144,144]{2,1,0:T(8,128)(2,1)} %inv.5, bf16[32,144,144]{2,1,0:T(8,128)(2,1)} %couple.3, bf16[32,16,144]{2,1,0:T(8,128)(2,1)} %face.1), custom_call_target="tpu_custom_call" | custom-call | flops 42467328 | bytes 163840 | tf_op jit(solution)/shard_map/condense/pallas_call | solution.py:342
  4.9 16.0 %all_to_all.25.got.first = bf16[32,10,2,128]{3,2,1,0:T(2,128)(2,1)S(1)} all-to-all(bf16[32,10,2,128]{3,2,1,0:T(2,128)(2,1)S(1)} %condense.1), channel_id=1, replica_groups=mesh['sub'=8,'grp'=4] {'sub','grp'}, dimensions={0} | all-to-all | bytes 327680 | tf_op jit(solution)/shard_map/all_to_all | solution.py:25
  20.9 0.0 copy-done.6
  20.9 0.0 copy-done.7
  20.9 0.6 first_owner.1
  21.5 0.0 slice-start
  21.6 11.5 %all_to_all.26.got.second = bf16[32,13,2,128]{3,2,1,0:T(2,128)(2,1)S(1)} all-to-all(bf16[32,13,2,128]{3,2,1,0:T(2,128)(2,1)S(1)} %first_owner.1), channel_id=1, replica_groups=mesh['sub'=8,'grp'=4] {'sub','grp'}, dimensions={0} | all-to-all | bytes 425984 | tf_op jit(solution)/shard_map/all_to_all | solution.py:25
  33.1 0.0 copy-done.3
  33.1 0.0 copy-done.4
  33.1 0.6 restrict.1
  33.6 9.6 %all_to_all.27.got = bf16[32,8,128]{2,1,0:T(8,128)(2,1)S(1)} all-to-all(bf16[32,8,128]{2,1,0:T(8,128)(2,1)S(1)} %get-tuple-element.4), channel_id=1, replica_groups=mesh['sub'=8,'grp'=4] {'sub','grp'}, dimensions={0} | all-to-all | bytes 131072 | tf_op jit(solution)/shard_map/all_to_all | solution.py:25
  43.2 0.0 copy-done.1
  43.2 1.9 %correct.1 = bf16[32,9,2,128]{3,2,1,0:T(2,128)(2,1)S(1)} custom-call(s32[1,32]{1,0:T(1,128)S(1)} %copy-done.4, bf16[32,8,128]{2,1,0:T(8,128)(2,1)S(1)} %all_to_all.27.got, bf16[32,10,2,128]{3,2,1,0:T(2,128)(2,1)S(1)} %all_to_all.25.got.first, bf16[32,13,2,128]{3,2,1,0:T(2,128)(2,1)S(1)} %all_to_all.26.got.second, ...), custom_call_target="tpu_custom_call" | custom-call | flops 42467328 | bytes 4325888 | tf_op jit(solution)/shard_map/correct/pallas_call | solution.py:342
  45.2 10.3 %all_to_all.28.got = bf16[32,9,2,128]{3,2,1,0:T(2,128)(2,1)S(1)} all-to-all(bf16[32,9,2,128]{3,2,1,0:T(2,128)(2,1)S(1)} %correct.1), channel_id=1, replica_groups=mesh['sub'=8,'grp'=4] {'sub','grp'}, dimensions={0} | all-to-all | bytes 294912 | tf_op jit(solution)/shard_map/all_to_all | solution.py:25
  55.5 0.4 owner.1
  55.9 10.3 %all_to_all.29.got = bf16[32,9,2,128]{3,2,1,0:T(2,128)(2,1)S(1)} all-to-all(bf16[32,9,2,128]{3,2,1,0:T(2,128)(2,1)S(1)} %owner.1), channel_id=1, replica_groups=mesh['sub'=8,'grp'=4] {'sub','grp'}, dimensions={0} | all-to-all | bytes 294912 | tf_op jit(solution)/shard_map/all_to_all | solution.py:25
  66.2 0.0 slice-done
  66.2 0.0 slice-done.1
  66.2 0.0 copy-done
  66.2 0.0 copy-done.2
  66.3 0.0 copy-done.5
  66.3 2.6 %extend.1 = (bf16[64,16,144]{2,1,0:T(8,128)(2,1)}, bf16[32,16,144]{2,1,0:T(8,128)(2,1)}) custom-call(s32[1,32]{1,0:T(1,128)S(1)} %copy-done.5, bf16[32,9,2,128]{3,2,1,0:T(2,128)(2,1)S(1)} %all_to_all.29.got, bf16[64,16,144]{2,1,0:T(8,128)(2,1)S(1)} %copy-done.2, bf16[32,144,144]{2,1,0:T(8,128)(2,1)S(1)} %copy-done, bf16[64,144,144]{2,1,0:T(8,128)(2,1)S(1)} %bitcast.1), custom_call_target="tpu_custom_call" | custom-call | flops 42467328 | bytes 8536576 | tf_op jit(solution)/shard_map/extend/pallas_call | solution.py:342
  (8 shorter events, 0.0 us)
Async XLA Ops:
  0.6 20.3 %copy-start.6 = (s32[1,32]{1,0:T(1,128)S(1)}, s32[1,32]{1,0:T(1,128)}, u32[]{:S(2)}) copy-start(s32[1,32]{1,0:T(1,128)} %recv.3) | copy-start | bytes 388
  0.6 20.3 %copy-start.7 = (f32[128,512]{1,0:T(8,128)S(1)}, f32[128,512]{1,0:T(8,128)}, u32[]{:S(2)}) copy-start(f32[128,512]{1,0:T(8,128)} %cinv.1) | copy-start | bytes 786436
  20.9 12.1 %copy-start.3 = (bf16[32,64,144]{2,1,0:T(8,128)(2,1)S(1)}, bf16[32,64,144]{2,1,0:T(8,128)(2,1)}, u32[]{:S(2)}) copy-start(bf16[32,64,144]{2,1,0:T(8,128)(2,1)} %basis.3) | copy-start | bytes 1769476
  20.9 12.1 %copy-start.4 = (s32[1,32]{1,0:T(1,128)S(1)}, s32[1,32]{1,0:T(1,128)}, u32[]{:S(2)}) copy-start(s32[1,32]{1,0:T(1,128)} %sharers.3) | copy-start | bytes 388
  21.5 44.7 %slice-start = ((s8[4718592]{0:T(1024)(128)(4,1)}), s8[4194304]{0:T(1024)(128)(4,1)S(1)}, s32[]{:S(2)}) async-start(s8[4718592]{0:T(1024)(128)(4,1)} %bitcast), calls=%async_computation.5 | async-start | bytes 8388608
  33.1 10.2 %copy-start.1 = (bf16[32,144,144]{2,1,0:T(8,128)(2,1)S(1)}, bf16[32,144,144]{2,1,0:T(8,128)(2,1)}, u32[]{:S(2)}) copy-start(bf16[32,144,144]{2,1,0:T(8,128)(2,1)} %inv.4) | copy-start | bytes 3981316
  33.1 33.2 %slice-start.1 = ((s8[4718592]{0:T(1024)(128)(4,1)}), s8[524288]{0:T(1024)(128)(4,1)S(1)}, s32[]{:S(2)}) async-start(s8[4718592]{0:T(1024)(128)(4,1)} %bitcast), calls=%async_computation.6 | async-start | bytes 1048576
  43.2 23.0 %copy-start = (bf16[32,144,144]{2,1,0:T(8,128)(2,1)S(1)}, bf16[32,144,144]{2,1,0:T(8,128)(2,1)}, u32[]{:S(2)}) copy-start(bf16[32,144,144]{2,1,0:T(8,128)(2,1)} %couple.3) | copy-start | bytes 3981316
  43.2 23.0 %copy-start.2 = (bf16[64,16,144]{2,1,0:T(8,128)(2,1)S(1)}, bf16[64,16,144]{2,1,0:T(8,128)(2,1)}, u32[]{:S(2)}) copy-start(bf16[64,16,144]{2,1,0:T(8,128)(2,1)} %inner.3) | copy-start | bytes 884740
  43.2 23.0 %copy-start.5 = (s32[1,32]{1,0:T(1,128)S(1)}, s32[1,32]{1,0:T(1,128)}, u32[]{:S(2)}) copy-start(s32[1,32]{1,0:T(1,128)} %elem.1) | copy-start | bytes 388
